TPU v7x, 32 devices: a whole 2x2x4 slice. The times are simulated.
32 devices in a mesh: dp: 4 (over z), expert: 8 (over y, x, core).
Axes of the slice: x: 2, y: 2, z: 4, core: 2. Of those that a mesh axis runs over, the one named last changes fastest.
Arguments:
- residual: bfloat16 [4096, 1280], P(('dp', 'expert')), may hold values from -6 to 6
- context: bfloat16 [4096, 1280], P(('dp', 'expert')), may hold values from -6 to 6
- w_out: bfloat16 [1280, 1280], P(('dp', 'expert')), may hold values from -0.15625 to 0.15625
- w_router: bfloat16 [1280, 16], replicated, may hold values from -0.15625 to 0.15625
- expert_ids: int32 [4096, 2], P(('dp', 'expert')), may hold values from 0 to 15, all different within a row; in each aligned block of 128 rows (0 to 127, 128 to 255, ...) at most 20 rows name the same one
- w_fc1: bfloat16 [16, 1280, 5120], P('expert', None, 'dp'), may hold values from -0.15625 to 0.15625
- w_fc2: bfloat16 [16, 5120, 1280], P('expert', 'dp'), may hold values from -0.078125 to 0.078125
- cotangent: bfloat16 [4096, 1280], P(('dp', 'expert')), may hold values from -6 to 6
Outputs:
- layer_out: bfloat16 [4096, 1280], P(('dp', 'expert'))
- d_residual: bfloat16 [4096, 1280], P(('dp', 'expert'))
- d_context: bfloat16 [4096, 1280], P(('dp', 'expert'))
- grad_out: float32 [1280, 1280], P(('dp', 'expert'))
- grad_router: float32 [1280, 16], P(('dp', 'expert'))
- grad_fc1: float32 [16, 1280, 5120], P('expert', None, 'dp')
- grad_fc2: float32 [16, 5120, 1280], P('expert', 'dp')
Inputs may be any that keep to these rules, and one draw needn't show every extreme that they name: `expert_ids`: each row names 2 different experts. Among the 128 rows of one device no expert is named more than 20 times, and some device has an expert named exactly 20 times.
All inputs are finite; a program needn't handle non-finite values.
Results may differ from a plain program's by a relative error of at most 0.01.
Values may be sent and summed in bfloat16 or wider, within the bound.
No kernel may reach another device: no remote copies, remote signals or barrier semaphores. Data moves between devices by JAX's collectives and lax.ppermute only.
A program may use at most 192 MiB of HBM per device.

v0:
```python
import jax
import jax.numpy as jnp
from jax import lax
from jax.sharding import PartitionSpec as P

LN_EPS = 1e-06


def normal_cdf(value):
    return 0.5 * (1.0 + lax.erf(value * 0.7071067811865476))


def gelu_act(value):
    return value * normal_cdf(value)


def gelu_slope(value):
    return normal_cdf(value) + value * jnp.exp(-0.5 * value * value) * 0.3989422804014327


def on_device(residual, context, w_out, w_router, expert_ids, w_fc1, w_fc2, cotangent):
    tok_rows = residual.shape[0]
    width = residual.shape[1]
    top_k = expert_ids.shape[1]
    devices = lax.axis_size(("dp", "expert"))
    expert_devs = lax.axis_size("expert")
    exp_dev = w_fc1.shape[0]
    experts = exp_dev * expert_devs
    capacity = max(2, (5 * top_k * tok_rows + 4 * experts - 1) // (4 * experts))
    grad_scale = float(tok_rows * devices) ** (-0.5)
    w_full = lax.all_gather(w_out, ("dp", "expert"), axis=0, tiled=True)
    stream = residual.astype(jnp.float32) + jnp.dot(
        context, w_full, preferred_element_type=jnp.float32
    )
    average = jnp.mean(stream, axis=1, keepdims=True)
    centred = stream - average
    variance = jnp.mean(centred * centred, axis=1, keepdims=True)
    inv_std = lax.rsqrt(variance + LN_EPS)
    normed = centred * inv_std
    normed_bf = normed.astype(jnp.bfloat16)
    logits = jnp.dot(normed_bf, w_router, preferred_element_type=jnp.float32)
    expert_iota = jnp.arange(experts, dtype=jnp.int32)
    picked = (expert_ids[:, :, None] == expert_iota[None, None, :]).astype(jnp.float32)
    chosen = jnp.sum(picked * logits[:, None, :], axis=2)
    gate_probs = jax.nn.sigmoid(chosen - chosen[:, ::-1])
    flat_ids = expert_ids.reshape(-1)
    onehot = (flat_ids[:, None] == expert_iota[None, :]).astype(jnp.int32)
    before = jnp.cumsum(onehot, axis=0) - onehot
    position = jnp.sum(before * onehot, axis=1)
    target_slot = flat_ids * capacity + position
    slot_iota = jnp.arange(experts * capacity, dtype=jnp.int32)
    slot_map = (slot_iota[:, None] == target_slot[None, :]).astype(jnp.bfloat16)
    pair_in = jnp.broadcast_to(normed_bf[:, None, :], (tok_rows, top_k, width)).reshape(-1, width)
    cot_float = cotangent.astype(jnp.float32)
    pair_cot = (
        (gate_probs[:, :, None] * cot_float[:, None, :]).astype(jnp.bfloat16).reshape(-1, width)
    )
    slot_shape = (expert_devs, exp_dev, capacity, width)
    send_in = (
        jnp.dot(slot_map, pair_in, preferred_element_type=jnp.float32)
        .astype(jnp.bfloat16)
        .reshape(slot_shape)
    )
    send_cot = (
        jnp.dot(slot_map, pair_cot, preferred_element_type=jnp.float32)
        .astype(jnp.bfloat16)
        .reshape(slot_shape)
    )
    owner_in, owner_cot = (
        lax.all_to_all(send_in, "expert", split_axis=0, concat_axis=0, tiled=True),
        lax.all_to_all(send_cot, "expert", split_axis=0, concat_axis=0, tiled=True),
    )
    recv_in, recv_cot = (
        lax.all_gather(owner_in, "dp", axis=0, tiled=True),
        lax.all_gather(owner_cot, "dp", axis=0, tiled=True),
    )
    preact = jnp.einsum("secd,edh->sech", recv_in, w_fc1, preferred_element_type=jnp.float32)
    hidden = gelu_act(preact).astype(jnp.bfloat16)
    part_out = jnp.einsum("sech,ehd->secd", hidden, w_fc2, preferred_element_type=jnp.float32)
    d_hidden = jnp.einsum("secd,ehd->sech", recv_cot, w_fc2, preferred_element_type=jnp.float32)
    d_preact = (d_hidden * gelu_slope(preact)).astype(jnp.bfloat16)
    part_back = jnp.einsum("sech,edh->secd", d_preact, w_fc1, preferred_element_type=jnp.float32)
    grad_fc2 = grad_scale * jnp.einsum(
        "sech,secd->ehd", hidden, recv_cot, preferred_element_type=jnp.float32
    )
    grad_fc1 = grad_scale * jnp.einsum(
        "secd,sech->edh", recv_in, d_preact, preferred_element_type=jnp.float32
    )
    summed_out, summed_back = (
        lax.psum_scatter(
            part_out.astype(jnp.bfloat16), "dp", scatter_dimension=0, tiled=True
        ).astype(jnp.float32),
        lax.psum_scatter(
            part_back.astype(jnp.bfloat16), "dp", scatter_dimension=0, tiled=True
        ).astype(jnp.float32),
    )
    home_out, home_back = (
        lax.all_to_all(
            summed_out.astype(jnp.bfloat16), "expert", split_axis=0, concat_axis=0, tiled=True
        ),
        lax.all_to_all(
            summed_back.astype(jnp.bfloat16), "expert", split_axis=0, concat_axis=0, tiled=True
        ),
    )
    slot_out = home_out.reshape(experts * capacity, width)
    slot_back = home_back.reshape(experts * capacity, width)
    pair_out = jnp.dot(slot_map.T, slot_out, preferred_element_type=jnp.float32).reshape(
        tok_rows, top_k, width
    )
    pair_back = jnp.dot(slot_map.T, slot_back, preferred_element_type=jnp.float32).reshape(
        tok_rows, top_k, width
    )
    mixture = jnp.sum(gate_probs[:, :, None] * pair_out, axis=1)
    layer_out = (stream + mixture).astype(jnp.bfloat16)
    d_gate = jnp.sum(cot_float[:, None, :] * pair_out, axis=2)
    d_chosen = gate_probs * (d_gate - jnp.sum(gate_probs * d_gate, axis=1, keepdims=True))
    d_logits = jnp.sum(picked * d_chosen[:, :, None], axis=1)
    d_normed = jnp.sum(pair_back, axis=1) + jnp.dot(
        d_logits, w_router.astype(jnp.float32).T, precision=lax.Precision.HIGHEST
    )
    d_stream = cot_float + inv_std * (
        d_normed
        - jnp.mean(d_normed, axis=1, keepdims=True)
        - normed * jnp.mean(d_normed * normed, axis=1, keepdims=True)
    )
    d_residual = d_stream.astype(jnp.bfloat16)
    d_context = jnp.dot(d_residual, w_full.T, preferred_element_type=jnp.float32).astype(
        jnp.bfloat16
    )
    out_term = jnp.dot(context.T, d_residual, preferred_element_type=jnp.float32)
    router_term = jnp.dot(
        normed_bf.astype(jnp.float32).T, d_logits, precision=lax.Precision.HIGHEST
    )
    both_grads = lax.psum_scatter(
        grad_scale * jnp.concatenate([out_term, router_term], axis=1),
        ("dp", "expert"),
        scatter_dimension=0,
        tiled=True,
    )
    grad_out = both_grads[:, :width]
    grad_router = both_grads[:, width:]
    return (layer_out, d_residual, d_context, grad_out, grad_router, grad_fc1, grad_fc2)


def solution(mesh):
    in_specs = (
        P(("dp", "expert"), None),
        P(("dp", "expert"), None),
        P(("dp", "expert"), None),
        P(),
        P(("dp", "expert"), None),
        P("expert", None, "dp"),
        P("expert", "dp", None),
        P(("dp", "expert"), None),
    )
    out_specs = (
        P(("dp", "expert"), None),
        P(("dp", "expert"), None),
        P(("dp", "expert"), None),
        P(("dp", "expert"), None),
        P(("dp", "expert"), None),
        P("expert", None, "dp"),
        P("expert", "dp", None),
    )
    return jax.shard_map(
        on_device, mesh=mesh, in_specs=in_specs, out_specs=out_specs, check_vma=False
    )
```

profile of v0, /device:TPU:0, one launch (start us, length us, event | category | flops | bytes accessed | tf_op | source)
XLA Modules:
  0.0 579.4 jit_solution(12981182207088786917)
XLA Ops:
  7.2 0.7 all-gather.4.cloned.1.call-update
  8.0 0.8 copy.69
  9.0 0.6 reduce-window.6
  10.0 63.2 %all-gather.4.cloned.1.call-done = bf16[1280,1280]{1,0:T(8,128)(2,1)} async-done(((bf16[40,1280]{1,0:T(8,128)(2,1)}), bf16[1280,1280]{1,0:T(8,128)(2,1)}) %all-gather.4.cloned.1.call-update) | async-done | bytes 3276816 | tf_op jit(solution)/shard_map/all_gather | solution.py:31
  73.2 2.7 fusion.41
  76.9 0.4 convolution_convert_fusion.1
  77.4 0.6 copy.72
  78.1 15.4 %all_to_all.20 = bf16[8,2,20,1280]{3,1,2,0:T(2,128)(2,1)S(1)} all-to-all(bf16[8,2,20,1280]{3,1,2,0:T(2,128)(2,1)S(1)} %copy.72), channel_id=1, replica_groups=mesh['dp'=4,'expert'=8] {'expert'}, dimensions={0} | all-to-all | bytes 1638400 | tf_op jit(solution)/shard_map/all_to_all | solution.py:70
  93.5 1.0 copy.73
  94.6 1.4 mul.154.clone
  96.0 2.2 mul.155
  98.8 0.5 convolution_convert_fusion
  99.4 0.6 copy.79
  100.0 15.3 %all_to_all.21 = bf16[8,2,20,1280]{3,1,2,0:T(2,128)(2,1)S(1)} all-to-all(bf16[8,2,20,1280]{3,1,2,0:T(2,128)(2,1)S(1)} %copy.79), channel_id=1, replica_groups=mesh['dp'=4,'expert'=8] {'expert'}, dimensions={0} | all-to-all | bytes 1638400 | tf_op jit(solution)/shard_map/all_to_all | solution.py:71
  115.3 1.0 copy.80
  116.6 41.4 %all-gather.6.cloned.1.call-done = bf16[32,2,20,1280]{3,0,2,1:T(8,128)(2,1)} async-done(((bf16[8,2,20,1280]{3,0,2,1:T(8,128)(2,1)}), bf16[32,2,20,1280]{3,0,2,1:T(8,128)(2,1)}) %all-gather.6.cloned.1.call-update) | async-done | bytes 3276816 | tf_op jit(solution)/shard_map/all_gather | solution.py:74
  158.0 10.7 %fusion.19 = (bf16[32,2,20,1280]{3,0,2,1:T(8,128)(2,1)}, f32[2,32,20,1280]{3,1,2,0:T(8,128)}) fusion(bf16[32,2,20,1280]{3,0,2,1:T(8,128)(2,1)} %all-gather.6.cloned.1.call-done, bf16[2,1280,1280]{2,1,0:T(8,128)(2,1)} %param.13), kind=kOutput, calls=%fused_computation.24 | convolution fusion | flops 4202496000 | bytes 19660800 | tf_op jit(solution)/shard_map/secd,edh->sech/dot_general | solution.py:77
  168.7 55.2 %all-gather.8.cloned.1.call-done = bf16[32,2,20,1280]{3,0,2,1:T(8,128)(2,1)} async-done(((bf16[8,2,20,1280]{3,0,2,1:T(8,128)(2,1)}), bf16[32,2,20,1280]{3,0,2,1:T(8,128)(2,1)}) %all-gather.8.cloned.1.call-update) | async-done | bytes 3276816 | tf_op jit(solution)/shard_map/all_gather | solution.py:75
  223.9 10.4 %fusion.5 = bf16[32,2,20,1280]{3,0,2,1:T(8,128)(2,1)S(1)} fusion(bf16[32,2,20,1280]{3,0,2,1:T(8,128)(2,1)} %all-gather.8.cloned.1.call-done, bf16[2,1280,1280]{2,1,0:T(8,128)(2,1)} %param.14, f32[2,32,20,1280]{3,1,2,0:T(8,128)} %get-tuple-element.51), kind=kOutput, calls=%fused_computation.10 | convolution fusion | flops 4210688000 | bytes 19660800 | tf_op jit(solution)/shard_map/secd,ehd->sech/dot_general | solution.py:80
  234.2 8.7 %fusion.26 = bf16[32,2,20,1280]{3,0,2,1:T(8,128)(2,1)S(1)} fusion(bf16[32,2,20,1280]{3,0,2,1:T(8,128)(2,1)S(1)} %fusion.5, bf16[2,1280,1280]{2,1,0:T(8,128)(2,1)} %param.13), kind=kOutput, calls=%fused_computation.27 | convolution fusion | flops 4195942400 | bytes 13107200 | tf_op jit(solution)/shard_map/sech,edh->secd/dot_general | solution.py:82
  243.0 3.7 copy.91
  246.7 5.4 reshape.144
  252.5 8.3 %fusion.29 = bf16[32,2,20,1280]{3,0,2,1:T(8,128)(2,1)S(1)} fusion(bf16[32,2,20,1280]{3,0,2,1:T(8,128)(2,1)} %get-tuple-element.50, bf16[2,1280,1280]{2,1,0:T(8,128)(2,1)} %param.14), kind=kOutput, calls=%fused_computation.28 | convolution fusion | flops 4195942400 | bytes 13107200 | tf_op jit(solution)/shard_map/sech,ehd->secd/dot_general | solution.py:79
  260.7 3.7 copy.89
  264.5 5.4 reshape.142
  269.9 43.5 %reduce-scatter.10.cloned.1.call-done = bf16[8,51200]{1,0:T(8,128)(2,1)} async-done(((bf16[32,51200]{1,0:T(8,128)(2,1)}), bf16[8,51200]{1,0:T(8,128)(2,1)}) %reduce-scatter.10.cloned.1.call-update) | async-done | bytes 819216
  313.4 2.9 copy.81
  316.3 3.7 all-to-all-start.3
  319.9 0.9 convert_element_type.70
  321.4 56.7 %reduce-scatter.8.cloned.1.call-done = bf16[8,51200]{1,0:T(8,128)(2,1)} async-done(((bf16[32,51200]{1,0:T(8,128)(2,1)}), bf16[8,51200]{1,0:T(8,128)(2,1)}) %reduce-scatter.8.cloned.1.call-update) | async-done | bytes 819216
  378.0 2.9 copy.74
  380.9 4.2 all-to-all-start.1
  385.5 10.7 %bitcast_multiply_fusion = f32[2,1280,1280]{2,1,0:T(8,128)} fusion(bf16[32,2,20,1280]{3,0,2,1:T(8,128)(2,1)} %get-tuple-element.50, bf16[32,2,20,1280]{3,0,2,1:T(8,128)(2,1)} %all-gather.8.cloned.1.call-done), kind=kOutput, calls=%fused_computation | convolution fusion | flops 4197580800 | bytes 19660800 | tf_op jit(solution)/shard_map/sech,secd->ehd/dot_general | solution.py:83
  396.5 1.6 all-to-all-done.1
  398.1 1.2 copy.75
  399.3 1.1 reshape.136
  400.4 0.5 convolution_reduce_fusion
  400.9 2.1 multiply_reduce_fusion
  403.3 1.4 fusion.40
  404.7 1.0 add_convert_fusion
  405.8 1.0 convolution_bitcast_fusion
  406.8 3.2 maximum_multiply_fusion
  410.0 10.9 %bitcast_multiply_fusion.1 = f32[2,1280,1280]{2,1,0:T(8,128)} fusion(bf16[32,2,20,1280]{3,0,2,1:T(8,128)(2,1)} %all-gather.6.cloned.1.call-done, bf16[32,2,20,1280]{3,0,2,1:T(8,128)(2,1)} %copy-done.7), kind=kOutput, calls=%fused_computation.1 | convolution fusion | flops 4197580800 | bytes 19660800 | tf_op jit(solution)/shard_map/secd,sech->edh/dot_general | solution.py:86
  420.9 1.9 convolution_convert_fusion.2
  422.8 145.9 %all-reduce.3.cloned.1.call-done = f32[1280,1296]{0,1:T(8,128)} async-done(((f32[1280,1296]{0,1:T(8,128)}), f32[1280,1296]{0,1:T(8,128)}) %all-reduce.3.cloned.1.call-update) | async-done | bytes 6635536
  568.7 1.5 constant_dynamic-slice_fusion
  570.3 0.9 copy.84
  571.2 1.4 dynamic-slice.2
  (60 shorter events, 4.5 us)
Async XLA Ops:
  7.2 66.0 %copy-start = (bf16[128,1280]{1,0:T(8,128)(2,1)S(1)}, bf16[128,1280]{1,0:T(8,128)(2,1)}, u32[]{:S(2)}) copy-start(bf16[128,1280]{1,0:T(8,128)(2,1)} %param.9) | copy-start | bytes 983044
  7.2 66.0 %all-gather.4.cloned.1.call-start = ((), (), s32[]{:S(2)}) async-start(), calls=%async_computation.6 | async-start | bytes 3379200 | tf_op jit(solution)/shard_map/all_gather | solution.py:31
  7.9 150.1 %all-gather.6.cloned.1.call-start = ((), (), s32[]{:S(2)}) async-start(), calls=%async_computation.7 | async-start | bytes 4096000 | tf_op jit(solution)/shard_map/all_gather | solution.py:74
  75.9 18.7 %copy-start.3 = (bf16[128,1280]{1,0:T(8,128)(2,1)S(1)}, bf16[128,1280]{1,0:T(8,128)(2,1)}, u32[]{:S(2)}) copy-start(bf16[128,1280]{1,0:T(8,128)(2,1)} %param.15) | copy-start | bytes 983044
  76.8 21.3 %copy-start.5 = (bf16[1280,16]{0,1:T(8,128)(2,1)S(1)}, bf16[1280,16]{0,1:T(8,128)(2,1)}, u32[]{:S(2)}) copy-start(bf16[1280,16]{0,1:T(8,128)(2,1)} %param.11) | copy-start | bytes 122884
  76.9 21.5 %copy-start.6 = (s32[128,2]{0,1:T(2,128)S(1)}, s32[128,2]{0,1:T(2,128)}, u32[]{:S(2)}) copy-start(s32[128,2]{0,1:T(2,128)} %param.12) | copy-start | bytes 3076
  94.5 129.3 %all-gather.8.cloned.1.call-start = ((), (), s32[]{:S(2)}) async-start(), calls=%async_computation.8 | async-start | bytes 4096000 | tf_op jit(solution)/shard_map/all_gather | solution.py:75
  116.4 197.0 %reduce-scatter.10.cloned.1.call-start = ((), (), s32[]{:S(2)}) async-start(), calls=%async_computation.10 | async-start | bytes 4096000
  234.2 8.7 %copy-start.7 = (bf16[32,2,20,1280]{3,0,2,1:T(8,128)(2,1)}, bf16[32,2,20,1280]{3,0,2,1:T(8,128)(2,1)S(1)}, u32[]{:S(2)}) copy-start(bf16[32,2,20,1280]{3,0,2,1:T(8,128)(2,1)S(1)} %fusion.5) | copy-start | bytes 9830404
  252.2 125.8 %reduce-scatter.8.cloned.1.call-start = ((), (), s32[]{:S(2)}) async-start(), calls=%async_computation.9 | async-start | bytes 4096000
  264.5 55.5 %copy-start.4 = (bf16[128,1280]{1,0:T(8,128)(2,1)S(1)}, bf16[128,1280]{1,0:T(8,128)(2,1)}, u32[]{:S(2)}) copy-start(bf16[128,1280]{1,0:T(8,128)(2,1)} %param.15) | copy-start | bytes 983044
  316.3 64.6 %all-to-all-start.3 = ((bf16[8,2,20,1280]{3,1,2,0:T(2,128)(2,1)}), bf16[8,2,20,1280]{3,1,2,0:T(2,128)(2,1)S(1)}, u32[]{:S(2)}, u32[]{:S(2)}) async-start(bf16[8,2,20,1280]{3,1,2,0:T(2,128)(2,1)} %copy.81), calls=%async_computation.3 | async-start | bytes 1638400 | tf_op jit(solution)/shard_map/all_to_all | solution.py:101
  380.9 17.2 %all-to-all-start.1 = ((bf16[8,2,20,1280]{3,1,2,0:T(2,128)(2,1)}), bf16[8,2,20,1280]{3,1,2,0:T(2,128)(2,1)}, u32[]{:S(2)}, u32[]{:S(2)}) async-start(bf16[8,2,20,1280]{3,1,2,0:T(2,128)(2,1)} %copy.74), calls=%async_computation.1 | async-start | bytes 1638400 | tf_op jit(solution)/shard_map/all_to_all | solution.py:98
  385.2 183.6 %all-reduce.3.cloned.1.call-start = ((), (), s32[]{:S(2)}) async-start(), calls=%async_computation.11 | async-start | bytes 13271040
  405.8 15.1 %copy-start.2 = (bf16[128,1280]{1,0:T(8,128)(2,1)}, bf16[128,1280]{1,0:T(8,128)(2,1)S(1)}, u32[]{:S(2)}) copy-start(bf16[128,1280]{1,0:T(8,128)(2,1)S(1)} %get-tuple-element.46) | copy-start | bytes 983044
  410.0 10.9 %copy-start.1 = (bf16[1280,1280]{1,0:T(8,128)(2,1)S(1)}, bf16[1280,1280]{1,0:T(8,128)(2,1)}, u32[]{:S(2)}) copy-start(bf16[1280,1280]{1,0:T(8,128)(2,1)} %all-gather.4.cloned.1.call-done) | copy-start | bytes 9830404
Sparse Core Ops, SparseCore 0:
  10.8 62.2 all-gather.3
  94.7 63.3 all-gather.5
  159.6 64.2 all-gather.7
  252.3 61.0 reduce-scatter.9
  315.6 62.4 reduce-scatter.7
  410.1 158.5 all-reduce.2
where the time goes:
time: 580 us; the launch traced here: 579 us
  waiting for transfers between devices  408 us (70%)
  matrix products  70.5 us (12%)
  local copies, waits for them, and re-layouts  40.3 us (7%)
  blocking collectives  30.7 us (5%)
  between operations  14.4 us (2%)
  starting transfers between devices  8.79 us (2%)
  other arithmetic  6.44 us (1%)
    unnamed x9, waiting for transfers between devices  247 us
    all_gather x1, waiting for transfers between devices, on_device(): w_full = lax.all_gather(w_out, ('dp', 'expert'), axis=0, tiled=True)  63.2 us
    all_gather x1, waiting for transfers between devices, on_device(): lax.all_gather(owner_cot, 'dp', axis=0, tiled=True)  55.2 us
    all_gather x1, waiting for transfers between devices, on_device(): lax.all_gather(owner_in, 'dp', axis=0, tiled=True)  41.4 us
    unnamed x22, local copies, waits for them, and re-layouts  20.1 us
    all_to_all x1, blocking collectives, on_device(): lax.all_to_all(send_in, 'expert', split_axis=0, concat_axis=0, tiled=True)  15.4 us
    all_to_all x1, blocking collectives, on_device(): lax.all_to_all(send_cot, 'expert', split_axis=0, concat_axis=0, tiled=True)  15.3 us
  transfers between devices with their start and end apart: 8, of which 7 were waited for; matrix products, arithmetic and copies ran while one was open for 12% of the time, Pallas kernels for 0%

commit v1 on v0

v1 whole, which is shorter than its diff:
```python
import functools

import jax
import jax.numpy as jnp
from jax import lax
from jax.experimental import pallas as pl
from jax.experimental.pallas import tpu as pltpu
from jax.sharding import PartitionSpec as P

from jax.experimental.layout import Layout, with_layout_constraint

LN_EPS = 1e-06
BF = jnp.bfloat16
F32 = jnp.float32
HI = lax.Precision.HIGHEST


def dot32(a, b, dims=((1,), (0,)), precision=None):
    return lax.dot_general(
        a, b, (dims, ((), ())), preferred_element_type=F32, precision=precision
    )


def swap(value, axis, bit):
    n = lax.axis_size(axis)
    return lax.ppermute(value, axis, [(i, i ^ bit) for i in range(n)])


def exchange(value):
    return lax.all_to_all(value, "expert", split_axis=0, concat_axis=0, tiled=True)


def line_steps(value, axis):
    n = lax.axis_size(axis)
    up, down = {}, {}
    cur_u = cur_d = value
    for s in range(1, n):
        cur_u = lax.ppermute(cur_u, axis, [(i, i + 1) for i in range(s - 1, n - 1)])
        cur_d = lax.ppermute(cur_d, axis, [(i, i - 1) for i in range(1, n - s + 1)])
        up[s], down[s] = cur_u, cur_d
    return up, down


def line_block(up, down, index, n, j):
    found = {}
    for i in range(n):
        found.setdefault((i ^ j) - i, []).append(i)
    total = None
    for gap, places in found.items():
        piece = down[gap] if gap > 0 else up[-gap]
        if total is None:
            total = piece
            continue
        here = functools.reduce(jnp.logical_or, [index == i for i in places])
        total = jnp.where(here, piece, total)
    return total


def chunk_of(size):
    for chunk in (256, 128):
        if size % chunk == 0:
            return chunk
    return size


def ffn_kernel(x_ref, c_ref, sel_ref, wr_ref, w1_ref, w2_ref, out_ref, back_ref, gh_ref, dp_ref, s_ref, gate, acc_o, acc_b, acc_s):
    step = pl.program_id(1)
    x = x_ref[...].reshape(c_ref.shape[1:])
    c = c_ref[0]

    @pl.when(step == 0)
    def _():
        logits = dot32(x, wr_ref[...])
        gate[...] = jax.nn.sigmoid(jnp.sum(logits * sel_ref[0], axis=1, keepdims=True))
        acc_o[...] = jnp.zeros_like(acc_o)
        acc_b[...] = jnp.zeros_like(acc_b)
        acc_s[...] = jnp.zeros_like(acc_s)

    g = gate[...]
    w1 = w1_ref[0]
    w2 = w2_ref[0]
    pre = dot32(x, w1)
    cdf = 0.5 * (1.0 + lax.erf(pre * 0.7071067811865476))
    hid = pre * cdf
    slope = cdf + pre * jnp.exp(-0.5 * pre * pre) * 0.3989422804014327
    hid_bf = hid.astype(BF)
    acc_o[...] += dot32(hid_bf, w2)
    dh = dot32(c, w2, ((1,), (1,))) * g
    dp = (dh * slope).astype(BF)
    acc_b[...] += dot32(dp, w1, ((1,), (1,)))
    acc_s[...] += jnp.sum(dh * hid, axis=1, keepdims=True)
    gh_ref[0] = (hid * g).astype(BF)
    dp_ref[0] = dp

    @pl.when(step == pl.num_programs(1) - 1)
    def _():
        out_ref[...] = (acc_o[...] * g).astype(BF).reshape(out_ref.shape)
        back_ref[...] = acc_b[...].astype(BF).reshape(back_ref.shape)
        s_ref[0] = acc_s[...]


def ffn(x, c, sel, w_router, w1, w2):
    e, rows, width = c.shape
    sources, seg = x.shape[0], x.shape[2]
    hidden = w1.shape[2]
    experts = w_router.shape[1]
    hc = chunk_of(hidden)
    row_spec = pl.BlockSpec((1, rows, width), lambda i, j: (i, 0, 0))
    src_spec = pl.BlockSpec((sources, None, seg, width), lambda i, j: (0, i, 0, 0))
    hid_spec = pl.BlockSpec((1, rows, hc), lambda i, j: (i, 0, j))
    return pl.pallas_call(
        ffn_kernel,
        grid=(e, hidden // hc),
        in_specs=[
            src_spec,
            row_spec,
            pl.BlockSpec((1, rows, experts), lambda i, j: (i, 0, 0)),
            pl.BlockSpec((width, experts), lambda i, j: (0, 0)),
            pl.BlockSpec((1, width, hc), lambda i, j: (i, 0, j)),
            pl.BlockSpec((1, hc, width), lambda i, j: (i, j, 0)),
        ],
        out_specs=[src_spec, src_spec, hid_spec, hid_spec, pl.BlockSpec((1, rows, 1), lambda i, j: (i, 0, 0))],
        out_shape=[
            jax.ShapeDtypeStruct(x.shape, BF),
            jax.ShapeDtypeStruct(x.shape, BF),
            jax.ShapeDtypeStruct((e, rows, hidden), BF),
            jax.ShapeDtypeStruct((e, rows, hidden), BF),
            jax.ShapeDtypeStruct((e, rows, 1), F32),
        ],
        scratch_shapes=[
            pltpu.VMEM((rows, 1), F32),
            pltpu.VMEM((rows, width), F32),
            pltpu.VMEM((rows, width), F32),
            pltpu.VMEM((rows, 1), F32),
        ],
        cost_estimate=pl.CostEstimate(
            flops=8 * e * rows * width * hidden,
            bytes_accessed=4 * e * width * hidden + 8 * e * rows * (width + hidden),
            transcendentals=2 * e * rows * hidden,
        ),
        compiler_params=pltpu.CompilerParams(dimension_semantics=("arbitrary", "arbitrary")),
    )(x, c, sel, w_router, w1, w2)


def wgrad_kernel(scale, pairs, *refs):
    total = None
    for i in range(pairs):
        left, right = [r[...].reshape(-1, r.shape[-1]) for r in (refs[i], refs[pairs + i])]
        term = dot32(left, right, ((0,), (0,)))
        total = term if total is None else total + term
    refs[-1][0] = total * scale


def wgrad(scale, lefts, rights):
    m = lefts[0].shape[-1]
    e, _, n = [a for a in rights + lefts if a.ndim == 3][0].shape
    n = rights[0].shape[-1]
    mc = chunk_of(m)
    rows = sum([a.size // (e * m) for a in lefts])

    def spec(a, size, step):
        if a.ndim == 3:
            return pl.BlockSpec((None, a.shape[1], size), lambda i, j: (i, 0, j * step))
        return pl.BlockSpec((a.shape[0], None, a.shape[2], size), lambda i, j: (0, i, 0, j * step))

    return pl.pallas_call(
        functools.partial(wgrad_kernel, scale, len(lefts)),
        grid=(e, m // mc),
        in_specs=[spec(a, mc, 1) for a in lefts] + [spec(b, n, 0) for b in rights],
        out_specs=pl.BlockSpec((1, mc, n), lambda i, j: (i, j, 0)),
        out_shape=jax.ShapeDtypeStruct((e, m, n), F32),
        cost_estimate=pl.CostEstimate(
            flops=2 * e * rows * m * n,
            bytes_accessed=4 * e * m * n + 2 * e * rows * (m + n),
            transcendentals=0,
        ),
        compiler_params=pltpu.CompilerParams(dimension_semantics=("arbitrary", "arbitrary")),
    )(*lefts, *rights)


def on_device(residual, context, w_out, w_router, expert_ids, w_fc1, w_fc2, cotangent):
    tok, width = residual.shape
    top_k = expert_ids.shape[1]
    n_dp = lax.axis_size("dp")
    n_ex = lax.axis_size("expert")
    z = lax.axis_index("dp")
    ex = lax.axis_index("expert")
    exp_dev = w_fc1.shape[0]
    experts = exp_dev * n_ex
    cap = max(2, (5 * top_k * tok + 4 * experts - 1) // (4 * experts))
    scale = float(tok * n_dp * n_ex) ** (-0.5)
    shard = w_out.shape[0]
    rows_q = n_dp * shard
    hi, lo = n_ex // 2, n_ex // 4
    groups = [list(range(n_dp // 2)), list(range(n_dp // 2, n_dp))]
    per = n_dp // 2
    seg = per * cap
    slots = n_ex * exp_dev * seg

    own_ids = expert_ids.T
    ids = [own_ids] + [swap(own_ids, "dp", j) for j in range(1, n_dp)]

    col = lax.broadcasted_iota(jnp.int32, (1, width), 1)
    place = col // rows_q
    within = col % rows_q
    rel = jnp.zeros_like(place)
    b, m = 1, n_ex // 2
    while m:
        rel = rel + ((place // m) % 2) * b
        b, m = b * 2, m // 2
    source = ((z ^ (within // shard)) * n_ex + (ex ^ rel)) * shard + within % shard
    reorder = (lax.broadcasted_iota(jnp.int32, (width, width), 0) == source).astype(BF)
    ctx_rel = dot32(context, reorder).astype(BF)

    tri = (
        lax.broadcasted_iota(jnp.int32, (tok, tok), 0)
        < lax.broadcasted_iota(jnp.int32, (tok, tok), 1)
    ).astype(BF)
    e_iota = lax.broadcasted_iota(jnp.int32, (experts, tok), 0)

    def spots_of(block):
        hot = [(e_iota == block[k : k + 1]).astype(F32) for k in range(top_k)]
        before = dot32(sum(hot).astype(BF), tri)
        return [jnp.sum(h * before, axis=0, keepdims=True).astype(jnp.int32) for h in hot]

    own_spots = spots_of(own_ids)
    spot_iota = lax.broadcasted_iota(jnp.int32, (experts * cap, 1), 0)
    own_map = sum([(spot_iota == own_ids[k : k + 1] * cap + own_spots[k]).astype(BF) for k in range(top_k)])
    own_sent = dot32(own_map, cotangent).astype(BF)
    own_cot = exchange(own_sent)

    ids = lax.optimization_barrier(ids)
    spots = [spots_of(block) for block in ids]
    slot_iota = lax.broadcasted_iota(jnp.int32, (slots, 1), 0)
    maps = []
    for group in groups:
        by_k = []
        for k in range(top_k):
            target = [
                (ids[j][k : k + 1] // exp_dev) * (exp_dev * seg)
                + (ids[j][k : k + 1] % exp_dev) * seg
                + i * cap
                + spots[j][k]
                for i, j in enumerate(group)
            ]
            by_k.append((slot_iota == jnp.concatenate(target, axis=1)).astype(BF))
        maps.append(by_k)
    merged = [m[0] + m[1] for m in maps]

    def spread(value):
        n = value.shape[1]
        padded = -(-n // 1024) * 1024
        tile = jnp.pad(value, ((0, 0), (0, padded - n))).reshape(-1, 128)
        got = exchange(tile)
        return got.reshape(n_ex, padded)[:, :n]

    others = []
    for group, by_k in zip(groups, maps):
        total = None
        for k in range(top_k):
            value = jnp.concatenate([ids[j][1 - k : 2 - k] for j in group], axis=1).astype(BF)
            term = dot32(value, by_k[k], ((1,), (1,)))
            total = term if total is None else total + term
        others.append(total.reshape(n_ex, exp_dev * seg))
    others = spread(jnp.concatenate(others, axis=1))
    rows = n_ex * seg
    sels = []
    own_expert = ex * exp_dev + lax.broadcasted_iota(jnp.int32, (exp_dev, 1, 1), 0)
    lane_expert = lax.broadcasted_iota(jnp.int32, (1, 1, experts), 2)
    for g in range(len(groups)):
        other = others[:, g * exp_dev * seg : (g + 1) * exp_dev * seg]
        other = other.reshape(n_ex, exp_dev, seg).transpose(1, 0, 2).reshape(exp_dev, rows, 1)
        sels.append(
            (lane_expert == own_expert).astype(F32)
            - (lane_expert == other.astype(jnp.int32)).astype(F32)
        )

    def dispatch(blocks, hot):
        sent = dot32(hot, jnp.concatenate(blocks, axis=0)).astype(BF)
        return exchange(sent).reshape(n_ex, exp_dev, seg, width)

    w_dp = jnp.concatenate([w_out] + [swap(w_out, "dp", j) for j in range(1, n_dp)], axis=0)
    from_hi = swap(w_dp, "expert", hi)
    from_lo = swap(w_dp, "expert", lo)
    half_q = rows_q // 2
    diag_a = swap(from_hi[:half_q], "expert", lo)
    diag_b = swap(from_lo[half_q:], "expert", hi)
    w_rel = [jnp.concatenate([w_dp, from_hi, from_lo, diag_a, diag_b], axis=0)]
    bit = lo // 2
    while bit:
        w_rel = w_rel + [swap(piece, "expert", bit) for piece in w_rel]
        bit //= 2

    stream = residual.astype(F32)
    span = w_rel[0].shape[0]
    for i, piece in enumerate(w_rel):
        stream = stream + dot32(ctx_rel[:, i * span : (i + 1) * span], piece)
    average = jnp.mean(stream, axis=1, keepdims=True)
    centred = stream - average
    variance = jnp.mean(centred * centred, axis=1, keepdims=True)
    inv_std = lax.rsqrt(variance + LN_EPS)
    normed = centred * inv_std
    normed_bf = normed.astype(BF)
    xs = [normed_bf] + [swap(normed_bf, "dp", j) for j in range(1, n_dp)]
    slot_in = [dispatch([xs[j] for j in group], hot) for group, hot in zip(groups, merged)]

    up, down = line_steps(own_cot, "dp")
    cots = [own_cot] + [line_block(up, down, z, n_dp, j) for j in range(1, n_dp)]
    line = exp_dev * rows
    at = lax.broadcasted_iota(jnp.int32, (line, 1), 0)
    e_at, src_at, blk_at, pos_at = at // rows, at % rows // seg, at % seg // cap, at % cap
    came_from = ((blk_at * n_ex + src_at) * exp_dev + e_at) * cap + pos_at
    arrange = (came_from == lax.broadcasted_iota(jnp.int32, (line, line), 1)).astype(BF)
    slot_cot = [
        dot32(arrange, jnp.concatenate([cots[j] for j in group], axis=0)).astype(BF).reshape(exp_dev, rows, width)
        for group in groups
    ]

    logits = dot32(w_router, normed_bf, ((0,), (1,)))
    late_ids = lax.optimization_barrier(own_ids)
    picks = [(e_iota == late_ids[k : k + 1]).astype(F32) for k in range(top_k)]
    chosen = jnp.concatenate([jnp.sum(h * logits, axis=0, keepdims=True) for h in picks], axis=0)
    gates = jax.nn.sigmoid(chosen - chosen[::-1])

    results = []
    for x, c, sel in zip(slot_in, slot_cot, sels):
        results.append(ffn(x, c, sel, w_router, w_fc1, w_fc2))

    def collect(value, hot):
        got = exchange(value.reshape(-1, width))
        return dot32(hot, got, ((0,), (0,)))

    def reduce_dp(parts):
        total = parts[0]
        for j in range(1, n_dp):
            total = total + swap(parts[j].astype(BF), "dp", j).astype(F32)
        return total

    def blocks_of(values):
        return [v[i * tok : (i + 1) * tok] for v in values for i in range(per)]

    back_sum = reduce_dp(blocks_of([collect(r[1], hot) for r, hot in zip(results, merged)]))
    score = [
        r[4].reshape(exp_dev, n_ex, seg).transpose(1, 0, 2).reshape(n_ex, exp_dev * seg)
        for r in results
    ]
    score = spread(jnp.concatenate(score, axis=1))
    part = exp_dev * seg
    score_parts = []
    for g, by_k in enumerate(maps):
        line = score[:, g * part : (g + 1) * part].reshape(1, slots)
        both = jnp.concatenate([dot32(line, by_k[k].astype(F32), precision=HI) for k in range(top_k)], axis=0)
        score_parts += [both[:, i * tok : (i + 1) * tok] for i in range(per)]
    score_sum = score_parts[0]
    for j in range(1, n_dp):
        score_sum = score_sum + swap(score_parts[j], "dp", j)
    mixture = reduce_dp(blocks_of([collect(r[0], hot) for r, hot in zip(results, merged)]))
    d_chosen = score_sum - gates * jnp.sum(score_sum, axis=0, keepdims=True)
    d_logits = sum([picks[k] * d_chosen[k : k + 1] for k in range(top_k)])
    d_normed = back_sum + dot32(d_logits, w_router.astype(F32), ((0,), (1,)), precision=HI)
    cot_float = cotangent.astype(F32)
    d_stream = cot_float + inv_std * (
        d_normed
        - jnp.mean(d_normed, axis=1, keepdims=True)
        - normed * jnp.mean(d_normed * normed, axis=1, keepdims=True)
    )
    d_residual, late_stream = lax.optimization_barrier((d_stream.astype(BF), stream))
    layer_out = (late_stream + mixture).astype(BF)
    d_rel = jnp.concatenate([dot32(d_residual, piece, ((1,), (1,))).astype(BF) for piece in w_rel], axis=1)
    d_context = dot32(d_rel, reorder, ((1,), (1,))).astype(BF)

    router_term = dot32(normed_bf.astype(F32), d_logits, ((0,), (1,)), precision=HI)
    router_term = dot32(reorder.astype(F32), router_term, ((0,), (0,)), precision=HI)
    pad = -experts % 128
    part_out = jnp.concatenate(
        [dot32(ctx_rel, d_residual, ((0,), (0,))), jnp.pad(router_term, ((0, 0), (0, pad)))], axis=1
    )
    part_out = with_layout_constraint(part_out, Layout(major_to_minor=(0, 1)))
    bit = 1
    while bit < lo:
        half = part_out.shape[0] // 2
        part_out = part_out[:half] + swap(part_out[half:].astype(BF), "expert", bit).astype(F32)
        bit *= 2
    mid = width // 2
    quarters = [part_out[i * rows_q : (i + 1) * rows_q] for i in range(4)]
    left = [q[:, :mid] for q in quarters]
    right = [q[:, mid:] for q in quarters]
    got_l = swap(jnp.concatenate([left[2], left[3]], axis=0).astype(BF), "expert", lo).astype(F32)
    got_r = swap(jnp.concatenate([right[1], right[3]], axis=0).astype(BF), "expert", hi).astype(F32)
    fin_l = swap((left[1] + got_l[rows_q:]).astype(BF), "expert", hi).astype(F32)
    fin_r = swap((right[2] + got_r[rows_q:]).astype(BF), "expert", lo).astype(F32)
    kept = jnp.concatenate([left[0] + got_l[:rows_q] + fin_l, right[0] + got_r[:rows_q] + fin_r], axis=1)
    grads = kept[:shard]
    for j in range(1, n_dp):
        grads = grads + swap(kept[j * shard : (j + 1) * shard].astype(BF), "dp", j).astype(F32)
    grad_out = scale * grads[:, :width]
    grad_router = scale * grads[:, width : width + experts]

    grad_fc1 = wgrad(scale, slot_in, [r[3] for r in results])
    grad_fc2 = wgrad(scale, [r[2] for r in results], slot_cot)
    return (layer_out, d_residual, d_context, grad_out, grad_router, grad_fc1, grad_fc2)


def solution(mesh):
    rows = P(("dp", "expert"), None)
    first = P("expert", None, "dp")
    second = P("expert", "dp", None)

    return jax.shard_map(
        on_device,
        mesh=mesh,
        in_specs=(rows, rows, rows, P(), rows, first, second, rows),
        out_specs=(rows, rows, rows, rows, rows, first, second),
        check_vma=False,
    )
```

time: 580 us -> 381 us (0.66)
  waiting for transfers between devices: 408 us -> 135 us
  starting transfers between devices: 8.79 us -> 91.4 us
  Pallas kernels: 0 us -> 72.6 us
  matrix products: 70.5 us -> 41.1 us
  local copies, waits for them, and re-layouts: 40.3 us -> 12.3 us
  blocking collectives: 30.7 us -> 8.55 us
  between operations: 14.4 us -> 1.5 us
  other arithmetic: 6.44 us -> 16 us
    unnamed x9 -> x0, waiting for transfers between devices: 247 us -> none
    all_gather x3 -> x0, waiting for transfers between devices: 160 us -> none  [the longest x1 63.2 us: on_device(): w_full = lax.all_gather(w_out, ('dp', 'expert'), axis=0, tiled=True)]
    ppermute x0 -> x37, waiting for transfers between devices: none -> 98.3 us  [the longest x31 81 us: swap(): return lax.ppermute(value, axis, [(i, i ^ bit) for i in range(n)])]
    pallas_call x0 -> x4, Pallas kernels: none -> 72.6 us  [the longest x2 43.8 us: ffn(): pl.pallas_call(ffn_kernel, grid=(e, hidden // hc), in_specs=[src_spec, ro...]
    ppermute x0 -> x37, starting transfers between devices: none -> 57.2 us  [the longest x31 44.6 us: swap(): return lax.ppermute(value, axis, [(i, i ^ bit) for i in range(n)])]
    all_to_all x2 -> x8, waiting for transfers between devices: 1.61 us -> 37.1 us  [exchange(): lax.all_to_all(value, 'expert', split_axis=0, concat_axis=0, tiled=True)]
    dot_general x16 -> x33, matrix products: 70.5 us -> 41.1 us  [dot32(): lax.dot_general(a, b, (dims, ((), ())), preferred_element_type=F32, preci...]
    all_to_all x2 -> x8, starting transfers between devices: 7.88 us -> 34.2 us  [exchange(): lax.all_to_all(value, 'expert', split_axis=0, concat_axis=0, tiled=True)]
  transfers between devices with their start and end apart: 8 -> 45, of which waited for: 7 -> 21; matrix products, arithmetic and copies ran while one was open for 12% -> 16% of each run, Pallas kernels for 0% -> 13%
where the time goes in v1:
time: 381 us; the launch traced here: 379 us
  waiting for transfers between devices  135 us (35%)
  starting transfers between devices  91.4 us (24%)
  Pallas kernels  72.6 us (19%)
  matrix products  41.1 us (11%)
  other arithmetic  16 us (4%)
  local copies, waits for them, and re-layouts  12.3 us (3%)
  blocking collectives  8.55 us (2%)
    ppermute x31, waiting for transfers between devices, swap(): return lax.ppermute(value, axis, [(i, i ^ bit) for i in range(n)])  81 us
    ppermute x31, starting transfers between devices, swap(): return lax.ppermute(value, axis, [(i, i ^ bit) for i in range(n)])  44.6 us
    pallas_call x2, Pallas kernels, ffn(): pl.pallas_call(ffn_kernel, grid=(e, hidden // hc), in_specs=[src_spec, ro...  43.8 us
    dot_general x33, matrix products, dot32(): lax.dot_general(a, b, (dims, ((), ())), preferred_element_type=F32, preci...  41.1 us
    all_to_all x8, waiting for transfers between devices, exchange(): lax.all_to_all(value, 'expert', split_axis=0, concat_axis=0, tiled=True)  37.1 us
    all_to_all x8, starting transfers between devices, exchange(): lax.all_to_all(value, 'expert', split_axis=0, concat_axis=0, tiled=True)  34.2 us
    pallas_call x2, Pallas kernels, wgrad(): pl.pallas_call(functools.partial(wgrad_kernel, scale, len(lefts)), grid=(...  28.8 us
    ppermute x3, waiting for transfers between devices, line_steps(): cur_d = lax.ppermute(cur_d, axis, [(i, i - 1) for i in range(1, n - s + 1)])  17.1 us
  transfers between devices with their start and end apart: 45, of which 21 were waited for; matrix products, arithmetic and copies ran while one was open for 16% of the time, Pallas kernels for 13%

profile of v1, /device:TPU:0, one launch (start us, length us, event | category | flops | bytes accessed | tf_op | source)
XLA Modules:
  0.0 378.7 jit_solution(8311121188912920936)
XLA Ops:
  0.7 5.1 %collective-permute-start.10 = (s32[2,128]{1,0:T(2,128)}, s32[2,128]{1,0:T(2,128)S(1)}, u32[]{:S(2)}, u32[]{:S(2)}) collective-permute-start(s32[2,128]{1,0:T(2,128)} %bitcast.168), channel_id=1, source_target_pairs={{0,24},{8,16},{16,8},{24,0},{1,25},{9,17},{17,9},{25,1},{2,26},{10... | collective-permute-start | bytes 3080 | tf_op jit(solution)/shard_map/ppermute | solution.py:26
  6.4 2.3 collective-permute-start.1
  12.4 2.2 convolution_convert_fusion.4
  14.6 4.2 %all-to-all-start.1 = ((bf16[8,40,1280]{2,1,0:T(8,128)(2,1)}), bf16[8,40,1280]{2,1,0:T(8,128)(2,1)}, u32[]{:S(2)}, u32[]{:S(2)}) async-start(bf16[8,40,1280]{2,1,0:T(8,128)(2,1)} %bitcast.20), calls=%async_computation.1 | async-start | bytes 1638400 | tf_op jit(solution)/shard_map/all_to_all | solution.py:30
  20.7 6.5 %collective-permute-done.2 = bf16[40,1280]{1,0:T(8,128)(2,1)S(1)} collective-permute-done((bf16[40,1280]{1,0:T(8,128)(2,1)S(1)}, bf16[40,1280]{1,0:T(8,128)(2,1)S(1)}, u32[]{:S(2)}, u32[]{:S(2)}) %collective-permute-start.2) | collective-permute-done | bytes 102432 | tf_op jit(solution)/shard_map/ppermute | solution.py:26
  30.4 9.2 %collective-permute-done.4 = bf16[160,1280]{1,0:T(8,128)(2,1)S(1)} collective-permute-done((bf16[160,1280]{1,0:T(8,128)(2,1)S(1)}, bf16[160,1280]{1,0:T(8,128)(2,1)S(1)}, u32[]{:S(2)}, u32[]{:S(2)}) %collective-permute-start.4) | collective-permute-done | bytes 409632 | tf_op jit(solution)/shard_map/ppermute | solution.py:26
  41.9 5.6 %collective-permute-done.5 = bf16[80,1280]{1,0:T(8,128)(2,1)S(1)} collective-permute-done((bf16[80,1280]{1,0:T(8,128)(2,1)S(1)}, bf16[80,1280]{1,0:T(8,128)(2,1)S(1)}, u32[]{:S(2)}, u32[]{:S(2)}) %collective-permute-start.5) | collective-permute-done | bytes 204832 | tf_op jit(solution)/shard_map/ppermute | solution.py:26
  50.2 5.4 %collective-permute-start.12 = (bf16[320,1280]{1,0:T(8,128)(2,1)}, bf16[320,1280]{1,0:T(8,128)(2,1)}, u32[]{:S(2)}, u32[]{:S(2)}) collective-permute-start(bf16[320,1280]{1,0:T(8,128)(2,1)} %bitcast.21), channel_id=1, source_target_pairs={{0,8},{8,16},{16,24},{1,9},{9,17},{17,25},{2,10},{10,18},{18,26},{... | collective-permute-start | bytes 2457608 | tf_op jit(solution)/shard_map/ppermute | solution.py:38
  59.6 3.3 all-to-all-start.2
  63.0 9.3 %collective-permute-done.13 = bf16[320,1280]{1,0:T(8,128)(2,1)} collective-permute-done((bf16[320,1280]{1,0:T(8,128)(2,1)}, bf16[320,1280]{1,0:T(8,128)(2,1)}, u32[]{:S(2)}, u32[]{:S(2)}) %collective-permute-start.13) | collective-permute-done | bytes 819232 | tf_op jit(solution)/shard_map/ppermute | solution.py:39
  75.4 4.5 %collective-permute-done.11 = bf16[128,1280]{1,0:T(8,128)(2,1)} collective-permute-done((bf16[128,1280]{1,0:T(8,128)(2,1)S(1)}, bf16[128,1280]{1,0:T(8,128)(2,1)}, u32[]{:S(2)}, u32[]{:S(2)}) %collective-permute-start.11) | collective-permute-done | bytes 327712 | tf_op jit(solution)/shard_map/ppermute | solution.py:26
  79.9 2.8 convolution_convert_fusion.1
  82.7 4.4 %all-to-all-start = ((bf16[8,80,1280]{2,1,0:T(8,128)(2,1)}), bf16[8,80,1280]{2,1,0:T(8,128)(2,1)}, u32[]{:S(2)}, u32[]{:S(2)}) async-start(bf16[8,80,1280]{2,1,0:T(8,128)(2,1)} %bitcast.157), calls=%async_computation | async-start | bytes 3276800 | tf_op jit(solution)/shard_map/all_to_all | solution.py:30
  88.5 7.8 %collective-permute-done.18 = bf16[320,1280]{1,0:T(8,128)(2,1)} collective-permute-done((bf16[320,1280]{1,0:T(8,128)(2,1)}, bf16[320,1280]{1,0:T(8,128)(2,1)}, u32[]{:S(2)}, u32[]{:S(2)}) %collective-permute-start.18) | collective-permute-done | bytes 819232 | tf_op jit(solution)/shard_map/ppermute | solution.py:39
  100.4 2.3 collective-permute-start.16
  102.7 2.7 collective-permute-start.15
  107.5 5.4 %collective-permute-done.16 = bf16[128,1280]{1,0:T(8,128)(2,1)S(1)} collective-permute-done((bf16[128,1280]{1,0:T(8,128)(2,1)S(1)}, bf16[128,1280]{1,0:T(8,128)(2,1)S(1)}, u32[]{:S(2)}, u32[]{:S(2)}) %collective-permute-start.16) | collective-permute-done | bytes 327712 | tf_op jit(solution)/shard_map/ppermute | solution.py:26
  112.9 19.6 %collective-permute-done.15 = bf16[128,1280]{1,0:T(8,128)(2,1)S(1)} collective-permute-done((bf16[128,1280]{1,0:T(8,128)(2,1)S(1)}, bf16[128,1280]{1,0:T(8,128)(2,1)S(1)}, u32[]{:S(2)}, u32[]{:S(2)}) %collective-permute-start.15) | collective-permute-done | bytes 327712 | tf_op jit(solution)/shard_map/ppermute | solution.py:26
  134.3 4.5 %all-to-all-start.4 = ((bf16[8,80,1280]{2,1,0:T(8,128)(2,1)}), bf16[8,80,1280]{2,1,0:T(8,128)(2,1)}, u32[]{:S(2)}, u32[]{:S(2)}) async-start(bf16[8,80,1280]{2,1,0:T(8,128)(2,1)} %bitcast.159), calls=%async_computation.4 | async-start | bytes 3276800 | tf_op jit(solution)/shard_map/all_to_all | solution.py:30
  140.7 3.9 %convolution_convert_fusion.3 = bf16[640,1280]{1,0:T(8,128)(2,1)} fusion(bf16[320,1280]{1,0:T(8,128)(2,1)S(1)} %get-tuple-element.88, bf16[320,1280]{1,0:T(8,128)(2,1)} %bitcast.21, s32[640]{0:T(1024)S(1)} %fusion.148), kind=kOutput, calls=%fused_computation.15 | convolution fusion | flops 1053081600 | bytes 3279360 | tf_op jit(solution)/shard_map/dot_general | solution.py:19
  144.6 2.7 convolution_convert_fusion.2
  147.3 21.8 %shard_map.135 = (bf16[8,2,40,1280]{3,2,1,0:T(8,128)(2,1)}, bf16[8,2,40,1280]{3,2,1,0:T(8,128)(2,1)}, bf16[2,320,1280]{2,1,0:T(8,128)(2,1)}, bf16[2,320,1280]{2,1,0:T(8,128)(2,1)}, f32[2,320,1]{2,1,0:T(8,128)}) custom-call(bf16[8,2,40,1280]{3,2,1,0:T(8,128)(2,1)} %bitcast.13.x_ref.refs_0_, bf16[2,320,1280]{2,1,0:T(8,128)(2,1)} %bitcast.150, ...), custom_call_target="tpu_custom_call" | custom-call | flops 8388608000 | bytes 26214400 | tf_op jit(solution)/shard_map/pallas_call | solution.py:111
  170.5 22.0 %shard_map.136 = (bf16[8,2,40,1280]{3,2,1,0:T(8,128)(2,1)}, bf16[8,2,40,1280]{3,2,1,0:T(8,128)(2,1)}, bf16[2,320,1280]{2,1,0:T(8,128)(2,1)}, bf16[2,320,1280]{2,1,0:T(8,128)(2,1)}, f32[2,320,1]{2,1,0:T(8,128)}) custom-call(bf16[8,2,40,1280]{3,2,1,0:T(8,128)(2,1)} %bitcast.37.x_ref.refs_1_, bf16[2,320,1280]{2,1,0:T(8,128)(2,1)} %bitcast.152, ...), custom_call_target="tpu_custom_call" | custom-call | flops 8388608000 | bytes 26214400 | tf_op jit(solution)/shard_map/pallas_call | solution.py:111
  193.9 8.5 %all_to_all.96 = f32[8,8,128]{2,1,0:T(8,128)S(1)} all-to-all(f32[8,8,128]{2,1,0:T(8,128)S(1)} %copy.42), channel_id=1, replica_groups=mesh['dp'=4,'expert'=8] {'expert'}, dimensions={0} | all-to-all | bytes 65536 | tf_op jit(solution)/shard_map/all_to_all | solution.py:30
  202.4 4.3 %all-to-all-start.3 = ((bf16[8,80,1280]{2,1,0:T(8,128)(2,1)}), bf16[8,80,1280]{2,1,0:T(8,128)(2,1)}, u32[]{:S(2)}, u32[]{:S(2)}) async-start(bf16[8,80,1280]{2,1,0:T(8,128)(2,1)} %bitcast.158), calls=%async_computation.3 | async-start | bytes 3276800 | tf_op jit(solution)/shard_map/all_to_all | solution.py:30
  208.2 20.3 %all-to-all-done.3 = bf16[8,80,1280]{2,1,0:T(8,128)(2,1)} async-done(((bf16[8,80,1280]{2,1,0:T(8,128)(2,1)}), bf16[8,80,1280]{2,1,0:T(8,128)(2,1)}, u32[]{:S(2)}, u32[]{:S(2)}) %all-to-all-start.3) | async-done | bytes 1638432 | tf_op jit(solution)/shard_map/all_to_all | solution.py:30
  228.4 4.3 %all-to-all-start.5 = ((bf16[8,80,1280]{2,1,0:T(8,128)(2,1)}), bf16[8,80,1280]{2,1,0:T(8,128)(2,1)}, u32[]{:S(2)}, u32[]{:S(2)}) async-start(bf16[8,80,1280]{2,1,0:T(8,128)(2,1)} %bitcast.156), calls=%async_computation.5 | async-start | bytes 3276800 | tf_op jit(solution)/shard_map/all_to_all | solution.py:30
  232.8 2.5 collective-permute-start.25
  236.7 14.4 %shard_map.137 = f32[2,1280,1280]{2,1,0:T(8,128)} custom-call(bf16[8,2,40,1280]{3,2,1,0:T(8,128)(2,1)} %bitcast.13.x_ref.refs_0_, bf16[8,2,40,1280]{3,2,1,0:T(8,128)(2,1)} %bitcast.37.x_ref.refs_1_, bf16[2,320,1280]{2,1,0:T(8,128)(2,1)} %get-tuple-element.35.refs_2_, bf16[2,320,1280]{2,1,0:T(8,128)(2,1)} %get-tuple-element.36.refs_3_), custom_call_target="tpu_custom_call" | custom-call | flops 4194304000 | bytes 19660800 | tf_op jit(solution)/shard_map/pallas_call | solution.py:166
  251.2 3.3 all-to-all-done.5
  254.4 4.5 %all-to-all-start.7 = ((bf16[8,80,1280]{2,1,0:T(8,128)(2,1)}), bf16[8,80,1280]{2,1,0:T(8,128)(2,1)}, u32[]{:S(2)}, u32[]{:S(2)}) async-start(bf16[8,80,1280]{2,1,0:T(8,128)(2,1)} %bitcast.155), calls=%async_computation.7 | async-start | bytes 3276800 | tf_op jit(solution)/shard_map/all_to_all | solution.py:30
  265.2 3.0 collective-permute-start.21
  269.6 4.5 %fusion.2 = f32[1280,16]{1,0:T(8,128)} fusion(f32[1280,16]{0,1:T(8,128)S(1)} %fusion.132, s32[1280]{0:T(1024)S(1)} %fusion.122), kind=kOutput, calls=%fused_computation.5 | convolution fusion | flops 317849600 | bytes 168960 | tf_op jit(solution)/shard_map/dot_general | solution.py:19
  274.1 6.4 %all-to-all-done.7 = bf16[8,80,1280]{2,1,0:T(8,128)(2,1)} async-done(((bf16[8,80,1280]{2,1,0:T(8,128)(2,1)}), bf16[8,80,1280]{2,1,0:T(8,128)(2,1)}, u32[]{:S(2)}, u32[]{:S(2)}) %all-to-all-start.7) | async-done | bytes 1638432 | tf_op jit(solution)/shard_map/all_to_all | solution.py:30
  280.5 4.6 %all-to-all-start.8 = ((bf16[8,80,1280]{2,1,0:T(8,128)(2,1)}), bf16[8,80,1280]{2,1,0:T(8,128)(2,1)}, u32[]{:S(2)}, u32[]{:S(2)}) async-start(bf16[8,80,1280]{2,1,0:T(8,128)(2,1)} %bitcast.154), calls=%async_computation.8 | async-start | bytes 3276800 | tf_op jit(solution)/shard_map/all_to_all | solution.py:30
  285.0 2.2 fusion.50
  288.1 3.0 collective-permute-done.21
  295.0 2.9 copy-done.2
  299.3 7.2 %all-to-all-done.8 = bf16[8,80,1280]{2,1,0:T(8,128)(2,1)} async-done(((bf16[8,80,1280]{2,1,0:T(8,128)(2,1)}), bf16[8,80,1280]{2,1,0:T(8,128)(2,1)}, u32[]{:S(2)}, u32[]{:S(2)}) %all-to-all-start.8) | async-done | bytes 1638432 | tf_op jit(solution)/shard_map/all_to_all | solution.py:30
  311.9 14.4 %shard_map.138 = f32[2,1280,1280]{2,1,0:T(8,128)} custom-call(bf16[2,320,1280]{2,1,0:T(8,128)(2,1)} %get-tuple-element.37.refs_0_, bf16[2,320,1280]{2,1,0:T(8,128)(2,1)} %get-tuple-element.38.refs_1_, bf16[2,320,1280]{2,1,0:T(8,128)(2,1)} %bitcast.151, bf16[2,320,1280]{2,1,0:T(8,128)(2,1)} %bitcast.153), custom_call_target="tpu_custom_call" | custom-call | flops 4194304000 | bytes 19660800 | tf_op jit(solution)/shard_map/pallas_call | solution.py:166
  326.9 7.0 %collective-permute-done.27 = bf16[128,1280]{1,0:T(8,128)(2,1)S(1)} collective-permute-done((bf16[128,1280]{1,0:T(8,128)(2,1)}, bf16[128,1280]{1,0:T(8,128)(2,1)S(1)}, u32[]{:S(2)}, u32[]{:S(2)}) %collective-permute-start.27) | collective-permute-done | bytes 327712 | tf_op jit(solution)/shard_map/ppermute | solution.py:26
  335.8 3.0 fusion.230
  343.6 5.2 %collective-permute-done.30 = bf16[320,640]{1,0:T(8,128)(2,1)S(1)} collective-permute-done((bf16[320,640]{1,0:T(8,128)(2,1)S(1)}, bf16[320,640]{1,0:T(8,128)(2,1)S(1)}, u32[]{:S(2)}, u32[]{:S(2)}) %collective-permute-start.30) | collective-permute-done | bytes 409632 | tf_op jit(solution)/shard_map/ppermute | solution.py:26
  350.0 4.4 %collective-permute-done.32 = bf16[320,768]{1,0:T(8,128)(2,1)S(1)} collective-permute-done((bf16[320,768]{1,0:T(8,128)(2,1)S(1)}, bf16[320,768]{1,0:T(8,128)(2,1)S(1)}, u32[]{:S(2)}, u32[]{:S(2)}) %collective-permute-start.32) | collective-permute-done | bytes 491552 | tf_op jit(solution)/shard_map/ppermute | solution.py:26
  356.6 4.1 %collective-permute-done.33 = bf16[160,768]{1,0:T(8,128)(2,1)S(1)} collective-permute-done((bf16[160,768]{1,0:T(8,128)(2,1)S(1)}, bf16[160,768]{1,0:T(8,128)(2,1)S(1)}, u32[]{:S(2)}, u32[]{:S(2)}) %collective-permute-start.33) | collective-permute-done | bytes 245792 | tf_op jit(solution)/shard_map/ppermute | solution.py:26
  361.0 7.3 %collective-permute-start.34 = (bf16[40,1408]{1,0:T(8,128)(2,1)S(1)}, bf16[40,1408]{1,0:T(8,128)(2,1)S(1)}, u32[]{:S(2)}, u32[]{:S(2)}) collective-permute-start(bf16[40,1408]{1,0:T(8,128)(2,1)S(1)} %get-tuple-element.93), channel_id=1, source_target_pairs={{0,8},{8,0},{16,24},{24,16},{1,9},{9,1},{17,25},{25,17},{2,10},{10... | collective-permute-start | bytes 337928 | tf_op jit(solution)/shard_map/ppermute | solution.py:26
  368.3 2.4 collective-permute-start.36
  374.9 2.4 collective-permute-done.35
  (213 shorter events, 73.5 us)
Async XLA Ops:
  0.6 18.4 %copy-start = (bf16[128,1280]{1,0:T(8,128)(2,1)S(1)}, bf16[128,1280]{1,0:T(8,128)(2,1)}, u32[]{:S(2)}) copy-start(bf16[128,1280]{1,0:T(8,128)(2,1)} %param.9) | copy-start | bytes 983044
  0.6 18.3 %copy-start.13 = (bf16[40,1280]{1,0:T(8,128)(2,1)S(1)}, bf16[40,1280]{1,0:T(8,128)(2,1)}, u32[]{:S(2)}) copy-start(bf16[40,1280]{1,0:T(8,128)(2,1)} %param.10) | copy-start | bytes 307204
  0.7 19.4 %collective-permute-start.10 = (s32[2,128]{1,0:T(2,128)}, s32[2,128]{1,0:T(2,128)S(1)}, u32[]{:S(2)}, u32[]{:S(2)}) collective-permute-start(s32[2,128]{1,0:T(2,128)} %bitcast.168), channel_id=1, source_target_pairs={{0,24},{8,16},{16,8},{24,0},{1,25},{9,17},{17,9},{25,1},{2,26},{10... | collective-permute-start | bytes 3080 | tf_op jit(solution)/shard_map/ppermute | solution.py:26
  5.8 14.5 %collective-permute-start.9 = (s32[2,128]{1,0:T(2,128)}, s32[2,128]{1,0:T(2,128)S(1)}, u32[]{:S(2)}, u32[]{:S(2)}) collective-permute-start(s32[2,128]{1,0:T(2,128)} %bitcast.169), channel_id=1, source_target_pairs={{0,16},{8,24},{16,0},{24,8},{1,17},{9,25},{17,1},{25,9},{2,18},{10... | collective-permute-start | bytes 3080 | tf_op jit(solution)/shard_map/ppermute | solution.py:26
  5.8 14.5 %collective-permute-start.8 = (s32[2,128]{1,0:T(2,128)}, s32[2,128]{1,0:T(2,128)S(1)}, u32[]{:S(2)}, u32[]{:S(2)}) collective-permute-start(s32[2,128]{1,0:T(2,128)} %bitcast.170), channel_id=1, source_target_pairs={{0,8},{8,0},{16,24},{24,16},{1,9},{9,1},{17,25},{25,17},{2,10},{10... | collective-permute-start | bytes 3080 | tf_op jit(solution)/shard_map/ppermute | solution.py:26
  6.4 14.2 %collective-permute-start.1 = (bf16[40,1280]{1,0:T(8,128)(2,1)}, bf16[40,1280]{1,0:T(8,128)(2,1)S(1)}, u32[]{:S(2)}, u32[]{:S(2)}) collective-permute-start(bf16[40,1280]{1,0:T(8,128)(2,1)} %param.10), channel_id=1, source_target_pairs={{0,16},{8,24},{16,0},{24,8},{1,17},{9,25},{17,1},{25,9},{2,18},{10... | collective-permute-start | bytes 307208 | tf_op jit(solution)/shard_map/ppermute | solution.py:26
  8.7 11.9 %collective-permute-start = (bf16[40,1280]{1,0:T(8,128)(2,1)}, bf16[40,1280]{1,0:T(8,128)(2,1)S(1)}, u32[]{:S(2)}, u32[]{:S(2)}) collective-permute-start(bf16[40,1280]{1,0:T(8,128)(2,1)} %param.10), channel_id=1, source_target_pairs={{0,8},{8,0},{16,24},{24,16},{1,9},{9,1},{17,25},{25,17},{2,10},{10... | collective-permute-start | bytes 307208 | tf_op jit(solution)/shard_map/ppermute | solution.py:26
  14.6 34.3 %all-to-all-start.1 = ((bf16[8,40,1280]{2,1,0:T(8,128)(2,1)}), bf16[8,40,1280]{2,1,0:T(8,128)(2,1)}, u32[]{:S(2)}, u32[]{:S(2)}) async-start(bf16[8,40,1280]{2,1,0:T(8,128)(2,1)} %bitcast.20), calls=%async_computation.1 | async-start | bytes 1638400 | tf_op jit(solution)/shard_map/all_to_all | solution.py:30
  20.1 7.0 %collective-permute-start.2 = (bf16[40,1280]{1,0:T(8,128)(2,1)S(1)}, bf16[40,1280]{1,0:T(8,128)(2,1)S(1)}, u32[]{:S(2)}, u32[]{:S(2)}) collective-permute-start(bf16[40,1280]{1,0:T(8,128)(2,1)S(1)} %copy-done.13), channel_id=1, source_target_pairs={{0,24},{8,16},{16,8},{24,0},{1,25},{9,17},{17,9},{25,1},{2,26},{10... | collective-permute-start | bytes 307208 | tf_op jit(solution)/shard_map/ppermute | solution.py:26
  27.1 12.4 %collective-permute-start.4 = (bf16[160,1280]{1,0:T(8,128)(2,1)S(1)}, bf16[160,1280]{1,0:T(8,128)(2,1)S(1)}, u32[]{:S(2)}, u32[]{:S(2)}) collective-permute-start(bf16[160,1280]{1,0:T(8,128)(2,1)S(1)} %get-tuple-element.96), channel_id=1, source_target_pairs={{0,2},{1,3},{2,0},{3,1},{4,6},{5,7},{6,4},{7,5},{8,10},{9,11},{10,... | collective-permute-start | bytes 1228808 | tf_op jit(solution)/shard_map/ppermute | solution.py:26
  28.9 12.3 %collective-permute-start.3 = (bf16[160,1280]{1,0:T(8,128)(2,1)S(1)}, bf16[160,1280]{1,0:T(8,128)(2,1)S(1)}, u32[]{:S(2)}, u32[]{:S(2)}) collective-permute-start(bf16[160,1280]{1,0:T(8,128)(2,1)S(1)} %get-tuple-element.96), channel_id=1, source_target_pairs={{0,4},{1,5},{2,6},{3,7},{4,0},{5,1},{6,2},{7,3},{8,12},{9,13},{10,... | collective-permute-start | bytes 1228808 | tf_op jit(solution)/shard_map/ppermute | solution.py:26
  39.6 7.9 %collective-permute-start.6 = (bf16[80,1280]{1,0:T(8,128)(2,1)S(1)}, bf16[80,1280]{1,0:T(8,128)(2,1)S(1)}, u32[]{:S(2)}, u32[]{:S(2)}) collective-permute-start(bf16[80,1280]{1,0:T(8,128)(2,1)S(1)} %slice.270), channel_id=1, source_target_pairs={{0,4},{1,5},{2,6},{3,7},{4,0},{5,1},{6,2},{7,3},{8,12},{9,13},{10,... | collective-permute-start | bytes 614408 | tf_op jit(solution)/shard_map/ppermute | solution.py:26
  41.2 6.3 %collective-permute-start.5 = (bf16[80,1280]{1,0:T(8,128)(2,1)S(1)}, bf16[80,1280]{1,0:T(8,128)(2,1)S(1)}, u32[]{:S(2)}, u32[]{:S(2)}) collective-permute-start(bf16[80,1280]{1,0:T(8,128)(2,1)S(1)} %slice.269), channel_id=1, source_target_pairs={{0,2},{1,3},{2,0},{3,1},{4,6},{5,7},{6,4},{7,5},{8,10},{9,11},{10,... | collective-permute-start | bytes 614408 | tf_op jit(solution)/shard_map/ppermute | solution.py:26
  47.6 8.1 %collective-permute-start.7 = (bf16[640,1280]{1,0:T(8,128)(2,1)S(1)}, bf16[640,1280]{1,0:T(8,128)(2,1)}, u32[]{:S(2)}, u32[]{:S(2)}) collective-permute-start(bf16[640,1280]{1,0:T(8,128)(2,1)S(1)} %constant_dynamic-update-slice_fusion.4), channel_id=1, source_target_pairs={{0,1},{1,0},{2,3},{3,2},{4,5},{5,4},{6,7},{7,6},{8,9},{9,8},{10,11... | collective-permute-start | bytes 4915208 | tf_op jit(solution)/shard_map/ppermute | solution.py:26
  48.9 23.3 %collective-permute-start.13 = (bf16[320,1280]{1,0:T(8,128)(2,1)}, bf16[320,1280]{1,0:T(8,128)(2,1)}, u32[]{:S(2)}, u32[]{:S(2)}) collective-permute-start(bf16[320,1280]{1,0:T(8,128)(2,1)} %bitcast.21), channel_id=1, source_target_pairs={{8,0},{16,8},{24,16},{9,1},{17,9},{25,17},{10,2},{18,10},{26,18},{... | collective-permute-start | bytes 2457608 | tf_op jit(solution)/shard_map/ppermute | solution.py:39
  50.2 23.5 %collective-permute-start.12 = (bf16[320,1280]{1,0:T(8,128)(2,1)}, bf16[320,1280]{1,0:T(8,128)(2,1)}, u32[]{:S(2)}, u32[]{:S(2)}) collective-permute-start(bf16[320,1280]{1,0:T(8,128)(2,1)} %bitcast.21), channel_id=1, source_target_pairs={{0,8},{8,16},{16,24},{1,9},{9,17},{17,25},{2,10},{10,18},{18,26},{... | collective-permute-start | bytes 2457608 | tf_op jit(solution)/shard_map/ppermute | solution.py:38
  58.5 21.4 %collective-permute-start.11 = (bf16[128,1280]{1,0:T(8,128)(2,1)S(1)}, bf16[128,1280]{1,0:T(8,128)(2,1)}, u32[]{:S(2)}, u32[]{:S(2)}) collective-permute-start(bf16[128,1280]{1,0:T(8,128)(2,1)S(1)} %fusion.44), channel_id=1, source_target_pairs={{0,8},{8,0},{16,24},{24,16},{1,9},{9,1},{17,25},{25,17},{2,10},{10... | collective-permute-start | bytes 983048 | tf_op jit(solution)/shard_map/ppermute | solution.py:26
  59.6 23.0 %all-to-all-start.2 = ((f32[8,8,128]{2,1,0:T(8,128)}), f32[8,8,128]{2,1,0:T(8,128)S(1)}, u32[]{:S(2)}, u32[]{:S(2)}) async-start(f32[8,8,128]{2,1,0:T(8,128)} %bitcast.147), calls=%async_computation.2 | async-start | bytes 65536 | tf_op jit(solution)/shard_map/all_to_all | solution.py:30
  72.3 24.1 %collective-permute-start.18 = (bf16[320,1280]{1,0:T(8,128)(2,1)}, bf16[320,1280]{1,0:T(8,128)(2,1)}, u32[]{:S(2)}, u32[]{:S(2)}) collective-permute-start(bf16[320,1280]{1,0:T(8,128)(2,1)} %collective-permute-done.13), channel_id=1, source_target_pairs={{8,0},{16,8},{9,1},{17,9},{10,2},{18,10},{11,3},{19,11},{12,4},{20... | collective-permute-start | bytes 2457608 | tf_op jit(solution)/shard_map/ppermute | solution.py:39
  73.7 23.9 %collective-permute-start.17 = (bf16[320,1280]{1,0:T(8,128)(2,1)}, bf16[320,1280]{1,0:T(8,128)(2,1)}, u32[]{:S(2)}, u32[]{:S(2)}) collective-permute-start(bf16[320,1280]{1,0:T(8,128)(2,1)} %collective-permute-done.12), channel_id=1, source_target_pairs={{8,16},{16,24},{9,17},{17,25},{10,18},{18,26},{11,19},{19,27},{12,... | collective-permute-start | bytes 2457608 | tf_op jit(solution)/shard_map/ppermute | solution.py:38
  82.7 51.7 %all-to-all-start = ((bf16[8,80,1280]{2,1,0:T(8,128)(2,1)}), bf16[8,80,1280]{2,1,0:T(8,128)(2,1)}, u32[]{:S(2)}, u32[]{:S(2)}) async-start(bf16[8,80,1280]{2,1,0:T(8,128)(2,1)} %bitcast.157), calls=%async_computation | async-start | bytes 3276800 | tf_op jit(solution)/shard_map/all_to_all | solution.py:30
  96.4 42.4 %collective-permute-start.20 = (bf16[320,1280]{1,0:T(8,128)(2,1)}, bf16[320,1280]{1,0:T(8,128)(2,1)}, u32[]{:S(2)}, u32[]{:S(2)}) collective-permute-start(bf16[320,1280]{1,0:T(8,128)(2,1)} %collective-permute-done.18), channel_id=1, source_target_pairs={{8,0},{9,1},{10,2},{11,3},{12,4},{13,5},{14,6},{15,7}} | collective-permute-start | bytes 2457608 | tf_op jit(solution)/shard_map/ppermute | solution.py:39
  97.7 41.1 %collective-permute-start.19 = (bf16[320,1280]{1,0:T(8,128)(2,1)}, bf16[320,1280]{1,0:T(8,128)(2,1)}, u32[]{:S(2)}, u32[]{:S(2)}) collective-permute-start(bf16[320,1280]{1,0:T(8,128)(2,1)} %collective-permute-done.17), channel_id=1, source_target_pairs={{16,24},{17,25},{18,26},{19,27},{20,28},{21,29},{22,30},{23,31}} | collective-permute-start | bytes 2457608 | tf_op jit(solution)/shard_map/ppermute | solution.py:38
  100.4 12.5 %collective-permute-start.16 = (bf16[128,1280]{1,0:T(8,128)(2,1)S(1)}, bf16[128,1280]{1,0:T(8,128)(2,1)S(1)}, u32[]{:S(2)}, u32[]{:S(2)}) collective-permute-start(bf16[128,1280]{1,0:T(8,128)(2,1)S(1)} %fusion.44), channel_id=1, source_target_pairs={{0,24},{8,16},{16,8},{24,0},{1,25},{9,17},{17,9},{25,1},{2,26},{10... | collective-permute-start | bytes 983048 | tf_op jit(solution)/shard_map/ppermute | solution.py:26
  102.7 29.8 %collective-permute-start.15 = (bf16[128,1280]{1,0:T(8,128)(2,1)S(1)}, bf16[128,1280]{1,0:T(8,128)(2,1)S(1)}, u32[]{:S(2)}, u32[]{:S(2)}) collective-permute-start(bf16[128,1280]{1,0:T(8,128)(2,1)S(1)} %fusion.44), channel_id=1, source_target_pairs={{0,16},{8,24},{16,0},{24,8},{1,17},{9,25},{17,1},{25,9},{2,18},{10... | collective-permute-start | bytes 983048 | tf_op jit(solution)/shard_map/ppermute | solution.py:26
  134.3 36.2 %all-to-all-start.4 = ((bf16[8,80,1280]{2,1,0:T(8,128)(2,1)}), bf16[8,80,1280]{2,1,0:T(8,128)(2,1)}, u32[]{:S(2)}, u32[]{:S(2)}) async-start(bf16[8,80,1280]{2,1,0:T(8,128)(2,1)} %bitcast.159), calls=%async_computation.4 | async-start | bytes 3276800 | tf_op jit(solution)/shard_map/all_to_all | solution.py:30
  202.4 26.0 %all-to-all-start.3 = ((bf16[8,80,1280]{2,1,0:T(8,128)(2,1)}), bf16[8,80,1280]{2,1,0:T(8,128)(2,1)}, u32[]{:S(2)}, u32[]{:S(2)}) async-start(bf16[8,80,1280]{2,1,0:T(8,128)(2,1)} %bitcast.158), calls=%async_computation.3 | async-start | bytes 3276800 | tf_op jit(solution)/shard_map/all_to_all | solution.py:30
  228.4 26.0 %all-to-all-start.5 = ((bf16[8,80,1280]{2,1,0:T(8,128)(2,1)}), bf16[8,80,1280]{2,1,0:T(8,128)(2,1)}, u32[]{:S(2)}, u32[]{:S(2)}) async-start(bf16[8,80,1280]{2,1,0:T(8,128)(2,1)} %bitcast.156), calls=%async_computation.5 | async-start | bytes 3276800 | tf_op jit(solution)/shard_map/all_to_all | solution.py:30
  232.7 18.4 %collective-permute-start.24 = (f32[2,128]{1,0:T(2,128)S(1)}, f32[2,128]{1,0:T(2,128)S(1)}, u32[]{:S(2)}, u32[]{:S(2)}) collective-permute-start(f32[2,128]{1,0:T(2,128)S(1)} %get-tuple-element.108), channel_id=1, source_target_pairs={{0,16},{8,24},{16,0},{24,8},{1,17},{9,25},{17,1},{25,9},{2,18},{10... | collective-permute-start | bytes 3080 | tf_op jit(solution)/shard_map/ppermute | solution.py:26
  232.8 18.3 %collective-permute-start.25 = (f32[2,128]{1,0:T(2,128)S(1)}, f32[2,128]{1,0:T(2,128)S(1)}, u32[]{:S(2)}, u32[]{:S(2)}) collective-permute-start(f32[2,128]{1,0:T(2,128)S(1)} %get-tuple-element.109), channel_id=1, source_target_pairs={{0,24},{8,16},{16,8},{24,0},{1,25},{9,17},{17,9},{25,1},{2,26},{10... | collective-permute-start | bytes 3080 | tf_op jit(solution)/shard_map/ppermute | solution.py:26
  235.6 15.5 %collective-permute-start.23 = (f32[2,128]{1,0:T(2,128)S(1)}, f32[2,128]{1,0:T(2,128)S(1)}, u32[]{:S(2)}, u32[]{:S(2)}) collective-permute-start(f32[2,128]{1,0:T(2,128)S(1)} %pad_maximum_fusion.3), channel_id=1, source_target_pairs={{0,8},{8,0},{16,24},{24,16},{1,9},{9,1},{17,25},{25,17},{2,10},{10... | collective-permute-start | bytes 3080 | tf_op jit(solution)/shard_map/ppermute | solution.py:26
  254.4 26.0 %all-to-all-start.7 = ((bf16[8,80,1280]{2,1,0:T(8,128)(2,1)}), bf16[8,80,1280]{2,1,0:T(8,128)(2,1)}, u32[]{:S(2)}, u32[]{:S(2)}) async-start(bf16[8,80,1280]{2,1,0:T(8,128)(2,1)} %bitcast.155), calls=%async_computation.7 | async-start | bytes 3276800 | tf_op jit(solution)/shard_map/all_to_all | solution.py:30
  262.2 25.9 %collective-permute-start.14 = (bf16[128,1280]{1,0:T(8,128)(2,1)}, bf16[128,1280]{1,0:T(8,128)(2,1)S(1)}, u32[]{:S(2)}, u32[]{:S(2)}) collective-permute-start(bf16[128,1280]{1,0:T(8,128)(2,1)} %slice.423), channel_id=1, source_target_pairs={{0,8},{8,0},{16,24},{24,16},{1,9},{9,1},{17,25},{25,17},{2,10},{10... | collective-permute-start | bytes 983048 | tf_op jit(solution)/shard_map/ppermute | solution.py:26
  265.2 25.9 %collective-permute-start.21 = (bf16[128,1280]{1,0:T(8,128)(2,1)}, bf16[128,1280]{1,0:T(8,128)(2,1)}, u32[]{:S(2)}, u32[]{:S(2)}) collective-permute-start(bf16[128,1280]{1,0:T(8,128)(2,1)} %get-tuple-element.91), channel_id=1, source_target_pairs={{0,16},{8,24},{16,0},{24,8},{1,17},{9,25},{17,1},{25,9},{2,18},{10... | collective-permute-start | bytes 983048 | tf_op jit(solution)/shard_map/ppermute | solution.py:26
  268.2 23.0 %collective-permute-start.22 = (bf16[128,1280]{1,0:T(8,128)(2,1)}, bf16[128,1280]{1,0:T(8,128)(2,1)}, u32[]{:S(2)}, u32[]{:S(2)}) collective-permute-start(bf16[128,1280]{1,0:T(8,128)(2,1)} %get-tuple-element.92), channel_id=1, source_target_pairs={{0,24},{8,16},{16,8},{24,0},{1,25},{9,17},{17,9},{25,1},{2,26},{10... | collective-permute-start | bytes 983048 | tf_op jit(solution)/shard_map/ppermute | solution.py:26
  280.5 26.0 %all-to-all-start.8 = ((bf16[8,80,1280]{2,1,0:T(8,128)(2,1)}), bf16[8,80,1280]{2,1,0:T(8,128)(2,1)}, u32[]{:S(2)}, u32[]{:S(2)}) async-start(bf16[8,80,1280]{2,1,0:T(8,128)(2,1)} %bitcast.154), calls=%async_computation.8 | async-start | bytes 3276800 | tf_op jit(solution)/shard_map/all_to_all | solution.py:30
  288.1 38.8 %collective-permute-start.26 = (bf16[128,1280]{1,0:T(8,128)(2,1)}, bf16[128,1280]{1,0:T(8,128)(2,1)S(1)}, u32[]{:S(2)}, u32[]{:S(2)}) collective-permute-start(bf16[128,1280]{1,0:T(8,128)(2,1)} %slice.422), channel_id=1, source_target_pairs={{0,8},{8,0},{16,24},{24,16},{1,9},{9,1},{17,25},{25,17},{2,10},{10... | collective-permute-start | bytes 983048 | tf_op jit(solution)/shard_map/ppermute | solution.py:26
  293.3 48.2 %copy-start.3 = (bf16[128,1280]{1,0:T(8,128)(2,1)}, bf16[128,1280]{1,0:T(8,128)(2,1)S(1)}, u32[]{:S(2)}) copy-start(bf16[128,1280]{1,0:T(8,128)(2,1)S(1)} %add_convert_fusion) | copy-start | bytes 983044
  299.3 36.5 %collective-permute-start.29 = (bf16[640,1408]{1,0:T(8,128)(2,1)}, bf16[640,1408]{1,0:T(8,128)(2,1)}, u32[]{:S(2)}, u32[]{:S(2)}) collective-permute-start(bf16[640,1408]{1,0:T(8,128)(2,1)} %slice.421), channel_id=1, source_target_pairs={{0,1},{1,0},{2,3},{3,2},{4,5},{5,4},{6,7},{7,6},{8,9},{9,8},{10,11... | collective-permute-start | bytes 5406728 | tf_op jit(solution)/shard_map/ppermute | solution.py:26
  309.5 24.4 %collective-permute-start.27 = (bf16[128,1280]{1,0:T(8,128)(2,1)}, bf16[128,1280]{1,0:T(8,128)(2,1)S(1)}, u32[]{:S(2)}, u32[]{:S(2)}) collective-permute-start(bf16[128,1280]{1,0:T(8,128)(2,1)} %get-tuple-element.89), channel_id=1, source_target_pairs={{0,16},{8,24},{16,0},{24,8},{1,17},{9,25},{17,1},{25,9},{2,18},{10... | collective-permute-start | bytes 983048 | tf_op jit(solution)/shard_map/ppermute | solution.py:26
  310.0 23.9 %collective-permute-start.28 = (bf16[128,1280]{1,0:T(8,128)(2,1)}, bf16[128,1280]{1,0:T(8,128)(2,1)}, u32[]{:S(2)}, u32[]{:S(2)}) collective-permute-start(bf16[128,1280]{1,0:T(8,128)(2,1)} %get-tuple-element.90), channel_id=1, source_target_pairs={{0,24},{8,16},{16,8},{24,0},{1,25},{9,17},{17,9},{25,1},{2,26},{10... | collective-permute-start | bytes 983048 | tf_op jit(solution)/shard_map/ppermute | solution.py:26
  338.8 10.0 %collective-permute-start.30 = (bf16[320,640]{1,0:T(8,128)(2,1)S(1)}, bf16[320,640]{1,0:T(8,128)(2,1)S(1)}, u32[]{:S(2)}, u32[]{:S(2)}) collective-permute-start(bf16[320,640]{1,0:T(8,128)(2,1)S(1)} %concatenate.120), channel_id=1, source_target_pairs={{0,2},{1,3},{2,0},{3,1},{4,6},{5,7},{6,4},{7,5},{8,10},{9,11},{10,... | collective-permute-start | bytes 1228808 | tf_op jit(solution)/shard_map/ppermute | solution.py:26
  340.6 13.8 %collective-permute-start.32 = (bf16[320,768]{1,0:T(8,128)(2,1)S(1)}, bf16[320,768]{1,0:T(8,128)(2,1)S(1)}, u32[]{:S(2)}, u32[]{:S(2)}) collective-permute-start(bf16[320,768]{1,0:T(8,128)(2,1)S(1)} %pad_maximum_fusion.1), channel_id=1, source_target_pairs={{0,4},{1,5},{2,6},{3,7},{4,0},{5,1},{6,2},{7,3},{8,12},{9,13},{10,... | collective-permute-start | bytes 1474568 | tf_op jit(solution)/shard_map/ppermute | solution.py:26
  348.9 7.6 %collective-permute-start.31 = (bf16[160,640]{1,0:T(8,128)(2,1)S(1)}, bf16[160,640]{1,0:T(8,128)(2,1)S(1)}, u32[]{:S(2)}, u32[]{:S(2)}) collective-permute-start(bf16[160,640]{1,0:T(8,128)(2,1)S(1)} %fusion.47), channel_id=1, source_target_pairs={{0,4},{1,5},{2,6},{3,7},{4,0},{5,1},{6,2},{7,3},{8,12},{9,13},{10,... | collective-permute-start | bytes 614408 | tf_op jit(solution)/shard_map/ppermute | solution.py:26
  354.5 6.3 %collective-permute-start.33 = (bf16[160,768]{1,0:T(8,128)(2,1)S(1)}, bf16[160,768]{1,0:T(8,128)(2,1)S(1)}, u32[]{:S(2)}, u32[]{:S(2)}) collective-permute-start(bf16[160,768]{1,0:T(8,128)(2,1)S(1)} %fusion.45), channel_id=1, source_target_pairs={{0,2},{1,3},{2,0},{3,1},{4,6},{5,7},{6,4},{7,5},{8,10},{9,11},{10,... | collective-permute-start | bytes 737288 | tf_op jit(solution)/shard_map/ppermute | solution.py:26
  361.0 11.9 %collective-permute-start.34 = (bf16[40,1408]{1,0:T(8,128)(2,1)S(1)}, bf16[40,1408]{1,0:T(8,128)(2,1)S(1)}, u32[]{:S(2)}, u32[]{:S(2)}) collective-permute-start(bf16[40,1408]{1,0:T(8,128)(2,1)S(1)} %get-tuple-element.93), channel_id=1, source_target_pairs={{0,8},{8,0},{16,24},{24,16},{1,9},{9,1},{17,25},{25,17},{2,10},{10... | collective-permute-start | bytes 337928 | tf_op jit(solution)/shard_map/ppermute | solution.py:26
  368.3 6.6 %collective-permute-start.36 = (bf16[40,1408]{1,0:T(8,128)(2,1)S(1)}, bf16[40,1408]{1,0:T(8,128)(2,1)S(1)}, u32[]{:S(2)}, u32[]{:S(2)}) collective-permute-start(bf16[40,1408]{1,0:T(8,128)(2,1)S(1)} %get-tuple-element.94), channel_id=1, source_target_pairs={{0,24},{8,16},{16,8},{24,0},{1,25},{9,17},{17,9},{25,1},{2,26},{10... | collective-permute-start | bytes 337928 | tf_op jit(solution)/shard_map/ppermute | solution.py:26
  370.7 6.6 %collective-permute-start.35 = (bf16[40,1408]{1,0:T(8,128)(2,1)S(1)}, bf16[40,1408]{1,0:T(8,128)(2,1)S(1)}, u32[]{:S(2)}, u32[]{:S(2)}) collective-permute-start(bf16[40,1408]{1,0:T(8,128)(2,1)S(1)} %get-tuple-element.95), channel_id=1, source_target_pairs={{0,16},{8,24},{16,0},{24,8},{1,17},{9,25},{17,1},{25,9},{2,18},{10... | collective-permute-start | bytes 337928 | tf_op jit(solution)/shard_map/ppermute | solution.py:26
  (12 other events, 69.3 us)

commit v2 on v1

--- a/solution.py
+++ b/solution.py
@@ -30,32 +30,6 @@
     return lax.all_to_all(value, "expert", split_axis=0, concat_axis=0, tiled=True)
 
 
-def line_steps(value, axis):
-    n = lax.axis_size(axis)
-    up, down = {}, {}
-    cur_u = cur_d = value
-    for s in range(1, n):
-        cur_u = lax.ppermute(cur_u, axis, [(i, i + 1) for i in range(s - 1, n - 1)])
-        cur_d = lax.ppermute(cur_d, axis, [(i, i - 1) for i in range(1, n - s + 1)])
-        up[s], down[s] = cur_u, cur_d
-    return up, down
-
-
-def line_block(up, down, index, n, j):
-    found = {}
-    for i in range(n):
-        found.setdefault((i ^ j) - i, []).append(i)
-    total = None
-    for gap, places in found.items():
-        piece = down[gap] if gap > 0 else up[-gap]
-        if total is None:
-            total = piece
-            continue
-        here = functools.reduce(jnp.logical_or, [index == i for i in places])
-        total = jnp.where(here, piece, total)
-    return total
-
-
 def chunk_of(size):
     for chunk in (256, 128):
         if size % chunk == 0:
@@ -63,10 +37,20 @@
     return size
 
 
+def flat(ref):
+    return ref[...].reshape(-1, ref.shape[-1])
+
+
+def row_block(a, size, step):
+    if a.ndim == 3:
+        return pl.BlockSpec((None, a.shape[1], size), lambda i, j: (i, 0, j * step))
+    return pl.BlockSpec((a.shape[0], None, a.shape[2], size), lambda i, j: (0, i, 0, j * step))
+
+
 def ffn_kernel(x_ref, c_ref, sel_ref, wr_ref, w1_ref, w2_ref, out_ref, back_ref, gh_ref, dp_ref, s_ref, gate, acc_o, acc_b, acc_s):
     step = pl.program_id(1)
-    x = x_ref[...].reshape(c_ref.shape[1:])
-    c = c_ref[0]
+    x = flat(x_ref)
+    c = flat(c_ref)
 
     @pl.when(step == 0)
     def _():
@@ -100,26 +84,24 @@
 
 
 def ffn(x, c, sel, w_router, w1, w2):
-    e, rows, width = c.shape
-    sources, seg = x.shape[0], x.shape[2]
-    hidden = w1.shape[2]
+    e, width, hidden = w1.shape
+    rows = x.size // (e * width)
     experts = w_router.shape[1]
     hc = chunk_of(hidden)
-    row_spec = pl.BlockSpec((1, rows, width), lambda i, j: (i, 0, 0))
-    src_spec = pl.BlockSpec((sources, None, seg, width), lambda i, j: (0, i, 0, 0))
+    row_spec = row_block(x, width, 0)
     hid_spec = pl.BlockSpec((1, rows, hc), lambda i, j: (i, 0, j))
     return pl.pallas_call(
         ffn_kernel,
         grid=(e, hidden // hc),
         in_specs=[
-            src_spec,
+            row_spec,
             row_spec,
             pl.BlockSpec((1, rows, experts), lambda i, j: (i, 0, 0)),
             pl.BlockSpec((width, experts), lambda i, j: (0, 0)),
             pl.BlockSpec((1, width, hc), lambda i, j: (i, 0, j)),
             pl.BlockSpec((1, hc, width), lambda i, j: (i, j, 0)),
         ],
-        out_specs=[src_spec, src_spec, hid_spec, hid_spec, pl.BlockSpec((1, rows, 1), lambda i, j: (i, 0, 0))],
+        out_specs=[row_spec, row_spec, hid_spec, hid_spec, pl.BlockSpec((1, rows, 1), lambda i, j: (i, 0, 0))],
         out_shape=[
             jax.ShapeDtypeStruct(x.shape, BF),
             jax.ShapeDtypeStruct(x.shape, BF),
@@ -145,28 +127,20 @@
 def wgrad_kernel(scale, pairs, *refs):
     total = None
     for i in range(pairs):
-        left, right = [r[...].reshape(-1, r.shape[-1]) for r in (refs[i], refs[pairs + i])]
-        term = dot32(left, right, ((0,), (0,)))
+        term = dot32(flat(refs[i]), flat(refs[pairs + i]), ((0,), (0,)))
         total = term if total is None else total + term
     refs[-1][0] = total * scale
 
 
-def wgrad(scale, lefts, rights):
+def wgrad(scale, e, lefts, rights):
     m = lefts[0].shape[-1]
-    e, _, n = [a for a in rights + lefts if a.ndim == 3][0].shape
     n = rights[0].shape[-1]
     mc = chunk_of(m)
     rows = sum([a.size // (e * m) for a in lefts])
-
-    def spec(a, size, step):
-        if a.ndim == 3:
-            return pl.BlockSpec((None, a.shape[1], size), lambda i, j: (i, 0, j * step))
-        return pl.BlockSpec((a.shape[0], None, a.shape[2], size), lambda i, j: (0, i, 0, j * step))
-
     return pl.pallas_call(
         functools.partial(wgrad_kernel, scale, len(lefts)),
         grid=(e, m // mc),
-        in_specs=[spec(a, mc, 1) for a in lefts] + [spec(b, n, 0) for b in rights],
+        in_specs=[row_block(a, mc, 1) for a in lefts] + [row_block(b, n, 0) for b in rights],
         out_specs=pl.BlockSpec((1, mc, n), lambda i, j: (i, j, 0)),
         out_shape=jax.ShapeDtypeStruct((e, m, n), F32),
         cost_estimate=pl.CostEstimate(
@@ -269,7 +243,11 @@
     lane_expert = lax.broadcasted_iota(jnp.int32, (1, 1, experts), 2)
     for g in range(len(groups)):
         other = others[:, g * exp_dev * seg : (g + 1) * exp_dev * seg]
-        other = other.reshape(n_ex, exp_dev, seg).transpose(1, 0, 2).reshape(exp_dev, rows, 1)
+        if g == 0:
+            other = other.reshape(n_ex, exp_dev, per, cap).transpose(1, 2, 0, 3)
+        else:
+            other = other.reshape(n_ex, exp_dev, seg).transpose(1, 0, 2)
+        other = other.reshape(exp_dev, rows, 1)
         sels.append(
             (lane_expert == own_expert).astype(F32)
             - (lane_expert == other.astype(jnp.int32)).astype(F32)
@@ -278,6 +256,21 @@
     def dispatch(blocks, hot):
         sent = dot32(hot, jnp.concatenate(blocks, axis=0)).astype(BF)
         return exchange(sent).reshape(n_ex, exp_dev, seg, width)
+
+    near, far = groups
+    line = exp_dev * rows
+    at = lax.broadcasted_iota(jnp.int32, (line, 1), 0)
+    e_at, blk_at, src_at, pos_at = at // rows, at % rows // (n_ex * cap), at % (n_ex * cap) // cap, at % cap
+    came_from = ((blk_at * n_ex + src_at) * exp_dev + e_at) * cap + pos_at
+    arrange = (came_from == lax.broadcasted_iota(jnp.int32, (line, line), 1)).astype(BF)
+
+    def gather_near(own):
+        every = [own] + [swap(own, "dp", j) for j in near[1:]]
+        return dot32(arrange, jnp.concatenate(every, axis=0)).astype(BF).reshape(exp_dev, rows, width)
+
+    cot_near = gather_near(own_cot)
+    cots = [swap(cotangent, "dp", j) for j in far]
+    slot_cot = [cot_near, dispatch(cots, merged[1])]
 
     w_dp = jnp.concatenate([w_out] + [swap(w_out, "dp", j) for j in range(1, n_dp)], axis=0)
     from_hi = swap(w_dp, "expert", hi)
@@ -301,20 +294,9 @@
     inv_std = lax.rsqrt(variance + LN_EPS)
     normed = centred * inv_std
     normed_bf = normed.astype(BF)
-    xs = [normed_bf] + [swap(normed_bf, "dp", j) for j in range(1, n_dp)]
-    slot_in = [dispatch([xs[j] for j in group], hot) for group, hot in zip(groups, merged)]
-
-    up, down = line_steps(own_cot, "dp")
-    cots = [own_cot] + [line_block(up, down, z, n_dp, j) for j in range(1, n_dp)]
-    line = exp_dev * rows
-    at = lax.broadcasted_iota(jnp.int32, (line, 1), 0)
-    e_at, src_at, blk_at, pos_at = at // rows, at % rows // seg, at % seg // cap, at % cap
-    came_from = ((blk_at * n_ex + src_at) * exp_dev + e_at) * cap + pos_at
-    arrange = (came_from == lax.broadcasted_iota(jnp.int32, (line, line), 1)).astype(BF)
-    slot_cot = [
-        dot32(arrange, jnp.concatenate([cots[j] for j in group], axis=0)).astype(BF).reshape(exp_dev, rows, width)
-        for group in groups
-    ]
+    xs = [swap(normed_bf, "dp", j) for j in far]
+    own_in = exchange(dot32(own_map, normed_bf).astype(BF))
+    slot_in = [gather_near(own_in), dispatch(xs, merged[1])]
 
     logits = dot32(w_router, normed_bf, ((0,), (1,)))
     late_ids = lax.optimization_barrier(own_ids)
@@ -326,35 +308,36 @@
     for x, c, sel in zip(slot_in, slot_cot, sels):
         results.append(ffn(x, c, sel, w_router, w_fc1, w_fc2))
 
-    def collect(value, hot):
-        got = exchange(value.reshape(-1, width))
-        return dot32(hot, got, ((0,), (0,)))
-
-    def reduce_dp(parts):
-        total = parts[0]
-        for j in range(1, n_dp):
-            total = total + swap(parts[j].astype(BF), "dp", j).astype(F32)
+    def collect(near_part, far_part):
+        pieces = dot32(arrange, near_part.reshape(line, width), ((0,), (0,))).astype(BF)
+        size = line // per
+        slots_own = pieces[:size].astype(F32)
+        for j in near[1:]:
+            slots_own = slots_own + swap(pieces[j * size : (j + 1) * size], "dp", j).astype(F32)
+        got = exchange(slots_own.astype(BF))
+        total = dot32(own_map, got, ((0,), (0,)))
+        got = exchange(far_part.reshape(-1, width))
+        parts = dot32(merged[1], got, ((0,), (0,))).astype(BF)
+        for i, j in enumerate(far):
+            total = total + swap(parts[i * tok : (i + 1) * tok], "dp", j).astype(F32)
         return total
 
-    def blocks_of(values):
-        return [v[i * tok : (i + 1) * tok] for v in values for i in range(per)]
-
-    back_sum = reduce_dp(blocks_of([collect(r[1], hot) for r, hot in zip(results, merged)]))
+    back_sum = collect(results[0][1], results[1][1])
     score = [
-        r[4].reshape(exp_dev, n_ex, seg).transpose(1, 0, 2).reshape(n_ex, exp_dev * seg)
-        for r in results
+        results[0][4].reshape(exp_dev, per, n_ex, cap).transpose(2, 0, 1, 3).reshape(n_ex, exp_dev * seg),
+        results[1][4].reshape(exp_dev, n_ex, seg).transpose(1, 0, 2).reshape(n_ex, exp_dev * seg),
     ]
     score = spread(jnp.concatenate(score, axis=1))
     part = exp_dev * seg
     score_parts = []
     for g, by_k in enumerate(maps):
-        line = score[:, g * part : (g + 1) * part].reshape(1, slots)
-        both = jnp.concatenate([dot32(line, by_k[k].astype(F32), precision=HI) for k in range(top_k)], axis=0)
+        packed = score[:, g * part : (g + 1) * part].reshape(1, slots)
+        both = jnp.concatenate([dot32(packed, by_k[k].astype(F32), precision=HI) for k in range(top_k)], axis=0)
         score_parts += [both[:, i * tok : (i + 1) * tok] for i in range(per)]
     score_sum = score_parts[0]
     for j in range(1, n_dp):
         score_sum = score_sum + swap(score_parts[j], "dp", j)
-    mixture = reduce_dp(blocks_of([collect(r[0], hot) for r, hot in zip(results, merged)]))
+    mixture = collect(results[0][0], results[1][0])
     d_chosen = score_sum - gates * jnp.sum(score_sum, axis=0, keepdims=True)
     d_logits = sum([picks[k] * d_chosen[k : k + 1] for k in range(top_k)])
     d_normed = back_sum + dot32(d_logits, w_router.astype(F32), ((0,), (1,)), precision=HI)
@@ -396,8 +379,8 @@
     grad_out = scale * grads[:, :width]
     grad_router = scale * grads[:, width : width + experts]
 
-    grad_fc1 = wgrad(scale, slot_in, [r[3] for r in results])
-    grad_fc2 = wgrad(scale, [r[2] for r in results], slot_cot)
+    grad_fc1 = wgrad(scale, exp_dev, slot_in, [r[3] for r in results])
+    grad_fc2 = wgrad(scale, exp_dev, [r[2] for r in results], slot_cot)
     return (layer_out, d_residual, d_context, grad_out, grad_router, grad_fc1, grad_fc2)
 
 

time: 381 us -> 388 us (1.018)
  matrix products: 41.1 us -> 52.6 us
  blocking collectives: 8.55 us -> 0 us
  starting transfers between devices: 91.4 us -> 99.7 us
  waiting for transfers between devices: 135 us -> 127 us
  local copies, waits for them, and re-layouts: 12.3 us -> 17.3 us
    ppermute x31 -> x34, waiting for transfers between devices: 81 us -> 111 us  [swap(): return lax.ppermute(value, axis, [(i, i ^ bit) for i in range(n)])]
    all_to_all x8 -> x10, waiting for transfers between devices: 37.1 us -> 15.8 us  [exchange(): lax.all_to_all(value, 'expert', split_axis=0, concat_axis=0, tiled=True)]
    ppermute x6 -> x0, waiting for transfers between devices: 17.3 us -> none  [the longest x3 17.1 us: line_steps(): cur_d = lax.ppermute(cur_d, axis, [(i, i - 1) for i in range(1, n - s + 1)])]
    ppermute x31 -> x34, starting transfers between devices: 44.6 us -> 58.9 us  [swap(): return lax.ppermute(value, axis, [(i, i ^ bit) for i in range(n)])]
    ppermute x6 -> x0, starting transfers between devices: 12.6 us -> none  [the longest x3 8.74 us: line_steps(): cur_u = lax.ppermute(cur_u, axis, [(i, i + 1) for i in range(s - 1, n - 1)])]
    dot_general x33 -> x36, matrix products: 41.1 us -> 52.6 us  [dot32(): lax.dot_general(a, b, (dims, ((), ())), preferred_element_type=F32, preci...]
    all_to_all x1 -> x0, blocking collectives: 8.55 us -> none  [exchange(): lax.all_to_all(value, 'expert', split_axis=0, concat_axis=0, tiled=True)]
    all_to_all x8 -> x10, starting transfers between devices: 34.2 us -> 40.8 us  [exchange(): lax.all_to_all(value, 'expert', split_axis=0, concat_axis=0, tiled=True)]
  transfers between devices with their start and end apart: 45 -> 44, of which waited for: 21 -> 21; matrix products, arithmetic and copies ran while one was open for 16% -> 19% of each run, Pallas kernels for 13% -> 13%
where the time goes in v2:
time: 388 us; the launch traced here: 386 us
  waiting for transfers between devices  127 us (33%)
  starting transfers between devices  99.7 us (26%)
  Pallas kernels  72.7 us (19%)
  matrix products  52.6 us (14%)
  local copies, waits for them, and re-layouts  17.3 us (4%)
  other arithmetic  15.1 us (4%)
    ppermute x34, waiting for transfers between devices, swap(): return lax.ppermute(value, axis, [(i, i ^ bit) for i in range(n)])  111 us
    ppermute x34, starting transfers between devices, swap(): return lax.ppermute(value, axis, [(i, i ^ bit) for i in range(n)])  58.9 us
    dot_general x36, matrix products, dot32(): lax.dot_general(a, b, (dims, ((), ())), preferred_element_type=F32, preci...  52.6 us
    pallas_call x2, Pallas kernels, ffn(): pl.pallas_call(ffn_kernel, grid=(e, hidden // hc), in_specs=[row_spec, ro...  43.8 us
    all_to_all x10, starting transfers between devices, exchange(): lax.all_to_all(value, 'expert', split_axis=0, concat_axis=0, tiled=True)  40.8 us
    pallas_call x2, Pallas kernels, wgrad(): pl.pallas_call(functools.partial(wgrad_kernel, scale, len(lefts)), grid=(...  28.9 us
    all_to_all x10, waiting for transfers between devices, exchange(): lax.all_to_all(value, 'expert', split_axis=0, concat_axis=0, tiled=True)  15.8 us
    unnamed x59, local copies, waits for them, and re-layouts  9 us
  transfers between devices with their start and end apart: 44, of which 21 were waited for; matrix products, arithmetic and copies ran while one was open for 19% of the time, Pallas kernels for 13%

profile of v2, /device:TPU:0, one launch (start us, length us, event | category | flops | bytes accessed | tf_op | source)
XLA Modules:
  0.0 385.7 jit_solution(16324947015070028138)
XLA Ops:
  0.6 5.1 %collective-permute-start.12 = (s32[2,128]{1,0:T(2,128)}, s32[2,128]{1,0:T(2,128)S(1)}, u32[]{:S(2)}, u32[]{:S(2)}) collective-permute-start(s32[2,128]{1,0:T(2,128)} %bitcast.179), channel_id=1, source_target_pairs={{0,24},{8,16},{16,8},{24,0},{1,25},{9,17},{17,9},{25,1},{2,26},{10... | collective-permute-start | bytes 3080 | tf_op jit(solution)/shard_map/ppermute | solution.py:26
  6.4 2.3 collective-permute-start.1
  15.5 5.9 %collective-permute-done.2 = bf16[40,1280]{1,0:T(8,128)(2,1)S(1)} collective-permute-done((bf16[40,1280]{1,0:T(8,128)(2,1)S(1)}, bf16[40,1280]{1,0:T(8,128)(2,1)S(1)}, u32[]{:S(2)}, u32[]{:S(2)}) %collective-permute-start.2) | collective-permute-done | bytes 102432 | tf_op jit(solution)/shard_map/ppermute | solution.py:26
  24.7 5.6 %collective-permute-done.4 = bf16[160,1280]{1,0:T(8,128)(2,1)S(1)} collective-permute-done((bf16[160,1280]{1,0:T(8,128)(2,1)S(1)}, bf16[160,1280]{1,0:T(8,128)(2,1)S(1)}, u32[]{:S(2)}, u32[]{:S(2)}) %collective-permute-start.4) | collective-permute-done | bytes 409632 | tf_op jit(solution)/shard_map/ppermute | solution.py:26
  34.0 5.3 %collective-permute-done.5 = bf16[80,1280]{1,0:T(8,128)(2,1)S(1)} collective-permute-done((bf16[80,1280]{1,0:T(8,128)(2,1)S(1)}, bf16[80,1280]{1,0:T(8,128)(2,1)S(1)}, u32[]{:S(2)}, u32[]{:S(2)}) %collective-permute-start.5) | collective-permute-done | bytes 204832 | tf_op jit(solution)/shard_map/ppermute | solution.py:26
  41.9 3.3 all-to-all-start.2
  50.1 4.2 %all-to-all-start.1 = ((bf16[8,40,1280]{2,1,0:T(8,128)(2,1)}), bf16[8,40,1280]{2,1,0:T(8,128)(2,1)}, u32[]{:S(2)}, u32[]{:S(2)}) async-start(bf16[8,40,1280]{2,1,0:T(8,128)(2,1)} %bitcast.11), calls=%async_computation.1 | async-start | bytes 1638400 | tf_op jit(solution)/shard_map/all_to_all | solution.py:30
  55.7 11.5 %all-to-all-done.1 = bf16[8,40,1280]{2,1,0:T(8,128)(2,1)} async-done(((bf16[8,40,1280]{2,1,0:T(8,128)(2,1)}), bf16[8,40,1280]{2,1,0:T(8,128)(2,1)}, u32[]{:S(2)}, u32[]{:S(2)}) %all-to-all-start.1) | async-done | bytes 819232 | tf_op jit(solution)/shard_map/all_to_all | solution.py:30
  67.2 4.2 %all-to-all-start = ((bf16[8,40,1280]{2,1,0:T(8,128)(2,1)}), bf16[8,40,1280]{2,1,0:T(8,128)(2,1)}, u32[]{:S(2)}, u32[]{:S(2)}) async-start(bf16[8,40,1280]{2,1,0:T(8,128)(2,1)} %bitcast.8), calls=%async_computation | async-start | bytes 1638400 | tf_op jit(solution)/shard_map/all_to_all | solution.py:30
  72.8 4.1 %collective-permute-start.9 = (bf16[320,1280]{1,0:T(8,128)(2,1)}, bf16[320,1280]{1,0:T(8,128)(2,1)}, u32[]{:S(2)}, u32[]{:S(2)}) collective-permute-start(bf16[320,1280]{1,0:T(8,128)(2,1)} %bitcast.12), channel_id=1, source_target_pairs={{0,8},{8,0},{16,24},{24,16},{1,9},{9,1},{17,25},{25,17},{2,10},{10... | collective-permute-start | bytes 2457608 | tf_op jit(solution)/shard_map/ppermute | solution.py:26
  76.9 7.2 %collective-permute-done.17 = bf16[128,1280]{1,0:T(8,128)(2,1)S(1)} collective-permute-done((bf16[128,1280]{1,0:T(8,128)(2,1)S(1)}, bf16[128,1280]{1,0:T(8,128)(2,1)S(1)}, u32[]{:S(2)}, u32[]{:S(2)}) %collective-permute-start.17) | collective-permute-done | bytes 327712 | tf_op jit(solution)/shard_map/ppermute | solution.py:26
  84.0 16.9 %collective-permute-done.16 = bf16[128,1280]{1,0:T(8,128)(2,1)} collective-permute-done((bf16[128,1280]{1,0:T(8,128)(2,1)S(1)}, bf16[128,1280]{1,0:T(8,128)(2,1)}, u32[]{:S(2)}, u32[]{:S(2)}) %collective-permute-start.16) | collective-permute-done | bytes 327712 | tf_op jit(solution)/shard_map/ppermute | solution.py:26
  101.0 2.8 convolution_convert_fusion
  103.7 4.3 %all-to-all-start.5 = ((bf16[8,80,1280]{2,1,0:T(8,128)(2,1)}), bf16[8,80,1280]{2,1,0:T(8,128)(2,1)}, u32[]{:S(2)}, u32[]{:S(2)}) async-start(bf16[8,80,1280]{2,1,0:T(8,128)(2,1)} %bitcast.169), calls=%async_computation.5 | async-start | bytes 3276800 | tf_op jit(solution)/shard_map/all_to_all | solution.py:30
  110.9 2.3 collective-permute-start.14
  113.2 4.1 %convolution_convert_fusion.4 = bf16[640,1280]{1,0:T(8,128)(2,1)} fusion(bf16[320,1280]{1,0:T(8,128)(2,1)} %collective-permute-done.9, bf16[320,1280]{1,0:T(8,128)(2,1)} %bitcast.12, s32[640]{0:T(1024)S(1)} %fusion.144), kind=kOutput, calls=%fused_computation.16 | convolution fusion | flops 1053081600 | bytes 3279360 | tf_op jit(solution)/shard_map/dot_general | solution.py:19
  117.5 18.7 %collective-permute-done.15 = bf16[128,1280]{1,0:T(8,128)(2,1)S(1)} collective-permute-done((bf16[128,1280]{1,0:T(8,128)(2,1)S(1)}, bf16[128,1280]{1,0:T(8,128)(2,1)S(1)}, u32[]{:S(2)}, u32[]{:S(2)}) %collective-permute-start.15) | collective-permute-done | bytes 327712 | tf_op jit(solution)/shard_map/ppermute | solution.py:26
  136.2 5.0 %collective-permute-done.14 = bf16[128,1280]{1,0:T(8,128)(2,1)S(1)} collective-permute-done((bf16[128,1280]{1,0:T(8,128)(2,1)S(1)}, bf16[128,1280]{1,0:T(8,128)(2,1)S(1)}, u32[]{:S(2)}, u32[]{:S(2)}) %collective-permute-start.14) | collective-permute-done | bytes 327712 | tf_op jit(solution)/shard_map/ppermute | solution.py:26
  143.0 4.5 %all-to-all-start.4 = ((bf16[8,80,1280]{2,1,0:T(8,128)(2,1)}), bf16[8,80,1280]{2,1,0:T(8,128)(2,1)}, u32[]{:S(2)}, u32[]{:S(2)}) async-start(bf16[8,80,1280]{2,1,0:T(8,128)(2,1)} %bitcast.170), calls=%async_computation.4 | async-start | bytes 3276800 | tf_op jit(solution)/shard_map/all_to_all | solution.py:30
  148.1 4.1 %convolution_convert_fusion.5 = bf16[640,1280]{1,0:T(8,128)(2,1)} fusion(bf16[320,1280]{1,0:T(8,128)(2,1)} %collective-permute-done.8, bf16[320,1280]{1,0:T(8,128)(2,1)} %bitcast.9, s32[640]{0:T(1024)S(1)} %fusion.144), kind=kOutput, calls=%fused_computation.17 | convolution fusion | flops 1053081600 | bytes 3279360 | tf_op jit(solution)/shard_map/dot_general | solution.py:19
  152.1 22.0 %shard_map.135 = (bf16[2,320,1280]{2,1,0:T(8,128)(2,1)}, bf16[2,320,1280]{2,1,0:T(8,128)(2,1)}, bf16[2,320,1280]{2,1,0:T(8,128)(2,1)}, bf16[2,320,1280]{2,1,0:T(8,128)(2,1)}, f32[2,320,1]{2,1,0:T(8,128)}) custom-call(bf16[2,320,1280]{2,1,0:T(8,128)(2,1)} %bitcast.165, bf16[2,320,1280]{2,1,0:T(8,128)(2,1)} %bitcast.163, ...), custom_call_target="tpu_custom_call" | custom-call | flops 8388608000 | bytes 26214400 | tf_op jit(solution)/shard_map/pallas_call | solution.py:93
  175.5 4.2 %convolution_convert_fusion.3 = bf16[640,1280]{1,0:T(8,128)(2,1)} fusion(bf16[640,1280]{1,0:T(8,128)(2,1)} %bitcast.208, s32[640]{0:T(1024)S(1)} %fusion.144), kind=kOutput, calls=%fused_computation.15 | convolution fusion | flops 1049804800 | bytes 3279360 | tf_op jit(solution)/shard_map/dot_general | solution.py:19
  179.7 21.9 %shard_map.136 = (bf16[8,2,40,1280]{3,2,1,0:T(8,128)(2,1)}, bf16[8,2,40,1280]{3,2,1,0:T(8,128)(2,1)}, bf16[2,320,1280]{2,1,0:T(8,128)(2,1)}, bf16[2,320,1280]{2,1,0:T(8,128)(2,1)}, f32[2,320,1]{2,1,0:T(8,128)}) custom-call(bf16[8,2,40,1280]{3,2,1,0:T(8,128)(2,1)} %bitcast.39.x_ref.refs_1_, bf16[8,2,40,1280]{3,2,1,0:T(8,128)(2,1)} %bitcast.41.c_ref.refs_3_, ...), custom_call_target="tpu_custom_call" | custom-call | flops 8388608000 | bytes 26214400 | tf_op jit(solution)/shard_map/pallas_call | solution.py:93
  203.6 3.9 %all-to-all-start.7 = ((f32[8,8,128]{2,1,0:T(8,128)}), f32[8,8,128]{2,1,0:T(8,128)S(1)}, u32[]{:S(2)}, u32[]{:S(2)}) async-start(f32[8,8,128]{2,1,0:T(8,128)} %copy.42), calls=%async_computation.7 | async-start | bytes 65536 | tf_op jit(solution)/shard_map/all_to_all | solution.py:30
  207.5 3.0 convolution_convert_fusion.2
  216.6 4.3 %all-to-all-start.6 = ((bf16[8,80,1280]{2,1,0:T(8,128)(2,1)}), bf16[8,80,1280]{2,1,0:T(8,128)(2,1)}, u32[]{:S(2)}, u32[]{:S(2)}) async-start(bf16[8,80,1280]{2,1,0:T(8,128)(2,1)} %bitcast.168), calls=%async_computation.6 | async-start | bytes 3276800 | tf_op jit(solution)/shard_map/all_to_all | solution.py:30
  225.7 3.2 collective-permute-start.21
  230.1 14.4 %shard_map.137 = f32[2,1280,1280]{2,1,0:T(8,128)} custom-call(bf16[2,320,1280]{2,1,0:T(8,128)(2,1)} %bitcast.166, bf16[8,2,40,1280]{3,2,1,0:T(8,128)(2,1)} %bitcast.39.x_ref.refs_1_, bf16[2,320,1280]{2,1,0:T(8,128)(2,1)} %get-tuple-element.35.refs_2_, bf16[2,320,1280]{2,1,0:T(8,128)(2,1)} %get-tuple-element.36.refs_3_), custom_call_target="tpu_custom_call" | custom-call | flops 4194304000 | bytes 19660800 | tf_op jit(solution)/shard_map/pallas_call | solution.py:140
  244.5 8.1 %collective-permute-done.21 = f32[2,128]{1,0:T(2,128)S(1)} collective-permute-done((f32[2,128]{1,0:T(2,128)}, f32[2,128]{1,0:T(2,128)S(1)}, u32[]{:S(2)}, u32[]{:S(2)}) %collective-permute-start.21) | collective-permute-done | bytes 1056 | tf_op jit(solution)/shard_map/ppermute | solution.py:26
  252.6 3.0 collective-permute-done.22
  259.3 3.8 all-to-all-start.3
  266.8 2.3 collective-permute-start.19
  269.3 4.5 %fusion.2 = f32[1280,16]{1,0:T(8,128)} fusion(f32[1280,16]{0,1:T(8,128)S(1)} %fusion.128, s32[1280]{0:T(1024)S(1)} %fusion.118), kind=kOutput, calls=%fused_computation.5 | convolution fusion | flops 317849600 | bytes 168960 | tf_op jit(solution)/shard_map/dot_general | solution.py:19
  276.0 4.3 %all-to-all-start.9 = ((bf16[8,80,1280]{2,1,0:T(8,128)(2,1)}), bf16[8,80,1280]{2,1,0:T(8,128)(2,1)}, u32[]{:S(2)}, u32[]{:S(2)}) async-start(bf16[8,80,1280]{2,1,0:T(8,128)(2,1)} %bitcast.167), calls=%async_computation.9 | async-start | bytes 3276800 | tf_op jit(solution)/shard_map/all_to_all | solution.py:30
  280.3 11.2 %collective-permute-done.18 = bf16[128,1280]{1,0:T(8,128)(2,1)} collective-permute-done((bf16[128,1280]{1,0:T(8,128)(2,1)}, bf16[128,1280]{1,0:T(8,128)(2,1)}, u32[]{:S(2)}, u32[]{:S(2)}) %collective-permute-start.18) | collective-permute-done | bytes 327712 | tf_op jit(solution)/shard_map/ppermute | solution.py:26
  296.1 2.9 copy-done.2
  303.3 3.9 %all-to-all-start.8 = ((bf16[8,40,1280]{2,1,0:T(8,128)(2,1)}), bf16[8,40,1280]{2,1,0:T(8,128)(2,1)S(1)}, u32[]{:S(2)}, u32[]{:S(2)}) async-start(bf16[8,40,1280]{2,1,0:T(8,128)(2,1)} %bitcast.159), calls=%async_computation.8 | async-start | bytes 1638400 | tf_op jit(solution)/shard_map/all_to_all | solution.py:30
  310.1 7.2 %collective-permute-start.24 = (bf16[128,1280]{1,0:T(8,128)(2,1)}, bf16[128,1280]{1,0:T(8,128)(2,1)}, u32[]{:S(2)}, u32[]{:S(2)}) collective-permute-start(bf16[128,1280]{1,0:T(8,128)(2,1)} %get-tuple-element.87), channel_id=1, source_target_pairs={{0,16},{8,24},{16,0},{24,8},{1,17},{9,25},{17,1},{25,9},{2,18},{10... | collective-permute-start | bytes 983048 | tf_op jit(solution)/shard_map/ppermute | solution.py:26
  317.4 2.6 collective-permute-start.25
  320.0 14.4 %shard_map.138 = f32[2,1280,1280]{2,1,0:T(8,128)} custom-call(bf16[2,320,1280]{2,1,0:T(8,128)(2,1)} %get-tuple-element.37.refs_0_, bf16[2,320,1280]{2,1,0:T(8,128)(2,1)} %get-tuple-element.38.refs_1_, bf16[2,320,1280]{2,1,0:T(8,128)(2,1)} %bitcast.164, bf16[8,2,40,1280]{3,2,1,0:T(8,128)(2,1)} %bitcast.41.c_ref.refs_3_), custom_call_target="tpu_custom_call" | custom-call | flops 4194304000 | bytes 19660800 | tf_op jit(solution)/shard_map/pallas_call | solution.py:140
  335.7 4.6 %collective-permute-done.24 = bf16[128,1280]{1,0:T(8,128)(2,1)} collective-permute-done((bf16[128,1280]{1,0:T(8,128)(2,1)}, bf16[128,1280]{1,0:T(8,128)(2,1)}, u32[]{:S(2)}, u32[]{:S(2)}) %collective-permute-start.24) | collective-permute-done | bytes 327712 | tf_op jit(solution)/shard_map/ppermute | solution.py:26
  342.5 3.0 fusion.226
  351.3 5.4 %collective-permute-done.27 = bf16[320,640]{1,0:T(8,128)(2,1)S(1)} collective-permute-done((bf16[320,640]{1,0:T(8,128)(2,1)S(1)}, bf16[320,640]{1,0:T(8,128)(2,1)S(1)}, u32[]{:S(2)}, u32[]{:S(2)}) %collective-permute-start.27) | collective-permute-done | bytes 409632 | tf_op jit(solution)/shard_map/ppermute | solution.py:26
  358.1 2.7 collective-permute-done.29
  364.0 3.2 collective-permute-done.30
  367.4 7.4 %collective-permute-start.31 = (bf16[40,1408]{1,0:T(8,128)(2,1)S(1)}, bf16[40,1408]{1,0:T(8,128)(2,1)S(1)}, u32[]{:S(2)}, u32[]{:S(2)}) collective-permute-start(bf16[40,1408]{1,0:T(8,128)(2,1)S(1)} %get-tuple-element.91), channel_id=1, source_target_pairs={{0,8},{8,0},{16,24},{24,16},{1,9},{9,1},{17,25},{25,17},{2,10},{10... | collective-permute-start | bytes 337928 | tf_op jit(solution)/shard_map/ppermute | solution.py:26
  374.9 2.6 collective-permute-start.33
  381.5 2.7 collective-permute-done.32
  (231 shorter events, 86.0 us)
Async XLA Ops:
  0.6 14.2 %collective-permute-start.12 = (s32[2,128]{1,0:T(2,128)}, s32[2,128]{1,0:T(2,128)S(1)}, u32[]{:S(2)}, u32[]{:S(2)}) collective-permute-start(s32[2,128]{1,0:T(2,128)} %bitcast.179), channel_id=1, source_target_pairs={{0,24},{8,16},{16,8},{24,0},{1,25},{9,17},{17,9},{25,1},{2,26},{10... | collective-permute-start | bytes 3080 | tf_op jit(solution)/shard_map/ppermute | solution.py:26
  5.8 9.2 %collective-permute-start.11 = (s32[2,128]{1,0:T(2,128)}, s32[2,128]{1,0:T(2,128)S(1)}, u32[]{:S(2)}, u32[]{:S(2)}) collective-permute-start(s32[2,128]{1,0:T(2,128)} %bitcast.180), channel_id=1, source_target_pairs={{0,16},{8,24},{16,0},{24,8},{1,17},{9,25},{17,1},{25,9},{2,18},{10... | collective-permute-start | bytes 3080 | tf_op jit(solution)/shard_map/ppermute | solution.py:26
  5.8 9.2 %collective-permute-start.10 = (s32[2,128]{1,0:T(2,128)}, s32[2,128]{1,0:T(2,128)S(1)}, u32[]{:S(2)}, u32[]{:S(2)}) collective-permute-start(s32[2,128]{1,0:T(2,128)} %bitcast.181), channel_id=1, source_target_pairs={{0,8},{8,0},{16,24},{24,16},{1,9},{9,1},{17,25},{25,17},{2,10},{10... | collective-permute-start | bytes 3080 | tf_op jit(solution)/shard_map/ppermute | solution.py:26
  6.4 9.0 %collective-permute-start.1 = (bf16[40,1280]{1,0:T(8,128)(2,1)}, bf16[40,1280]{1,0:T(8,128)(2,1)S(1)}, u32[]{:S(2)}, u32[]{:S(2)}) collective-permute-start(bf16[40,1280]{1,0:T(8,128)(2,1)} %param.10), channel_id=1, source_target_pairs={{0,16},{8,24},{16,0},{24,8},{1,17},{9,25},{17,1},{25,9},{2,18},{10... | collective-permute-start | bytes 307208 | tf_op jit(solution)/shard_map/ppermute | solution.py:26
  8.7 6.7 %collective-permute-start = (bf16[40,1280]{1,0:T(8,128)(2,1)}, bf16[40,1280]{1,0:T(8,128)(2,1)S(1)}, u32[]{:S(2)}, u32[]{:S(2)}) collective-permute-start(bf16[40,1280]{1,0:T(8,128)(2,1)} %param.10), channel_id=1, source_target_pairs={{0,8},{8,0},{16,24},{24,16},{1,9},{9,1},{17,25},{25,17},{2,10},{10... | collective-permute-start | bytes 307208 | tf_op jit(solution)/shard_map/ppermute | solution.py:26
  13.6 33.6 %copy-start.4 = (bf16[1280,128]{1,0:T(8,128)(2,1)}, bf16[1280,128]{1,0:T(8,128)(2,1)S(1)}, u32[]{:S(2)}) copy-start(bf16[1280,128]{1,0:T(8,128)(2,1)S(1)} %fusion.10) | copy-start | bytes 983044
  14.9 6.5 %collective-permute-start.2 = (bf16[40,1280]{1,0:T(8,128)(2,1)S(1)}, bf16[40,1280]{1,0:T(8,128)(2,1)S(1)}, u32[]{:S(2)}, u32[]{:S(2)}) collective-permute-start(bf16[40,1280]{1,0:T(8,128)(2,1)S(1)} %copy-done.15), channel_id=1, source_target_pairs={{0,24},{8,16},{16,8},{24,0},{1,25},{9,17},{17,9},{25,1},{2,26},{10... | collective-permute-start | bytes 307208 | tf_op jit(solution)/shard_map/ppermute | solution.py:26
  21.4 8.8 %collective-permute-start.4 = (bf16[160,1280]{1,0:T(8,128)(2,1)S(1)}, bf16[160,1280]{1,0:T(8,128)(2,1)S(1)}, u32[]{:S(2)}, u32[]{:S(2)}) collective-permute-start(bf16[160,1280]{1,0:T(8,128)(2,1)S(1)} %get-tuple-element.94), channel_id=1, source_target_pairs={{0,2},{1,3},{2,0},{3,1},{4,6},{5,7},{6,4},{7,5},{8,10},{9,11},{10,... | collective-permute-start | bytes 1228808 | tf_op jit(solution)/shard_map/ppermute | solution.py:26
  23.0 10.5 %collective-permute-start.3 = (bf16[160,1280]{1,0:T(8,128)(2,1)S(1)}, bf16[160,1280]{1,0:T(8,128)(2,1)S(1)}, u32[]{:S(2)}, u32[]{:S(2)}) collective-permute-start(bf16[160,1280]{1,0:T(8,128)(2,1)S(1)} %get-tuple-element.94), channel_id=1, source_target_pairs={{0,4},{1,5},{2,6},{3,7},{4,0},{5,1},{6,2},{7,3},{8,12},{9,13},{10,... | collective-permute-start | bytes 1228808 | tf_op jit(solution)/shard_map/ppermute | solution.py:26
  30.3 9.1 %collective-permute-start.6 = (bf16[80,1280]{1,0:T(8,128)(2,1)S(1)}, bf16[80,1280]{1,0:T(8,128)(2,1)S(1)}, u32[]{:S(2)}, u32[]{:S(2)}) collective-permute-start(bf16[80,1280]{1,0:T(8,128)(2,1)S(1)} %slice.264), channel_id=1, source_target_pairs={{0,4},{1,5},{2,6},{3,7},{4,0},{5,1},{6,2},{7,3},{8,12},{9,13},{10,... | collective-permute-start | bytes 614408 | tf_op jit(solution)/shard_map/ppermute | solution.py:26
  33.5 5.8 %collective-permute-start.5 = (bf16[80,1280]{1,0:T(8,128)(2,1)S(1)}, bf16[80,1280]{1,0:T(8,128)(2,1)S(1)}, u32[]{:S(2)}, u32[]{:S(2)}) collective-permute-start(bf16[80,1280]{1,0:T(8,128)(2,1)S(1)} %slice.263), channel_id=1, source_target_pairs={{0,2},{1,3},{2,0},{3,1},{4,6},{5,7},{6,4},{7,5},{8,10},{9,11},{10,... | collective-permute-start | bytes 614408 | tf_op jit(solution)/shard_map/ppermute | solution.py:26
  39.4 5.9 %collective-permute-start.7 = (bf16[640,1280]{1,0:T(8,128)(2,1)S(1)}, bf16[640,1280]{1,0:T(8,128)(2,1)}, u32[]{:S(2)}, u32[]{:S(2)}) collective-permute-start(bf16[640,1280]{1,0:T(8,128)(2,1)S(1)} %constant_dynamic-update-slice_fusion.4), channel_id=1, source_target_pairs={{0,1},{1,0},{2,3},{3,2},{4,5},{5,4},{6,7},{7,6},{8,9},{9,8},{10,11... | collective-permute-start | bytes 4915208 | tf_op jit(solution)/shard_map/ppermute | solution.py:26
  39.7 101.5 %copy-start.18 = (s32[1,256]{1,0:T(1,128)}, s32[1,256]{1,0:T(1,128)S(1)}, u32[]{:S(2)}) copy-start(s32[1,256]{1,0:T(1,128)S(1)} %pad_add_fusion.3) | copy-start | bytes 3076
  39.7 101.4 %copy-start.20 = (s32[1,256]{1,0:T(1,128)}, s32[1,256]{1,0:T(1,128)S(1)}, u32[]{:S(2)}) copy-start(s32[1,256]{1,0:T(1,128)S(1)} %pad_add_fusion.2) | copy-start | bytes 3076
  41.9 8.1 %all-to-all-start.2 = ((f32[8,8,128]{2,1,0:T(8,128)}), f32[8,8,128]{2,1,0:T(8,128)S(1)}, u32[]{:S(2)}, u32[]{:S(2)}) async-start(f32[8,8,128]{2,1,0:T(8,128)} %bitcast.156), calls=%async_computation.2 | async-start | bytes 65536 | tf_op jit(solution)/shard_map/all_to_all | solution.py:30
  50.1 17.1 %all-to-all-start.1 = ((bf16[8,40,1280]{2,1,0:T(8,128)(2,1)}), bf16[8,40,1280]{2,1,0:T(8,128)(2,1)}, u32[]{:S(2)}, u32[]{:S(2)}) async-start(bf16[8,40,1280]{2,1,0:T(8,128)(2,1)} %bitcast.11), calls=%async_computation.1 | async-start | bytes 1638400 | tf_op jit(solution)/shard_map/all_to_all | solution.py:30
  67.2 36.5 %all-to-all-start = ((bf16[8,40,1280]{2,1,0:T(8,128)(2,1)}), bf16[8,40,1280]{2,1,0:T(8,128)(2,1)}, u32[]{:S(2)}, u32[]{:S(2)}) async-start(bf16[8,40,1280]{2,1,0:T(8,128)(2,1)} %bitcast.8), calls=%async_computation | async-start | bytes 1638400 | tf_op jit(solution)/shard_map/all_to_all | solution.py:30
  71.5 12.6 %collective-permute-start.17 = (bf16[128,1280]{1,0:T(8,128)(2,1)S(1)}, bf16[128,1280]{1,0:T(8,128)(2,1)S(1)}, u32[]{:S(2)}, u32[]{:S(2)}) collective-permute-start(bf16[128,1280]{1,0:T(8,128)(2,1)S(1)} %copy-done.9), channel_id=1, source_target_pairs={{0,24},{8,16},{16,8},{24,0},{1,25},{9,17},{17,9},{25,1},{2,26},{10... | collective-permute-start | bytes 983048 | tf_op jit(solution)/shard_map/ppermute | solution.py:26
  71.7 29.3 %collective-permute-start.16 = (bf16[128,1280]{1,0:T(8,128)(2,1)S(1)}, bf16[128,1280]{1,0:T(8,128)(2,1)}, u32[]{:S(2)}, u32[]{:S(2)}) collective-permute-start(bf16[128,1280]{1,0:T(8,128)(2,1)S(1)} %copy-done.9), channel_id=1, source_target_pairs={{0,16},{8,24},{16,0},{24,8},{1,17},{9,25},{17,1},{25,9},{2,18},{10... | collective-permute-start | bytes 983048 | tf_op jit(solution)/shard_map/ppermute | solution.py:26
  72.8 40.4 %collective-permute-start.9 = (bf16[320,1280]{1,0:T(8,128)(2,1)}, bf16[320,1280]{1,0:T(8,128)(2,1)}, u32[]{:S(2)}, u32[]{:S(2)}) collective-permute-start(bf16[320,1280]{1,0:T(8,128)(2,1)} %bitcast.12), channel_id=1, source_target_pairs={{0,8},{8,0},{16,24},{24,16},{1,9},{9,1},{17,25},{25,17},{2,10},{10... | collective-permute-start | bytes 2457608 | tf_op jit(solution)/shard_map/ppermute | solution.py:26
  103.7 39.3 %all-to-all-start.5 = ((bf16[8,80,1280]{2,1,0:T(8,128)(2,1)}), bf16[8,80,1280]{2,1,0:T(8,128)(2,1)}, u32[]{:S(2)}, u32[]{:S(2)}) async-start(bf16[8,80,1280]{2,1,0:T(8,128)(2,1)} %bitcast.169), calls=%async_computation.5 | async-start | bytes 3276800 | tf_op jit(solution)/shard_map/all_to_all | solution.py:30
  108.5 39.5 %collective-permute-start.8 = (bf16[320,1280]{1,0:T(8,128)(2,1)}, bf16[320,1280]{1,0:T(8,128)(2,1)}, u32[]{:S(2)}, u32[]{:S(2)}) collective-permute-start(bf16[320,1280]{1,0:T(8,128)(2,1)} %bitcast.9), channel_id=1, source_target_pairs={{0,8},{8,0},{16,24},{24,16},{1,9},{9,1},{17,25},{25,17},{2,10},{10... | collective-permute-start | bytes 2457608 | tf_op jit(solution)/shard_map/ppermute | solution.py:26
  109.7 26.5 %collective-permute-start.15 = (bf16[128,1280]{1,0:T(8,128)(2,1)S(1)}, bf16[128,1280]{1,0:T(8,128)(2,1)S(1)}, u32[]{:S(2)}, u32[]{:S(2)}) collective-permute-start(bf16[128,1280]{1,0:T(8,128)(2,1)S(1)} %fusion.37), channel_id=1, source_target_pairs={{0,24},{8,16},{16,8},{24,0},{1,25},{9,17},{17,9},{25,1},{2,26},{10... | collective-permute-start | bytes 983048 | tf_op jit(solution)/shard_map/ppermute | solution.py:26
  110.9 30.3 %collective-permute-start.14 = (bf16[128,1280]{1,0:T(8,128)(2,1)S(1)}, bf16[128,1280]{1,0:T(8,128)(2,1)S(1)}, u32[]{:S(2)}, u32[]{:S(2)}) collective-permute-start(bf16[128,1280]{1,0:T(8,128)(2,1)S(1)} %fusion.37), channel_id=1, source_target_pairs={{0,16},{8,24},{16,0},{24,8},{1,17},{9,25},{17,1},{25,9},{2,18},{10... | collective-permute-start | bytes 983048 | tf_op jit(solution)/shard_map/ppermute | solution.py:26
  143.0 36.7 %all-to-all-start.4 = ((bf16[8,80,1280]{2,1,0:T(8,128)(2,1)}), bf16[8,80,1280]{2,1,0:T(8,128)(2,1)}, u32[]{:S(2)}, u32[]{:S(2)}) async-start(bf16[8,80,1280]{2,1,0:T(8,128)(2,1)} %bitcast.170), calls=%async_computation.4 | async-start | bytes 3276800 | tf_op jit(solution)/shard_map/all_to_all | solution.py:30
  203.6 13.0 %all-to-all-start.7 = ((f32[8,8,128]{2,1,0:T(8,128)}), f32[8,8,128]{2,1,0:T(8,128)S(1)}, u32[]{:S(2)}, u32[]{:S(2)}) async-start(f32[8,8,128]{2,1,0:T(8,128)} %copy.42), calls=%async_computation.7 | async-start | bytes 65536 | tf_op jit(solution)/shard_map/all_to_all | solution.py:30
  214.3 42.7 %collective-permute-start.13 = (bf16[320,1280]{1,0:T(8,128)(2,1)}, bf16[320,1280]{1,0:T(8,128)(2,1)S(1)}, u32[]{:S(2)}, u32[]{:S(2)}) collective-permute-start(bf16[320,1280]{1,0:T(8,128)(2,1)} %slice.268), channel_id=1, source_target_pairs={{0,8},{8,0},{16,24},{24,16},{1,9},{9,1},{17,25},{25,17},{2,10},{10... | collective-permute-start | bytes 2457608 | tf_op jit(solution)/shard_map/ppermute | solution.py:26
  216.6 83.8 %collective-permute-start.23 = (bf16[320,1280]{1,0:T(8,128)(2,1)}, bf16[320,1280]{1,0:T(8,128)(2,1)}, u32[]{:S(2)}, u32[]{:S(2)}) collective-permute-start(bf16[320,1280]{1,0:T(8,128)(2,1)} %slice.279), channel_id=1, source_target_pairs={{0,8},{8,0},{16,24},{24,16},{1,9},{9,1},{17,25},{25,17},{2,10},{10... | collective-permute-start | bytes 2457608 | tf_op jit(solution)/shard_map/ppermute | solution.py:26
  216.6 42.7 %all-to-all-start.6 = ((bf16[8,80,1280]{2,1,0:T(8,128)(2,1)}), bf16[8,80,1280]{2,1,0:T(8,128)(2,1)}, u32[]{:S(2)}, u32[]{:S(2)}) async-start(bf16[8,80,1280]{2,1,0:T(8,128)(2,1)} %bitcast.168), calls=%async_computation.6 | async-start | bytes 3276800 | tf_op jit(solution)/shard_map/all_to_all | solution.py:30
  225.7 27.0 %collective-permute-start.21 = (f32[2,128]{1,0:T(2,128)}, f32[2,128]{1,0:T(2,128)S(1)}, u32[]{:S(2)}, u32[]{:S(2)}) collective-permute-start(f32[2,128]{1,0:T(2,128)} %get-tuple-element.106), channel_id=1, source_target_pairs={{0,16},{8,24},{16,0},{24,8},{1,17},{9,25},{17,1},{25,9},{2,18},{10... | collective-permute-start | bytes 3080 | tf_op jit(solution)/shard_map/ppermute | solution.py:26
  228.9 26.8 %collective-permute-start.22 = (f32[2,128]{1,0:T(2,128)S(1)}, f32[2,128]{1,0:T(2,128)S(1)}, u32[]{:S(2)}, u32[]{:S(2)}) collective-permute-start(f32[2,128]{1,0:T(2,128)S(1)} %get-tuple-element.107), channel_id=1, source_target_pairs={{0,24},{8,16},{16,8},{24,0},{1,25},{9,17},{17,9},{25,1},{2,26},{10... | collective-permute-start | bytes 3080 | tf_op jit(solution)/shard_map/ppermute | solution.py:26
  230.1 25.6 %collective-permute-start.20 = (f32[2,128]{1,0:T(2,128)S(1)}, f32[2,128]{1,0:T(2,128)S(1)}, u32[]{:S(2)}, u32[]{:S(2)}) collective-permute-start(f32[2,128]{1,0:T(2,128)S(1)} %pad_maximum_fusion.3), channel_id=1, source_target_pairs={{0,8},{8,0},{16,24},{24,16},{1,9},{9,1},{17,25},{25,17},{2,10},{10... | collective-permute-start | bytes 3080 | tf_op jit(solution)/shard_map/ppermute | solution.py:26
  259.3 16.7 %all-to-all-start.3 = ((bf16[8,40,1280]{2,1,0:T(8,128)(2,1)}), bf16[8,40,1280]{2,1,0:T(8,128)(2,1)S(1)}, u32[]{:S(2)}, u32[]{:S(2)}) async-start(bf16[8,40,1280]{2,1,0:T(8,128)(2,1)} %bitcast.160), calls=%async_computation.3 | async-start | bytes 1638400 | tf_op jit(solution)/shard_map/all_to_all | solution.py:30
  266.1 25.4 %collective-permute-start.18 = (bf16[128,1280]{1,0:T(8,128)(2,1)}, bf16[128,1280]{1,0:T(8,128)(2,1)}, u32[]{:S(2)}, u32[]{:S(2)}) collective-permute-start(bf16[128,1280]{1,0:T(8,128)(2,1)} %get-tuple-element.89), channel_id=1, source_target_pairs={{0,16},{8,24},{16,0},{24,8},{1,17},{9,25},{17,1},{25,9},{2,18},{10... | collective-permute-start | bytes 983048 | tf_op jit(solution)/shard_map/ppermute | solution.py:26
  266.8 24.8 %collective-permute-start.19 = (bf16[128,1280]{1,0:T(8,128)(2,1)}, bf16[128,1280]{1,0:T(8,128)(2,1)}, u32[]{:S(2)}, u32[]{:S(2)}) collective-permute-start(bf16[128,1280]{1,0:T(8,128)(2,1)} %get-tuple-element.90), channel_id=1, source_target_pairs={{0,24},{8,16},{16,8},{24,0},{1,25},{9,17},{17,9},{25,1},{2,26},{10... | collective-permute-start | bytes 983048 | tf_op jit(solution)/shard_map/ppermute | solution.py:26
  276.0 27.3 %all-to-all-start.9 = ((bf16[8,80,1280]{2,1,0:T(8,128)(2,1)}), bf16[8,80,1280]{2,1,0:T(8,128)(2,1)}, u32[]{:S(2)}, u32[]{:S(2)}) async-start(bf16[8,80,1280]{2,1,0:T(8,128)(2,1)} %bitcast.167), calls=%async_computation.9 | async-start | bytes 3276800 | tf_op jit(solution)/shard_map/all_to_all | solution.py:30
  294.4 54.8 %copy-start.3 = (bf16[128,1280]{1,0:T(8,128)(2,1)}, bf16[128,1280]{1,0:T(8,128)(2,1)S(1)}, u32[]{:S(2)}) copy-start(bf16[128,1280]{1,0:T(8,128)(2,1)S(1)} %add_convert_fusion.3) | copy-start | bytes 983044
  300.3 42.2 %collective-permute-start.26 = (bf16[640,1408]{1,0:T(8,128)(2,1)}, bf16[640,1408]{1,0:T(8,128)(2,1)}, u32[]{:S(2)}, u32[]{:S(2)}) collective-permute-start(bf16[640,1408]{1,0:T(8,128)(2,1)} %slice.399), channel_id=1, source_target_pairs={{0,1},{1,0},{2,3},{3,2},{4,5},{5,4},{6,7},{7,6},{8,9},{9,8},{10,11... | collective-permute-start | bytes 5406728 | tf_op jit(solution)/shard_map/ppermute | solution.py:26
  303.3 32.5 %all-to-all-start.8 = ((bf16[8,40,1280]{2,1,0:T(8,128)(2,1)}), bf16[8,40,1280]{2,1,0:T(8,128)(2,1)S(1)}, u32[]{:S(2)}, u32[]{:S(2)}) async-start(bf16[8,40,1280]{2,1,0:T(8,128)(2,1)} %bitcast.159), calls=%async_computation.8 | async-start | bytes 1638400 | tf_op jit(solution)/shard_map/all_to_all | solution.py:30
  310.1 30.2 %collective-permute-start.24 = (bf16[128,1280]{1,0:T(8,128)(2,1)}, bf16[128,1280]{1,0:T(8,128)(2,1)}, u32[]{:S(2)}, u32[]{:S(2)}) collective-permute-start(bf16[128,1280]{1,0:T(8,128)(2,1)} %get-tuple-element.87), channel_id=1, source_target_pairs={{0,16},{8,24},{16,0},{24,8},{1,17},{9,25},{17,1},{25,9},{2,18},{10... | collective-permute-start | bytes 983048 | tf_op jit(solution)/shard_map/ppermute | solution.py:26
  317.4 22.9 %collective-permute-start.25 = (bf16[128,1280]{1,0:T(8,128)(2,1)}, bf16[128,1280]{1,0:T(8,128)(2,1)}, u32[]{:S(2)}, u32[]{:S(2)}) collective-permute-start(bf16[128,1280]{1,0:T(8,128)(2,1)} %get-tuple-element.88), channel_id=1, source_target_pairs={{0,24},{8,16},{16,8},{24,0},{1,25},{9,17},{17,9},{25,1},{2,26},{10... | collective-permute-start | bytes 983048 | tf_op jit(solution)/shard_map/ppermute | solution.py:26
  345.5 11.1 %collective-permute-start.27 = (bf16[320,640]{1,0:T(8,128)(2,1)S(1)}, bf16[320,640]{1,0:T(8,128)(2,1)S(1)}, u32[]{:S(2)}, u32[]{:S(2)}) collective-permute-start(bf16[320,640]{1,0:T(8,128)(2,1)S(1)} %concatenate.126), channel_id=1, source_target_pairs={{0,2},{1,3},{2,0},{3,1},{4,6},{5,7},{6,4},{7,5},{8,10},{9,11},{10,... | collective-permute-start | bytes 1228808 | tf_op jit(solution)/shard_map/ppermute | solution.py:26
  347.7 13.1 %collective-permute-start.29 = (bf16[320,768]{1,0:T(8,128)(2,1)S(1)}, bf16[320,768]{1,0:T(8,128)(2,1)S(1)}, u32[]{:S(2)}, u32[]{:S(2)}) collective-permute-start(bf16[320,768]{1,0:T(8,128)(2,1)S(1)} %pad_maximum_fusion.1), channel_id=1, source_target_pairs={{0,4},{1,5},{2,6},{3,7},{4,0},{5,1},{6,2},{7,3},{8,12},{9,13},{10,... | collective-permute-start | bytes 1474568 | tf_op jit(solution)/shard_map/ppermute | solution.py:26
  356.8 7.2 %collective-permute-start.28 = (bf16[160,640]{1,0:T(8,128)(2,1)S(1)}, bf16[160,640]{1,0:T(8,128)(2,1)S(1)}, u32[]{:S(2)}, u32[]{:S(2)}) collective-permute-start(bf16[160,640]{1,0:T(8,128)(2,1)S(1)} %fusion.40), channel_id=1, source_target_pairs={{0,4},{1,5},{2,6},{3,7},{4,0},{5,1},{6,2},{7,3},{8,12},{9,13},{10,... | collective-permute-start | bytes 614408 | tf_op jit(solution)/shard_map/ppermute | solution.py:26
  361.0 6.3 %collective-permute-start.30 = (bf16[160,768]{1,0:T(8,128)(2,1)S(1)}, bf16[160,768]{1,0:T(8,128)(2,1)S(1)}, u32[]{:S(2)}, u32[]{:S(2)}) collective-permute-start(bf16[160,768]{1,0:T(8,128)(2,1)S(1)} %fusion.38), channel_id=1, source_target_pairs={{0,2},{1,3},{2,0},{3,1},{4,6},{5,7},{6,4},{7,5},{8,10},{9,11},{10,... | collective-permute-start | bytes 737288 | tf_op jit(solution)/shard_map/ppermute | solution.py:26
  367.4 12.3 %collective-permute-start.31 = (bf16[40,1408]{1,0:T(8,128)(2,1)S(1)}, bf16[40,1408]{1,0:T(8,128)(2,1)S(1)}, u32[]{:S(2)}, u32[]{:S(2)}) collective-permute-start(bf16[40,1408]{1,0:T(8,128)(2,1)S(1)} %get-tuple-element.91), channel_id=1, source_target_pairs={{0,8},{8,0},{16,24},{24,16},{1,9},{9,1},{17,25},{25,17},{2,10},{10... | collective-permute-start | bytes 337928 | tf_op jit(solution)/shard_map/ppermute | solution.py:26
  374.9 6.7 %collective-permute-start.33 = (bf16[40,1408]{1,0:T(8,128)(2,1)S(1)}, bf16[40,1408]{1,0:T(8,128)(2,1)S(1)}, u32[]{:S(2)}, u32[]{:S(2)}) collective-permute-start(bf16[40,1408]{1,0:T(8,128)(2,1)S(1)} %get-tuple-element.92), channel_id=1, source_target_pairs={{0,24},{8,16},{16,8},{24,0},{1,25},{9,17},{17,9},{25,1},{2,26},{10... | collective-permute-start | bytes 337928 | tf_op jit(solution)/shard_map/ppermute | solution.py:26
  377.5 6.8 %collective-permute-start.32 = (bf16[40,1408]{1,0:T(8,128)(2,1)S(1)}, bf16[40,1408]{1,0:T(8,128)(2,1)S(1)}, u32[]{:S(2)}, u32[]{:S(2)}) collective-permute-start(bf16[40,1408]{1,0:T(8,128)(2,1)S(1)} %get-tuple-element.93), channel_id=1, source_target_pairs={{0,16},{8,24},{16,0},{24,8},{1,17},{9,25},{17,1},{25,9},{2,18},{10... | collective-permute-start | bytes 337928 | tf_op jit(solution)/shard_map/ppermute | solution.py:26
  (20 other events, 116.2 us)

commit v3 on v2

--- a/solution.py
+++ b/solution.py
@@ -6,8 +6,6 @@
 from jax.experimental import pallas as pl
 from jax.experimental.pallas import tpu as pltpu
 from jax.sharding import PartitionSpec as P
-
-from jax.experimental.layout import Layout, with_layout_constraint
 
 LN_EPS = 1e-06
 BF = jnp.bfloat16
@@ -298,6 +296,7 @@
     own_in = exchange(dot32(own_map, normed_bf).astype(BF))
     slot_in = [gather_near(own_in), dispatch(xs, merged[1])]
 
+    normed_rel = dot32(normed_bf, reorder).astype(BF)
     logits = dot32(w_router, normed_bf, ((0,), (1,)))
     late_ids = lax.optimization_barrier(own_ids)
     picks = [(e_iota == late_ids[k : k + 1]).astype(F32) for k in range(top_k)]
@@ -352,22 +351,37 @@
     d_rel = jnp.concatenate([dot32(d_residual, piece, ((1,), (1,))).astype(BF) for piece in w_rel], axis=1)
     d_context = dot32(d_rel, reorder, ((1,), (1,))).astype(BF)
 
-    router_term = dot32(normed_bf.astype(F32), d_logits, ((0,), (1,)), precision=HI)
-    router_term = dot32(reorder.astype(F32), router_term, ((0,), (0,)), precision=HI)
-    pad = -experts % 128
-    part_out = jnp.concatenate(
-        [dot32(ctx_rel, d_residual, ((0,), (0,))), jnp.pad(router_term, ((0, 0), (0, pad)))], axis=1
-    )
-    part_out = with_layout_constraint(part_out, Layout(major_to_minor=(0, 1)))
-    bit = 1
+    rest, thirds = d_logits, []
+    for _ in range(3):
+        thirds.append(rest.astype(BF))
+        rest = rest - thirds[-1].astype(F32)
+    thirds = jnp.concatenate(thirds, axis=0)
+    thirds = jnp.pad(thirds, ((0, -thirds.shape[0] % 128), (0, 0)))
+
+    def sums_of(cols):
+        return [
+            dot32(ctx_rel[:, cols], d_residual, ((0,), (0,))),
+            dot32(normed_rel[:, cols], thirds, ((0,), (1,))),
+        ]
+
+    half = width // 2
+    sent = jnp.concatenate([v.astype(BF) for v in sums_of(slice(half, width))], axis=1)
+    got = swap(sent, "expert", 1).astype(F32)
+    part_out, part_router = sums_of(slice(0, half))
+    part_out, part_router = part_out + got[:, :width], part_router + got[:, width:]
+    bit = 2
     while bit < lo:
-        half = part_out.shape[0] // 2
-        part_out = part_out[:half] + swap(part_out[half:].astype(BF), "expert", bit).astype(F32)
+        half = half // 2
+        sent = jnp.concatenate([part_out[half:], part_router[half:]], axis=1).astype(BF)
+        got = swap(sent, "expert", bit).astype(F32)
+        part_out, part_router = part_out[:half] + got[:, :width], part_router[:half] + got[:, width:]
         bit *= 2
     mid = width // 2
-    quarters = [part_out[i * rows_q : (i + 1) * rows_q] for i in range(4)]
-    left = [q[:, :mid] for q in quarters]
-    right = [q[:, mid:] for q in quarters]
+    left = [part_out[i * rows_q : (i + 1) * rows_q, :mid] for i in range(4)]
+    right = [
+        jnp.concatenate([part_out[i * rows_q : (i + 1) * rows_q, mid:], part_router[i * rows_q : (i + 1) * rows_q]], axis=1)
+        for i in range(4)
+    ]
     got_l = swap(jnp.concatenate([left[2], left[3]], axis=0).astype(BF), "expert", lo).astype(F32)
     got_r = swap(jnp.concatenate([right[1], right[3]], axis=0).astype(BF), "expert", hi).astype(F32)
     fin_l = swap((left[1] + got_l[rows_q:]).astype(BF), "expert", hi).astype(F32)
@@ -376,8 +390,9 @@
     grads = kept[:shard]
     for j in range(1, n_dp):
         grads = grads + swap(kept[j * shard : (j + 1) * shard].astype(BF), "dp", j).astype(F32)
-    grad_out = scale * grads[:, :width]
-    grad_router = scale * grads[:, width : width + experts]
+    grads = scale * grads
+    grad_out = grads[:, :width]
+    grad_router = sum([grads[:, width + i * experts : width + (i + 1) * experts] for i in range(3)])
 
     grad_fc1 = wgrad(scale, exp_dev, slot_in, [r[3] for r in results])
     grad_fc2 = wgrad(scale, exp_dev, [r[2] for r in results], slot_cot)

time: 388 us -> 385 us (level)
  starting transfers between devices: 99.7 us -> 115 us
  waiting for transfers between devices: 127 us -> 115 us
    ppermute x34, waiting for transfers between devices: 111 us -> 93.2 us  [swap(): return lax.ppermute(value, axis, [(i, i ^ bit) for i in range(n)])]
    ppermute x34, starting transfers between devices: 58.9 us -> 74.3 us  [swap(): return lax.ppermute(value, axis, [(i, i ^ bit) for i in range(n)])]
    all_to_all x10, waiting for transfers between devices: 15.8 us -> 22.1 us  [exchange(): lax.all_to_all(value, 'expert', split_axis=0, concat_axis=0, tiled=True)]
    unnamed x59 -> x61, local copies, waits for them, and re-layouts: 9 us -> 6.04 us
    dot_general x36 -> x38, matrix products: 52.6 us -> 50.8 us  [dot32(): lax.dot_general(a, b, (dims, ((), ())), preferred_element_type=F32, preci...]
  transfers between devices with their start and end apart: 44 -> 44, of which waited for: 21 -> 23; matrix products, arithmetic and copies ran while one was open for 19% -> 18% of each run, Pallas kernels for 13% -> 13%
where the time goes in v3:
time: 385 us; the launch traced here: 383 us
  starting transfers between devices  115 us (30%)
  waiting for transfers between devices  115 us (30%)
  Pallas kernels  72.7 us (19%)
  matrix products  50.8 us (13%)
  other arithmetic  14.4 us (4%)
  local copies, waits for them, and re-layouts  13.8 us (4%)
    ppermute x34, waiting for transfers between devices, swap(): return lax.ppermute(value, axis, [(i, i ^ bit) for i in range(n)])  93.2 us
    ppermute x34, starting transfers between devices, swap(): return lax.ppermute(value, axis, [(i, i ^ bit) for i in range(n)])  74.3 us
    dot_general x38, matrix products, dot32(): lax.dot_general(a, b, (dims, ((), ())), preferred_element_type=F32, preci...  50.8 us
    pallas_call x2, Pallas kernels, ffn(): pl.pallas_call(ffn_kernel, grid=(e, hidden // hc), in_specs=[row_spec, ro...  43.9 us
    all_to_all x10, starting transfers between devices, exchange(): lax.all_to_all(value, 'expert', split_axis=0, concat_axis=0, tiled=True)  40.5 us
    pallas_call x2, Pallas kernels, wgrad(): pl.pallas_call(functools.partial(wgrad_kernel, scale, len(lefts)), grid=(...  28.8 us
    all_to_all x10, waiting for transfers between devices, exchange(): lax.all_to_all(value, 'expert', split_axis=0, concat_axis=0, tiled=True)  22.1 us
  transfers between devices with their start and end apart: 44, of which 23 were waited for; matrix products, arithmetic and copies ran while one was open for 18% of the time, Pallas kernels for 13%

profile of v3, /device:TPU:0, one launch (start us, length us, event | category | flops | bytes accessed | tf_op | source)
XLA Modules:
  0.0 383.3 jit_solution(3045504608651769266)
XLA Ops:
  0.6 5.1 %collective-permute-start.12 = (s32[2,128]{1,0:T(2,128)}, s32[2,128]{1,0:T(2,128)S(1)}, u32[]{:S(2)}, u32[]{:S(2)}) collective-permute-start(s32[2,128]{1,0:T(2,128)} %bitcast.177), channel_id=1, source_target_pairs={{0,24},{8,16},{16,8},{24,0},{1,25},{9,17},{17,9},{25,1},{2,26},{10... | collective-permute-start | bytes 3080 | tf_op jit(solution)/shard_map/ppermute | solution.py:24
  6.4 2.3 collective-permute-start.1
  15.0 3.7 collective-permute-start.17
  19.2 3.3 collective-permute-done.2
  26.5 5.5 %collective-permute-done.4 = bf16[160,1280]{1,0:T(8,128)(2,1)S(1)} collective-permute-done((bf16[160,1280]{1,0:T(8,128)(2,1)}, bf16[160,1280]{1,0:T(8,128)(2,1)S(1)}, u32[]{:S(2)}, u32[]{:S(2)}) %collective-permute-start.4) | collective-permute-done | bytes 409632 | tf_op jit(solution)/shard_map/ppermute | solution.py:24
  36.3 4.8 %collective-permute-done.5 = bf16[80,1280]{1,0:T(8,128)(2,1)S(1)} collective-permute-done((bf16[80,1280]{1,0:T(8,128)(2,1)S(1)}, bf16[80,1280]{1,0:T(8,128)(2,1)S(1)}, u32[]{:S(2)}, u32[]{:S(2)}) %collective-permute-start.5) | collective-permute-done | bytes 204832 | tf_op jit(solution)/shard_map/ppermute | solution.py:24
  43.6 3.3 all-to-all-start.2
  51.8 4.2 %all-to-all-start.1 = ((bf16[8,40,1280]{2,1,0:T(8,128)(2,1)}), bf16[8,40,1280]{2,1,0:T(8,128)(2,1)}, u32[]{:S(2)}, u32[]{:S(2)}) async-start(bf16[8,40,1280]{2,1,0:T(8,128)(2,1)} %bitcast.11), calls=%async_computation.1 | async-start | bytes 1638400 | tf_op jit(solution)/shard_map/all_to_all | solution.py:28
  57.4 11.5 %all-to-all-done.1 = bf16[8,40,1280]{2,1,0:T(8,128)(2,1)} async-done(((bf16[8,40,1280]{2,1,0:T(8,128)(2,1)}), bf16[8,40,1280]{2,1,0:T(8,128)(2,1)}, u32[]{:S(2)}, u32[]{:S(2)}) %all-to-all-start.1) | async-done | bytes 819232 | tf_op jit(solution)/shard_map/all_to_all | solution.py:28
  68.9 4.2 %all-to-all-start = ((bf16[8,40,1280]{2,1,0:T(8,128)(2,1)}), bf16[8,40,1280]{2,1,0:T(8,128)(2,1)}, u32[]{:S(2)}, u32[]{:S(2)}) async-start(bf16[8,40,1280]{2,1,0:T(8,128)(2,1)} %bitcast.8), calls=%async_computation | async-start | bytes 1638400 | tf_op jit(solution)/shard_map/all_to_all | solution.py:28
  74.1 12.2 %collective-permute-start.9 = (bf16[320,1280]{1,0:T(8,128)(2,1)}, bf16[320,1280]{1,0:T(8,128)(2,1)}, u32[]{:S(2)}, u32[]{:S(2)}) collective-permute-start(bf16[320,1280]{1,0:T(8,128)(2,1)} %bitcast.12), channel_id=1, source_target_pairs={{0,8},{8,0},{16,24},{24,16},{1,9},{9,1},{17,25},{25,17},{2,10},{10... | collective-permute-start | bytes 2457608 | tf_op jit(solution)/shard_map/ppermute | solution.py:24
  86.4 2.9 convolution_convert_fusion.1
  89.3 4.3 %all-to-all-start.5 = ((bf16[8,80,1280]{2,1,0:T(8,128)(2,1)}), bf16[8,80,1280]{2,1,0:T(8,128)(2,1)}, u32[]{:S(2)}, u32[]{:S(2)}) async-start(bf16[8,80,1280]{2,1,0:T(8,128)(2,1)} %bitcast.167), calls=%async_computation.5 | async-start | bytes 3276800 | tf_op jit(solution)/shard_map/all_to_all | solution.py:28
  95.1 9.1 %collective-permute-start.8 = (bf16[320,1280]{1,0:T(8,128)(2,1)}, bf16[320,1280]{1,0:T(8,128)(2,1)}, u32[]{:S(2)}, u32[]{:S(2)}) collective-permute-start(bf16[320,1280]{1,0:T(8,128)(2,1)} %bitcast.9), channel_id=1, source_target_pairs={{0,8},{8,0},{16,24},{24,16},{1,9},{9,1},{17,25},{25,17},{2,10},{10... | collective-permute-start | bytes 2457608 | tf_op jit(solution)/shard_map/ppermute | solution.py:24
  105.5 4.1 %convolution_convert_fusion.5 = bf16[640,1280]{1,0:T(8,128)(2,1)} fusion(bf16[320,1280]{1,0:T(8,128)(2,1)} %collective-permute-done.9, bf16[320,1280]{1,0:T(8,128)(2,1)} %bitcast.12, s32[640]{0:T(1024)S(1)} %fusion.161), kind=kOutput, calls=%fused_computation.14 | convolution fusion | flops 1053081600 | bytes 3279360 | tf_op jit(solution)/shard_map/dot_general | solution.py:17
  110.0 2.8 collective-permute-start.14
  113.0 2.2 fusion.13
  115.2 15.9 %collective-permute-done.15 = bf16[128,1280]{1,0:T(8,128)(2,1)S(1)} collective-permute-done((bf16[128,1280]{1,0:T(8,128)(2,1)S(1)}, bf16[128,1280]{1,0:T(8,128)(2,1)S(1)}, u32[]{:S(2)}, u32[]{:S(2)}) %collective-permute-start.15) | collective-permute-done | bytes 327712 | tf_op jit(solution)/shard_map/ppermute | solution.py:24
  131.1 9.9 %collective-permute-done.14 = bf16[128,1280]{1,0:T(8,128)(2,1)S(1)} collective-permute-done((bf16[128,1280]{1,0:T(8,128)(2,1)S(1)}, bf16[128,1280]{1,0:T(8,128)(2,1)S(1)}, u32[]{:S(2)}, u32[]{:S(2)}) %collective-permute-start.14) | collective-permute-done | bytes 327712 | tf_op jit(solution)/shard_map/ppermute | solution.py:24
  142.8 4.5 %all-to-all-start.4 = ((bf16[8,80,1280]{2,1,0:T(8,128)(2,1)}), bf16[8,80,1280]{2,1,0:T(8,128)(2,1)}, u32[]{:S(2)}, u32[]{:S(2)}) async-start(bf16[8,80,1280]{2,1,0:T(8,128)(2,1)} %bitcast.168), calls=%async_computation.4 | async-start | bytes 3276800 | tf_op jit(solution)/shard_map/all_to_all | solution.py:28
  147.9 4.1 %convolution_convert_fusion.6 = bf16[640,1280]{1,0:T(8,128)(2,1)} fusion(bf16[320,1280]{1,0:T(8,128)(2,1)} %collective-permute-done.8, bf16[320,1280]{1,0:T(8,128)(2,1)} %bitcast.9, s32[640]{0:T(1024)S(1)} %fusion.161), kind=kOutput, calls=%fused_computation.15 | convolution fusion | flops 1053081600 | bytes 3279360 | tf_op jit(solution)/shard_map/dot_general | solution.py:17
  152.0 22.0 %shard_map.135 = (bf16[2,320,1280]{2,1,0:T(8,128)(2,1)}, bf16[2,320,1280]{2,1,0:T(8,128)(2,1)}, bf16[2,320,1280]{2,1,0:T(8,128)(2,1)}, bf16[2,320,1280]{2,1,0:T(8,128)(2,1)}, f32[2,320,1]{2,1,0:T(8,128)}) custom-call(bf16[2,320,1280]{2,1,0:T(8,128)(2,1)} %bitcast.163, bf16[2,320,1280]{2,1,0:T(8,128)(2,1)} %bitcast.161, ...), custom_call_target="tpu_custom_call" | custom-call | flops 8388608000 | bytes 26214400 | tf_op jit(solution)/shard_map/pallas_call | solution.py:91
  175.3 4.1 %convolution_convert_fusion.4 = bf16[640,1280]{1,0:T(8,128)(2,1)} fusion(bf16[640,1280]{1,0:T(8,128)(2,1)} %bitcast.206, s32[640]{0:T(1024)S(1)} %fusion.161), kind=kOutput, calls=%fused_computation.13 | convolution fusion | flops 1049804800 | bytes 3279360 | tf_op jit(solution)/shard_map/dot_general | solution.py:17
  179.5 21.9 %shard_map.136 = (bf16[8,2,40,1280]{3,2,1,0:T(8,128)(2,1)}, bf16[8,2,40,1280]{3,2,1,0:T(8,128)(2,1)}, bf16[2,320,1280]{2,1,0:T(8,128)(2,1)}, bf16[2,320,1280]{2,1,0:T(8,128)(2,1)}, f32[2,320,1]{2,1,0:T(8,128)}) custom-call(bf16[8,2,40,1280]{3,2,1,0:T(8,128)(2,1)} %bitcast.39.x_ref.refs_1_, bf16[8,2,40,1280]{3,2,1,0:T(8,128)(2,1)} %bitcast.41.c_ref.refs_3_, ...), custom_call_target="tpu_custom_call" | custom-call | flops 8388608000 | bytes 26214400 | tf_op jit(solution)/shard_map/pallas_call | solution.py:91
  203.4 3.9 %all-to-all-start.7 = ((f32[8,8,128]{2,1,0:T(8,128)}), f32[8,8,128]{2,1,0:T(8,128)S(1)}, u32[]{:S(2)}, u32[]{:S(2)}) async-start(f32[8,8,128]{2,1,0:T(8,128)} %copy.39), calls=%async_computation.7 | async-start | bytes 65536 | tf_op jit(solution)/shard_map/all_to_all | solution.py:28
  207.3 3.0 convolution_convert_fusion.3
  216.2 4.3 %all-to-all-start.6 = ((bf16[8,80,1280]{2,1,0:T(8,128)(2,1)}), bf16[8,80,1280]{2,1,0:T(8,128)(2,1)}, u32[]{:S(2)}, u32[]{:S(2)}) async-start(bf16[8,80,1280]{2,1,0:T(8,128)(2,1)} %bitcast.166), calls=%async_computation.6 | async-start | bytes 3276800 | tf_op jit(solution)/shard_map/all_to_all | solution.py:28
  225.3 2.4 collective-permute-start.22
  228.8 14.4 %shard_map.137 = f32[2,1280,1280]{2,1,0:T(8,128)} custom-call(bf16[2,320,1280]{2,1,0:T(8,128)(2,1)} %bitcast.164, bf16[8,2,40,1280]{3,2,1,0:T(8,128)(2,1)} %bitcast.39.x_ref.refs_1_, bf16[2,320,1280]{2,1,0:T(8,128)(2,1)} %get-tuple-element.35.refs_2_, bf16[2,320,1280]{2,1,0:T(8,128)(2,1)} %get-tuple-element.36.refs_3_), custom_call_target="tpu_custom_call" | custom-call | flops 4194304000 | bytes 19660800 | tf_op jit(solution)/shard_map/pallas_call | solution.py:138
  243.2 7.4 %collective-permute-done.21 = f32[2,128]{1,0:T(2,128)S(1)} collective-permute-done((f32[2,128]{1,0:T(2,128)}, f32[2,128]{1,0:T(2,128)S(1)}, u32[]{:S(2)}, u32[]{:S(2)}) %collective-permute-start.21) | collective-permute-done | bytes 1056 | tf_op jit(solution)/shard_map/ppermute | solution.py:24
  252.9 2.3 add_convert_fusion.1
  255.1 3.8 all-to-all-start.3
  266.9 5.0 %all-to-all-done.3 = bf16[8,40,1280]{2,1,0:T(8,128)(2,1)S(1)} async-done(((bf16[8,40,1280]{2,1,0:T(8,128)(2,1)}), bf16[8,40,1280]{2,1,0:T(8,128)(2,1)S(1)}, u32[]{:S(2)}, u32[]{:S(2)}) %all-to-all-start.3) | async-done | bytes 819232 | tf_op jit(solution)/shard_map/all_to_all | solution.py:28
  271.9 4.3 %all-to-all-start.9 = ((bf16[8,80,1280]{2,1,0:T(8,128)(2,1)}), bf16[8,80,1280]{2,1,0:T(8,128)(2,1)}, u32[]{:S(2)}, u32[]{:S(2)}) async-start(bf16[8,80,1280]{2,1,0:T(8,128)(2,1)} %bitcast.165), calls=%async_computation.9 | async-start | bytes 3276800 | tf_op jit(solution)/shard_map/all_to_all | solution.py:28
  276.2 11.0 %collective-permute-done.18 = bf16[128,1280]{1,0:T(8,128)(2,1)} collective-permute-done((bf16[128,1280]{1,0:T(8,128)(2,1)}, bf16[128,1280]{1,0:T(8,128)(2,1)}, u32[]{:S(2)}, u32[]{:S(2)}) %collective-permute-start.18) | collective-permute-done | bytes 327712 | tf_op jit(solution)/shard_map/ppermute | solution.py:24
  292.1 2.3 add_convert_fusion
  294.4 3.5 all-to-all-done.9
  297.9 3.5 all-to-all-start.8
  304.5 5.1 %collective-permute-start.24 = (bf16[128,1280]{1,0:T(8,128)(2,1)}, bf16[128,1280]{1,0:T(8,128)(2,1)}, u32[]{:S(2)}, u32[]{:S(2)}) collective-permute-start(bf16[128,1280]{1,0:T(8,128)(2,1)} %get-tuple-element.88), channel_id=1, source_target_pairs={{0,16},{8,24},{16,0},{24,8},{1,17},{9,25},{17,1},{25,9},{2,18},{10... | collective-permute-start | bytes 983048 | tf_op jit(solution)/shard_map/ppermute | solution.py:24
  311.1 14.4 %shard_map.138 = f32[2,1280,1280]{2,1,0:T(8,128)} custom-call(bf16[2,320,1280]{2,1,0:T(8,128)(2,1)} %get-tuple-element.37.refs_0_, bf16[2,320,1280]{2,1,0:T(8,128)(2,1)} %get-tuple-element.38.refs_1_, bf16[2,320,1280]{2,1,0:T(8,128)(2,1)} %bitcast.162, bf16[8,2,40,1280]{3,2,1,0:T(8,128)(2,1)} %bitcast.41.c_ref.refs_3_), custom_call_target="tpu_custom_call" | custom-call | flops 4194304000 | bytes 19660800 | tf_op jit(solution)/shard_map/pallas_call | solution.py:138
  325.5 7.0 %collective-permute-done.24 = bf16[128,1280]{1,0:T(8,128)(2,1)} collective-permute-done((bf16[128,1280]{1,0:T(8,128)(2,1)}, bf16[128,1280]{1,0:T(8,128)(2,1)}, u32[]{:S(2)}, u32[]{:S(2)}) %collective-permute-start.24) | collective-permute-done | bytes 327712 | tf_op jit(solution)/shard_map/ppermute | solution.py:24
  341.8 6.9 %collective-permute-done.27 = bf16[320,640]{1,0:T(8,128)(2,1)S(1)} collective-permute-done((bf16[320,640]{1,0:T(8,128)(2,1)S(1)}, bf16[320,640]{1,0:T(8,128)(2,1)S(1)}, u32[]{:S(2)}, u32[]{:S(2)}) %collective-permute-start.27) | collective-permute-done | bytes 409632 | tf_op jit(solution)/shard_map/ppermute | solution.py:24
  350.1 2.5 collective-permute-done.29
  352.7 3.2 collective-permute-done.28
  359.0 4.0 %collective-permute-done.30 = bf16[160,768]{1,0:T(8,128)(2,1)S(1)} collective-permute-done((bf16[160,768]{1,0:T(8,128)(2,1)S(1)}, bf16[160,768]{1,0:T(8,128)(2,1)S(1)}, u32[]{:S(2)}, u32[]{:S(2)}) %collective-permute-start.30) | collective-permute-done | bytes 245792 | tf_op jit(solution)/shard_map/ppermute | solution.py:24
  363.1 7.8 %collective-permute-start.31 = (bf16[40,1408]{1,0:T(8,128)(2,1)S(1)}, bf16[40,1408]{1,0:T(8,128)(2,1)S(1)}, u32[]{:S(2)}, u32[]{:S(2)}) collective-permute-start(bf16[40,1408]{1,0:T(8,128)(2,1)S(1)} %get-tuple-element.92), channel_id=1, source_target_pairs={{0,8},{8,0},{16,24},{24,16},{1,9},{9,1},{17,25},{25,17},{2,10},{10... | collective-permute-start | bytes 337928 | tf_op jit(solution)/shard_map/ppermute | solution.py:24
  375.2 2.9 collective-permute-done.33
  378.2 3.6 collective-permute-done.32
  (237 shorter events, 85.4 us)
Async XLA Ops:
  0.6 14.2 %collective-permute-start.12 = (s32[2,128]{1,0:T(2,128)}, s32[2,128]{1,0:T(2,128)S(1)}, u32[]{:S(2)}, u32[]{:S(2)}) collective-permute-start(s32[2,128]{1,0:T(2,128)} %bitcast.177), channel_id=1, source_target_pairs={{0,24},{8,16},{16,8},{24,0},{1,25},{9,17},{17,9},{25,1},{2,26},{10... | collective-permute-start | bytes 3080 | tf_op jit(solution)/shard_map/ppermute | solution.py:24
  5.8 9.3 %collective-permute-start.11 = (s32[2,128]{1,0:T(2,128)}, s32[2,128]{1,0:T(2,128)S(1)}, u32[]{:S(2)}, u32[]{:S(2)}) collective-permute-start(s32[2,128]{1,0:T(2,128)} %bitcast.178), channel_id=1, source_target_pairs={{0,16},{8,24},{16,0},{24,8},{1,17},{9,25},{17,1},{25,9},{2,18},{10... | collective-permute-start | bytes 3080 | tf_op jit(solution)/shard_map/ppermute | solution.py:24
  5.8 13.0 %collective-permute-start.10 = (s32[2,128]{1,0:T(2,128)}, s32[2,128]{1,0:T(2,128)S(1)}, u32[]{:S(2)}, u32[]{:S(2)}) collective-permute-start(s32[2,128]{1,0:T(2,128)} %bitcast.179), channel_id=1, source_target_pairs={{0,8},{8,0},{16,24},{24,16},{1,9},{9,1},{17,25},{25,17},{2,10},{10... | collective-permute-start | bytes 3080 | tf_op jit(solution)/shard_map/ppermute | solution.py:24
  6.4 12.8 %collective-permute-start.1 = (bf16[40,1280]{1,0:T(8,128)(2,1)}, bf16[40,1280]{1,0:T(8,128)(2,1)S(1)}, u32[]{:S(2)}, u32[]{:S(2)}) collective-permute-start(bf16[40,1280]{1,0:T(8,128)(2,1)} %param.10), channel_id=1, source_target_pairs={{0,16},{8,24},{16,0},{24,8},{1,17},{9,25},{17,1},{25,9},{2,18},{10... | collective-permute-start | bytes 307208 | tf_op jit(solution)/shard_map/ppermute | solution.py:24
  8.7 10.5 %collective-permute-start = (bf16[40,1280]{1,0:T(8,128)(2,1)}, bf16[40,1280]{1,0:T(8,128)(2,1)S(1)}, u32[]{:S(2)}, u32[]{:S(2)}) collective-permute-start(bf16[40,1280]{1,0:T(8,128)(2,1)} %param.10), channel_id=1, source_target_pairs={{0,8},{8,0},{16,24},{24,16},{1,9},{9,1},{17,25},{25,17},{2,10},{10... | collective-permute-start | bytes 307208 | tf_op jit(solution)/shard_map/ppermute | solution.py:24
  13.6 275.8 %copy-start.6 = (bf16[128,1280]{0,1:T(8,128)(2,1)}, bf16[128,1280]{0,1:T(8,128)(2,1)S(1)}, u32[]{:S(2)}) copy-start(bf16[128,1280]{0,1:T(8,128)(2,1)S(1)} %fusion.14) | copy-start | bytes 983044
  14.9 7.7 %collective-permute-start.2 = (bf16[40,1280]{1,0:T(8,128)(2,1)S(1)}, bf16[40,1280]{1,0:T(8,128)(2,1)S(1)}, u32[]{:S(2)}, u32[]{:S(2)}) collective-permute-start(bf16[40,1280]{1,0:T(8,128)(2,1)S(1)} %copy-done.13), channel_id=1, source_target_pairs={{0,24},{8,16},{16,8},{24,0},{1,25},{9,17},{17,9},{25,1},{2,26},{10... | collective-permute-start | bytes 307208 | tf_op jit(solution)/shard_map/ppermute | solution.py:24
  15.0 71.3 %collective-permute-start.17 = (bf16[128,1280]{1,0:T(8,128)(2,1)S(1)}, bf16[128,1280]{1,0:T(8,128)(2,1)}, u32[]{:S(2)}, u32[]{:S(2)}) collective-permute-start(bf16[128,1280]{1,0:T(8,128)(2,1)S(1)} %copy-done.8), channel_id=1, source_target_pairs={{0,24},{8,16},{16,8},{24,0},{1,25},{9,17},{17,9},{25,1},{2,26},{10... | collective-permute-start | bytes 983048 | tf_op jit(solution)/shard_map/ppermute | solution.py:24
  18.8 67.6 %collective-permute-start.16 = (bf16[128,1280]{1,0:T(8,128)(2,1)S(1)}, bf16[128,1280]{1,0:T(8,128)(2,1)}, u32[]{:S(2)}, u32[]{:S(2)}) collective-permute-start(bf16[128,1280]{1,0:T(8,128)(2,1)S(1)} %copy-done.8), channel_id=1, source_target_pairs={{0,16},{8,24},{16,0},{24,8},{1,17},{9,25},{17,1},{25,9},{2,18},{10... | collective-permute-start | bytes 983048 | tf_op jit(solution)/shard_map/ppermute | solution.py:24
  23.3 8.7 %collective-permute-start.4 = (bf16[160,1280]{1,0:T(8,128)(2,1)}, bf16[160,1280]{1,0:T(8,128)(2,1)S(1)}, u32[]{:S(2)}, u32[]{:S(2)}) collective-permute-start(bf16[160,1280]{1,0:T(8,128)(2,1)} %copy-done.16), channel_id=1, source_target_pairs={{0,2},{1,3},{2,0},{3,1},{4,6},{5,7},{6,4},{7,5},{8,10},{9,11},{10,... | collective-permute-start | bytes 1228808 | tf_op jit(solution)/shard_map/ppermute | solution.py:24
  24.8 10.4 %collective-permute-start.3 = (bf16[160,1280]{1,0:T(8,128)(2,1)}, bf16[160,1280]{1,0:T(8,128)(2,1)S(1)}, u32[]{:S(2)}, u32[]{:S(2)}) collective-permute-start(bf16[160,1280]{1,0:T(8,128)(2,1)} %copy-done.16), channel_id=1, source_target_pairs={{0,4},{1,5},{2,6},{3,7},{4,0},{5,1},{6,2},{7,3},{8,12},{9,13},{10,... | collective-permute-start | bytes 1228808 | tf_op jit(solution)/shard_map/ppermute | solution.py:24
  32.0 9.0 %collective-permute-start.6 = (bf16[80,1280]{1,0:T(8,128)(2,1)S(1)}, bf16[80,1280]{1,0:T(8,128)(2,1)S(1)}, u32[]{:S(2)}, u32[]{:S(2)}) collective-permute-start(bf16[80,1280]{1,0:T(8,128)(2,1)S(1)} %slice.287), channel_id=1, source_target_pairs={{0,4},{1,5},{2,6},{3,7},{4,0},{5,1},{6,2},{7,3},{8,12},{9,13},{10,... | collective-permute-start | bytes 614408 | tf_op jit(solution)/shard_map/ppermute | solution.py:24
  35.2 5.8 %collective-permute-start.5 = (bf16[80,1280]{1,0:T(8,128)(2,1)S(1)}, bf16[80,1280]{1,0:T(8,128)(2,1)S(1)}, u32[]{:S(2)}, u32[]{:S(2)}) collective-permute-start(bf16[80,1280]{1,0:T(8,128)(2,1)S(1)} %slice.286), channel_id=1, source_target_pairs={{0,2},{1,3},{2,0},{3,1},{4,6},{5,7},{6,4},{7,5},{8,10},{9,11},{10,... | collective-permute-start | bytes 614408 | tf_op jit(solution)/shard_map/ppermute | solution.py:24
  41.1 5.9 %collective-permute-start.7 = (bf16[640,1280]{1,0:T(8,128)(2,1)S(1)}, bf16[640,1280]{1,0:T(8,128)(2,1)}, u32[]{:S(2)}, u32[]{:S(2)}) collective-permute-start(bf16[640,1280]{1,0:T(8,128)(2,1)S(1)} %constant_dynamic-update-slice_fusion.4), channel_id=1, source_target_pairs={{0,1},{1,0},{2,3},{3,2},{4,5},{5,4},{6,7},{7,6},{8,9},{9,8},{10,11... | collective-permute-start | bytes 4915208 | tf_op jit(solution)/shard_map/ppermute | solution.py:24
  41.4 99.5 %copy-start.19 = (s32[1,256]{1,0:T(1,128)}, s32[1,256]{1,0:T(1,128)S(1)}, u32[]{:S(2)}) copy-start(s32[1,256]{1,0:T(1,128)S(1)} %pad_add_fusion.3) | copy-start | bytes 3076
  41.5 99.5 %copy-start.21 = (s32[1,256]{1,0:T(1,128)}, s32[1,256]{1,0:T(1,128)S(1)}, u32[]{:S(2)}) copy-start(s32[1,256]{1,0:T(1,128)S(1)} %pad_add_fusion.2) | copy-start | bytes 3076
  43.6 8.1 %all-to-all-start.2 = ((f32[8,8,128]{2,1,0:T(8,128)}), f32[8,8,128]{2,1,0:T(8,128)S(1)}, u32[]{:S(2)}, u32[]{:S(2)}) async-start(f32[8,8,128]{2,1,0:T(8,128)} %bitcast.156), calls=%async_computation.2 | async-start | bytes 65536 | tf_op jit(solution)/shard_map/all_to_all | solution.py:28
  51.8 17.2 %all-to-all-start.1 = ((bf16[8,40,1280]{2,1,0:T(8,128)(2,1)}), bf16[8,40,1280]{2,1,0:T(8,128)(2,1)}, u32[]{:S(2)}, u32[]{:S(2)}) async-start(bf16[8,40,1280]{2,1,0:T(8,128)(2,1)} %bitcast.11), calls=%async_computation.1 | async-start | bytes 1638400 | tf_op jit(solution)/shard_map/all_to_all | solution.py:28
  68.9 20.3 %all-to-all-start = ((bf16[8,40,1280]{2,1,0:T(8,128)(2,1)}), bf16[8,40,1280]{2,1,0:T(8,128)(2,1)}, u32[]{:S(2)}, u32[]{:S(2)}) async-start(bf16[8,40,1280]{2,1,0:T(8,128)(2,1)} %bitcast.8), calls=%async_computation | async-start | bytes 1638400 | tf_op jit(solution)/shard_map/all_to_all | solution.py:28
  74.1 31.3 %collective-permute-start.9 = (bf16[320,1280]{1,0:T(8,128)(2,1)}, bf16[320,1280]{1,0:T(8,128)(2,1)}, u32[]{:S(2)}, u32[]{:S(2)}) collective-permute-start(bf16[320,1280]{1,0:T(8,128)(2,1)} %bitcast.12), channel_id=1, source_target_pairs={{0,8},{8,0},{16,24},{24,16},{1,9},{9,1},{17,25},{25,17},{2,10},{10... | collective-permute-start | bytes 2457608 | tf_op jit(solution)/shard_map/ppermute | solution.py:24
  89.3 53.5 %all-to-all-start.5 = ((bf16[8,80,1280]{2,1,0:T(8,128)(2,1)}), bf16[8,80,1280]{2,1,0:T(8,128)(2,1)}, u32[]{:S(2)}, u32[]{:S(2)}) async-start(bf16[8,80,1280]{2,1,0:T(8,128)(2,1)} %bitcast.167), calls=%async_computation.5 | async-start | bytes 3276800 | tf_op jit(solution)/shard_map/all_to_all | solution.py:28
  95.1 52.8 %collective-permute-start.8 = (bf16[320,1280]{1,0:T(8,128)(2,1)}, bf16[320,1280]{1,0:T(8,128)(2,1)}, u32[]{:S(2)}, u32[]{:S(2)}) collective-permute-start(bf16[320,1280]{1,0:T(8,128)(2,1)} %bitcast.9), channel_id=1, source_target_pairs={{0,8},{8,0},{16,24},{24,16},{1,9},{9,1},{17,25},{25,17},{2,10},{10... | collective-permute-start | bytes 2457608 | tf_op jit(solution)/shard_map/ppermute | solution.py:24
  109.6 21.5 %collective-permute-start.15 = (bf16[128,1280]{1,0:T(8,128)(2,1)S(1)}, bf16[128,1280]{1,0:T(8,128)(2,1)S(1)}, u32[]{:S(2)}, u32[]{:S(2)}) collective-permute-start(bf16[128,1280]{1,0:T(8,128)(2,1)S(1)} %fusion.40), channel_id=1, source_target_pairs={{0,24},{8,16},{16,8},{24,0},{1,25},{9,17},{17,9},{25,1},{2,26},{10... | collective-permute-start | bytes 983048 | tf_op jit(solution)/shard_map/ppermute | solution.py:24
  110.0 31.0 %collective-permute-start.14 = (bf16[128,1280]{1,0:T(8,128)(2,1)S(1)}, bf16[128,1280]{1,0:T(8,128)(2,1)S(1)}, u32[]{:S(2)}, u32[]{:S(2)}) collective-permute-start(bf16[128,1280]{1,0:T(8,128)(2,1)S(1)} %fusion.40), channel_id=1, source_target_pairs={{0,16},{8,24},{16,0},{24,8},{1,17},{9,25},{17,1},{25,9},{2,18},{10... | collective-permute-start | bytes 983048 | tf_op jit(solution)/shard_map/ppermute | solution.py:24
  142.8 36.7 %all-to-all-start.4 = ((bf16[8,80,1280]{2,1,0:T(8,128)(2,1)}), bf16[8,80,1280]{2,1,0:T(8,128)(2,1)}, u32[]{:S(2)}, u32[]{:S(2)}) async-start(bf16[8,80,1280]{2,1,0:T(8,128)(2,1)} %bitcast.168), calls=%async_computation.4 | async-start | bytes 3276800 | tf_op jit(solution)/shard_map/all_to_all | solution.py:28
  203.4 12.8 %all-to-all-start.7 = ((f32[8,8,128]{2,1,0:T(8,128)}), f32[8,8,128]{2,1,0:T(8,128)S(1)}, u32[]{:S(2)}, u32[]{:S(2)}) async-start(f32[8,8,128]{2,1,0:T(8,128)} %copy.39), calls=%async_computation.7 | async-start | bytes 65536 | tf_op jit(solution)/shard_map/all_to_all | solution.py:28
  214.2 38.7 %collective-permute-start.13 = (bf16[320,1280]{1,0:T(8,128)(2,1)}, bf16[320,1280]{1,0:T(8,128)(2,1)S(1)}, u32[]{:S(2)}, u32[]{:S(2)}) collective-permute-start(bf16[320,1280]{1,0:T(8,128)(2,1)} %slice.291), channel_id=1, source_target_pairs={{0,8},{8,0},{16,24},{24,16},{1,9},{9,1},{17,25},{25,17},{2,10},{10... | collective-permute-start | bytes 2457608 | tf_op jit(solution)/shard_map/ppermute | solution.py:24
  214.2 77.2 %collective-permute-start.23 = (bf16[320,1280]{1,0:T(8,128)(2,1)}, bf16[320,1280]{1,0:T(8,128)(2,1)}, u32[]{:S(2)}, u32[]{:S(2)}) collective-permute-start(bf16[320,1280]{1,0:T(8,128)(2,1)} %slice.302), channel_id=1, source_target_pairs={{0,8},{8,0},{16,24},{24,16},{1,9},{9,1},{17,25},{25,17},{2,10},{10... | collective-permute-start | bytes 2457608 | tf_op jit(solution)/shard_map/ppermute | solution.py:24
  216.2 38.9 %all-to-all-start.6 = ((bf16[8,80,1280]{2,1,0:T(8,128)(2,1)}), bf16[8,80,1280]{2,1,0:T(8,128)(2,1)}, u32[]{:S(2)}, u32[]{:S(2)}) async-start(bf16[8,80,1280]{2,1,0:T(8,128)(2,1)} %bitcast.166), calls=%async_computation.6 | async-start | bytes 3276800 | tf_op jit(solution)/shard_map/all_to_all | solution.py:28
  225.3 25.3 %collective-permute-start.21 = (f32[2,128]{1,0:T(2,128)}, f32[2,128]{1,0:T(2,128)S(1)}, u32[]{:S(2)}, u32[]{:S(2)}) collective-permute-start(f32[2,128]{1,0:T(2,128)} %get-tuple-element.114), channel_id=1, source_target_pairs={{0,16},{8,24},{16,0},{24,8},{1,17},{9,25},{17,1},{25,9},{2,18},{10... | collective-permute-start | bytes 3080 | tf_op jit(solution)/shard_map/ppermute | solution.py:24
  225.3 26.8 %collective-permute-start.22 = (f32[2,128]{1,0:T(2,128)S(1)}, f32[2,128]{1,0:T(2,128)S(1)}, u32[]{:S(2)}, u32[]{:S(2)}) collective-permute-start(f32[2,128]{1,0:T(2,128)S(1)} %get-tuple-element.115), channel_id=1, source_target_pairs={{0,24},{8,16},{16,8},{24,0},{1,25},{9,17},{17,9},{25,1},{2,26},{10... | collective-permute-start | bytes 3080 | tf_op jit(solution)/shard_map/ppermute | solution.py:24
  227.7 25.1 %collective-permute-start.20 = (f32[2,128]{1,0:T(2,128)S(1)}, f32[2,128]{1,0:T(2,128)S(1)}, u32[]{:S(2)}, u32[]{:S(2)}) collective-permute-start(f32[2,128]{1,0:T(2,128)S(1)} %pad_maximum_fusion.3), channel_id=1, source_target_pairs={{0,8},{8,0},{16,24},{24,16},{1,9},{9,1},{17,25},{25,17},{2,10},{10... | collective-permute-start | bytes 3080 | tf_op jit(solution)/shard_map/ppermute | solution.py:24
  255.1 16.7 %all-to-all-start.3 = ((bf16[8,40,1280]{2,1,0:T(8,128)(2,1)}), bf16[8,40,1280]{2,1,0:T(8,128)(2,1)S(1)}, u32[]{:S(2)}, u32[]{:S(2)}) async-start(bf16[8,40,1280]{2,1,0:T(8,128)(2,1)} %bitcast.160), calls=%async_computation.3 | async-start | bytes 1638400 | tf_op jit(solution)/shard_map/all_to_all | solution.py:28
  262.0 25.1 %collective-permute-start.18 = (bf16[128,1280]{1,0:T(8,128)(2,1)}, bf16[128,1280]{1,0:T(8,128)(2,1)}, u32[]{:S(2)}, u32[]{:S(2)}) collective-permute-start(bf16[128,1280]{1,0:T(8,128)(2,1)} %get-tuple-element.90), channel_id=1, source_target_pairs={{0,16},{8,24},{16,0},{24,8},{1,17},{9,25},{17,1},{25,9},{2,18},{10... | collective-permute-start | bytes 983048 | tf_op jit(solution)/shard_map/ppermute | solution.py:24
  263.1 24.0 %collective-permute-start.19 = (bf16[128,1280]{1,0:T(8,128)(2,1)}, bf16[128,1280]{1,0:T(8,128)(2,1)}, u32[]{:S(2)}, u32[]{:S(2)}) collective-permute-start(bf16[128,1280]{1,0:T(8,128)(2,1)} %get-tuple-element.91), channel_id=1, source_target_pairs={{0,24},{8,16},{16,8},{24,0},{1,25},{9,17},{17,9},{25,1},{2,26},{10... | collective-permute-start | bytes 983048 | tf_op jit(solution)/shard_map/ppermute | solution.py:24
  271.9 26.0 %all-to-all-start.9 = ((bf16[8,80,1280]{2,1,0:T(8,128)(2,1)}), bf16[8,80,1280]{2,1,0:T(8,128)(2,1)}, u32[]{:S(2)}, u32[]{:S(2)}) async-start(bf16[8,80,1280]{2,1,0:T(8,128)(2,1)} %bitcast.165), calls=%async_computation.9 | async-start | bytes 3276800 | tf_op jit(solution)/shard_map/all_to_all | solution.py:28
  289.4 67.5 %copy-start.2 = (bf16[128,1280]{1,0:T(8,128)(2,1)}, bf16[128,1280]{1,0:T(8,128)(2,1)S(1)}, u32[]{:S(2)}) copy-start(bf16[128,1280]{1,0:T(8,128)(2,1)S(1)} %add_convert_fusion.3) | copy-start | bytes 983044
  291.4 43.3 %collective-permute-start.26 = (bf16[640,1408]{1,0:T(8,128)(2,1)}, bf16[640,1408]{1,0:T(8,128)(2,1)}, u32[]{:S(2)}, u32[]{:S(2)}) collective-permute-start(bf16[640,1408]{1,0:T(8,128)(2,1)} %pad_maximum_fusion), channel_id=1, source_target_pairs={{0,1},{1,0},{2,3},{3,2},{4,5},{5,4},{6,7},{7,6},{8,9},{9,8},{10,11... | collective-permute-start | bytes 5406728 | tf_op jit(solution)/shard_map/ppermute | solution.py:24
  297.9 27.6 %all-to-all-start.8 = ((bf16[8,40,1280]{2,1,0:T(8,128)(2,1)}), bf16[8,40,1280]{2,1,0:T(8,128)(2,1)S(1)}, u32[]{:S(2)}, u32[]{:S(2)}) async-start(bf16[8,40,1280]{2,1,0:T(8,128)(2,1)} %bitcast.159), calls=%async_computation.8 | async-start | bytes 1638400 | tf_op jit(solution)/shard_map/all_to_all | solution.py:28
  304.5 28.0 %collective-permute-start.24 = (bf16[128,1280]{1,0:T(8,128)(2,1)}, bf16[128,1280]{1,0:T(8,128)(2,1)}, u32[]{:S(2)}, u32[]{:S(2)}) collective-permute-start(bf16[128,1280]{1,0:T(8,128)(2,1)} %get-tuple-element.88), channel_id=1, source_target_pairs={{0,16},{8,24},{16,0},{24,8},{1,17},{9,25},{17,1},{25,9},{2,18},{10... | collective-permute-start | bytes 983048 | tf_op jit(solution)/shard_map/ppermute | solution.py:24
  309.6 22.9 %collective-permute-start.25 = (bf16[128,1280]{1,0:T(8,128)(2,1)}, bf16[128,1280]{1,0:T(8,128)(2,1)}, u32[]{:S(2)}, u32[]{:S(2)}) collective-permute-start(bf16[128,1280]{1,0:T(8,128)(2,1)} %get-tuple-element.89), channel_id=1, source_target_pairs={{0,24},{8,16},{16,8},{24,0},{1,25},{9,17},{17,9},{25,1},{2,26},{10... | collective-permute-start | bytes 983048 | tf_op jit(solution)/shard_map/ppermute | solution.py:24
  337.5 11.2 %collective-permute-start.27 = (bf16[320,640]{1,0:T(8,128)(2,1)S(1)}, bf16[320,640]{1,0:T(8,128)(2,1)S(1)}, u32[]{:S(2)}, u32[]{:S(2)}) collective-permute-start(bf16[320,640]{1,0:T(8,128)(2,1)S(1)} %concatenate.148), channel_id=1, source_target_pairs={{0,2},{1,3},{2,0},{3,1},{4,6},{5,7},{6,4},{7,5},{8,10},{9,11},{10,... | collective-permute-start | bytes 1228808 | tf_op jit(solution)/shard_map/ppermute | solution.py:24
  339.6 13.0 %collective-permute-start.29 = (bf16[320,768]{1,0:T(8,128)(2,1)S(1)}, bf16[320,768]{1,0:T(8,128)(2,1)S(1)}, u32[]{:S(2)}, u32[]{:S(2)}) collective-permute-start(bf16[320,768]{1,0:T(8,128)(2,1)S(1)} %maximum_maximum_fusion), channel_id=1, source_target_pairs={{0,4},{1,5},{2,6},{3,7},{4,0},{5,1},{6,2},{7,3},{8,12},{9,13},{10,... | collective-permute-start | bytes 1474568 | tf_op jit(solution)/shard_map/ppermute | solution.py:24
  348.8 7.1 %collective-permute-start.28 = (bf16[160,640]{1,0:T(8,128)(2,1)S(1)}, bf16[160,640]{1,0:T(8,128)(2,1)S(1)}, u32[]{:S(2)}, u32[]{:S(2)}) collective-permute-start(bf16[160,640]{1,0:T(8,128)(2,1)S(1)} %fusion.43), channel_id=1, source_target_pairs={{0,4},{1,5},{2,6},{3,7},{4,0},{5,1},{6,2},{7,3},{8,12},{9,13},{10,... | collective-permute-start | bytes 614408 | tf_op jit(solution)/shard_map/ppermute | solution.py:24
  356.1 6.9 %collective-permute-start.30 = (bf16[160,768]{1,0:T(8,128)(2,1)S(1)}, bf16[160,768]{1,0:T(8,128)(2,1)S(1)}, u32[]{:S(2)}, u32[]{:S(2)}) collective-permute-start(bf16[160,768]{1,0:T(8,128)(2,1)S(1)} %fusion.41), channel_id=1, source_target_pairs={{0,2},{1,3},{2,0},{3,1},{4,6},{5,7},{6,4},{7,5},{8,10},{9,11},{10,... | collective-permute-start | bytes 737288 | tf_op jit(solution)/shard_map/ppermute | solution.py:24
  363.1 12.1 %collective-permute-start.31 = (bf16[40,1408]{1,0:T(8,128)(2,1)S(1)}, bf16[40,1408]{1,0:T(8,128)(2,1)S(1)}, u32[]{:S(2)}, u32[]{:S(2)}) collective-permute-start(bf16[40,1408]{1,0:T(8,128)(2,1)S(1)} %get-tuple-element.92), channel_id=1, source_target_pairs={{0,8},{8,0},{16,24},{24,16},{1,9},{9,1},{17,25},{25,17},{2,10},{10... | collective-permute-start | bytes 337928 | tf_op jit(solution)/shard_map/ppermute | solution.py:24
  371.0 7.2 %collective-permute-start.33 = (bf16[40,1408]{1,0:T(8,128)(2,1)S(1)}, bf16[40,1408]{1,0:T(8,128)(2,1)S(1)}, u32[]{:S(2)}, u32[]{:S(2)}) collective-permute-start(bf16[40,1408]{1,0:T(8,128)(2,1)S(1)} %get-tuple-element.93), channel_id=1, source_target_pairs={{0,24},{8,16},{16,8},{24,0},{1,25},{9,17},{17,9},{25,1},{2,26},{10... | collective-permute-start | bytes 337928 | tf_op jit(solution)/shard_map/ppermute | solution.py:24
  372.5 9.3 %collective-permute-start.32 = (bf16[40,1408]{1,0:T(8,128)(2,1)S(1)}, bf16[40,1408]{1,0:T(8,128)(2,1)S(1)}, u32[]{:S(2)}, u32[]{:S(2)}) collective-permute-start(bf16[40,1408]{1,0:T(8,128)(2,1)S(1)} %get-tuple-element.94), channel_id=1, source_target_pairs={{0,16},{8,24},{16,0},{24,8},{1,17},{9,25},{17,1},{25,9},{2,18},{10... | collective-permute-start | bytes 337928 | tf_op jit(solution)/shard_map/ppermute | solution.py:24
  (21 other events, 119.3 us)
